TPU v7x, 256 devices: a whole 4x4x8 slice. The times are simulated.
256 devices in a mesh: seq: 16 (over z, y_lo), head: 16 (over x, y_hi, core).
Axes of the slice: x: 4, y: 4 (y_hi: 2, y_lo: 2; y = y_hi * 2 + y_lo), z: 8, core: 2. Of those that a mesh axis runs over, the one named last changes fastest.
Arguments:
- cache: bfloat16 [2048, 576], P('seq'), may hold values from -8 to 8
- query_nope: bfloat16 [2048, 16384], P('seq', 'head'), may hold values from -5 to 5
- query_rope: bfloat16 [2048, 8192], P('seq', 'head'), may hold values from -256 to 256
- scale_exp: int32 [2048], P('seq'), may hold values from -1 to 1
- offsets: int32 [32], P('seq'), may hold values from 0 to 1984
- up_key: bfloat16 [512, 16384], P(None, 'head'), may hold values from -0.25 to 0.25
- up_value: bfloat16 [512, 16384], P(None, 'head'), may hold values from -0.25 to 0.25
- grad_out: bfloat16 [2048, 16384], P('seq', 'head'), may hold values from -5 to 5
Outputs:
- d_cache: bfloat16 [2048, 576], P('seq')
- d_query_nope: bfloat16 [2048, 16384], P('seq', 'head')
- d_query_rope: bfloat16 [2048, 8192], P('seq', 'head')
All inputs are finite; a program needn't handle non-finite values.
Results may differ from a plain program's by a relative error of at most 0.0099.
Values may be sent and summed in bfloat16 or wider, within the bound.
No kernel may reach another device: no remote copies, remote signals or barrier semaphores. Data moves between devices by JAX's collectives and lax.ppermute only.
A program may use at most 64 MiB of HBM per device.

v0:
```python
import math

import jax
import jax.numpy as jnp
from jax import lax
from jax.sharding import PartitionSpec as P

LATENT = 512
ROPE = 64
NOPE = 128
QBLOCK = 64


def in_order(blocks, dim):
    blocks = jnp.moveaxis(blocks, 0, dim)
    lengths = blocks.shape
    return blocks.reshape(*lengths[:dim], lengths[dim] * lengths[dim + 1], *lengths[dim + 2 :])


def copy_for_each(shard, axis):
    copies = jnp.broadcast_to(shard, (lax.axis_size(axis), *shard.shape))
    return lax.all_to_all(copies, axis, split_axis=0, concat_axis=0, tiled=True)


def gathered_copies(shard, axis, dim):
    return in_order(copy_for_each(shard, axis), dim)


def cut_along(shard, dim, devices):
    before, after = (shard.shape[:dim], shard.shape[dim + 1 :])
    return jnp.moveaxis(shard.reshape(*before, devices, -1, *after), dim, 0)


def sum_at_owner(shard, axis, dim):
    devices = lax.axis_size(axis)
    blocks = lax.all_to_all(cut_along(shard, dim, devices), axis, 0, 0, tiled=True)
    return jnp.sum(blocks.astype(jnp.float32), axis=0)


def over_copies(shard, axis):
    return copy_for_each(shard, axis).astype(jnp.float32).sum(axis=0)


def per_device(cache, query_nope, query_rope, scale_exp, offsets, up_key, up_value, grad_out):
    width = cache.shape[1]
    own_keys = cache.shape[0]
    packed = cache.reshape(own_keys // 2, 2 * width)
    whole = gathered_copies(packed, "seq", 0).reshape(-1, width)
    keys_total = whole.shape[0]
    queries = query_nope.shape[0]
    heads = up_key.shape[1] // NOPE
    scale = (NOPE + ROPE) ** (-0.5)
    factor = jnp.exp2(scale_exp.astype(jnp.float32))[:, None]
    q_nope = (
        (query_nope.astype(jnp.float32) * factor).astype(jnp.bfloat16).reshape(queries, heads, NOPE)
    )
    q_rope = (
        (query_rope.astype(jnp.float32) * factor).astype(jnp.bfloat16).reshape(queries, heads, ROPE)
    )
    w_key = up_key.reshape(LATENT, heads, NOPE)
    w_value = up_value.reshape(LATENT, heads, NOPE)
    absorbed = jnp.einsum("qhd,chd->hqc", q_nope, w_key, preferred_element_type=jnp.float32).astype(
        jnp.bfloat16
    )
    extended = jnp.concatenate([absorbed, jnp.transpose(q_rope, (1, 0, 2))], axis=2)
    back = jnp.einsum(
        "qhd,chd->hqc",
        grad_out.reshape(queries, heads, NOPE),
        w_value,
        preferred_element_type=jnp.float32,
    ).astype(jnp.bfloat16)
    positions = (offsets[:, None] + jnp.arange(QBLOCK, dtype=jnp.int32)[None, :]).reshape(-1)
    latent = whole[:, :LATENT]
    group = math.gcd(heads, max(1, 512 // queries))
    visible = (
        jnp.arange(keys_total, dtype=jnp.int32)[None, :] <= jnp.tile(positions, group)[:, None]
    )
    along_rows = (((0,), (0,)), ((), ()))
    along_cols = (((1,), (1,)), ((), ()))
    d_cache = jnp.zeros((keys_total, width), jnp.float32)
    nope_parts = []
    rope_parts = []
    for first in range(0, heads, group):
        ext_rows = extended[first : first + group].reshape(group * queries, width)
        back_rows = back[first : first + group].reshape(group * queries, LATENT)
        raw = (
            lax.dot_general(ext_rows, whole, along_cols, preferred_element_type=jnp.float32) * scale
        )
        scores = jnp.where(visible, raw, -jnp.inf)
        top = jnp.max(scores, axis=1, keepdims=True)
        lse = top + jnp.log(jnp.sum(jnp.exp(scores - top), axis=1, keepdims=True))
        probs = jnp.exp(scores - lse)
        probs_b = probs.astype(jnp.bfloat16)
        latent_out = jnp.dot(probs_b, latent, preferred_element_type=jnp.float32)
        delta = jnp.sum(back_rows.astype(jnp.float32) * latent_out, axis=1, keepdims=True)
        dprob = lax.dot_general(back_rows, latent, along_cols, preferred_element_type=jnp.float32)
        dscore = (probs * (dprob - delta) * scale).astype(jnp.bfloat16)
        grad_ext = jnp.dot(dscore, whole, preferred_element_type=jnp.float32)
        d_cache = d_cache + lax.dot_general(
            dscore, ext_rows, along_rows, preferred_element_type=jnp.float32
        )
        d_cache = d_cache.at[:, :LATENT].add(
            lax.dot_general(probs_b, back_rows, along_rows, preferred_element_type=jnp.float32)
        )
        grad_abs = grad_ext[:, :LATENT].astype(jnp.bfloat16).reshape(group, queries, LATENT)
        part_nope = (
            jnp.einsum(
                "hqc,chd->qhd",
                grad_abs,
                w_key[:, first : first + group],
                preferred_element_type=jnp.float32,
            )
            * factor[:, :, None]
        )
        part_rope = (
            jnp.transpose(grad_ext[:, LATENT:].reshape(group, queries, ROPE), (1, 0, 2))
            * factor[:, :, None]
        )
        nope_parts.append(part_nope.astype(jnp.bfloat16))
        rope_parts.append(part_rope.astype(jnp.bfloat16))
    d_query_nope = jnp.concatenate(nope_parts, axis=1).reshape(queries, heads * NOPE)
    d_query_rope = jnp.concatenate(rope_parts, axis=1).reshape(queries, heads * ROPE)
    flat = d_cache.reshape(keys_total // 2, 2 * width)
    owned = sum_at_owner(flat.astype(jnp.bfloat16), "seq", 0)
    mine = over_copies(owned.astype(jnp.bfloat16), "head").astype(jnp.float32).reshape(-1, width)
    return (mine.astype(jnp.bfloat16), d_query_nope, d_query_rope)


def solution(mesh):
    in_specs = (
        P("seq", None),
        P("seq", "head"),
        P("seq", "head"),
        P("seq"),
        P("seq"),
        P(None, "head"),
        P(None, "head"),
        P("seq", "head"),
    )
    out_specs = (P("seq", None), P("seq", "head"), P("seq", "head"))
    return jax.shard_map(
        per_device, mesh=mesh, in_specs=in_specs, out_specs=out_specs, check_vma=False
    )
```

profile of v0, /device:TPU:1, one launch (start us, length us, event | category | flops | bytes accessed | tf_op | source)
XLA Modules:
  0.0 208.1 jit_solution(1661456652497321350)
XLA Ops:
  0.7 1.1 copy.45
  2.0 1.7 broadcast_in_dim.9
  3.7 10.1 %all-to-all-start = ((bf16[16,64,1152]{2,1,0:T(8,128)(2,1)}), bf16[16,64,1152]{2,1,0:T(8,128)(2,1)S(1)}, u32[]{:S(2)}, u32[]{:S(2)}) async-start(bf16[16,64,1152]{2,1,0:T(8,128)(2,1)} %broadcast_in_dim.9), calls=%async_computation | async-start | bytes 4718592 | tf_op jit(solution)/shard_map/all_to_all | solution.py:22
  14.0 0.8 copy.43
  14.8 0.9 multiply_convert_fusion.3
  15.7 0.9 copy.44
  16.6 2.3 %copy.40 = bf16[512,1024]{0,1:T(8,128)(2,1)} copy(bf16[512,1024]{1,0:T(8,128)(2,1)} %param.17) | data formatting | bytes 2097152 | tf_op args[5]
  18.9 1.4 convolution_convert_fusion
  20.3 1.1 fusion.36
  21.3 2.0 copy.48
  23.4 2.1 %copy.49 = bf16[512,512]{0,1:T(8,128)(2,1)} copy(bf16[512,512]{1,0:T(8,128)(2,1)} %bitcast.77) | data formatting | bytes 1048576 | tf_op jit(solution)/shard_map/reshape | solution.py:85
  26.1 1.8 convolution_convert_fusion.1
  27.9 2.2 %pad_maximum_fusion = (bf16[4,128,576]{2,1,0:T(8,128)(2,1)}, bf16[4,128,576]{2,1,0:T(8,128)(2,1)}) fusion(bf16[8,128,64]{2,1,0:T(8,128)(2,1)} %bitcast.90, bf16[8,128,512]{2,1,0:T(8,128)(2,1)S(1)} %convolution_convert_fusion.1), kind=kLoop, calls=%fused_computation.39 | loop fusion | flops 2359296 | bytes 2359296 | tf_op jit(solution)/shard_map/concatenate | solution.py:65
  30.1 38.1 %all-to-all-done = bf16[16,64,1152]{2,1,0:T(8,128)(2,1)S(1)} async-done(((bf16[16,64,1152]{2,1,0:T(8,128)(2,1)}), bf16[16,64,1152]{2,1,0:T(8,128)(2,1)S(1)}, u32[]{:S(2)}, u32[]{:S(2)}) %all-to-all-start) | async-done | bytes 2359328 | tf_op jit(solution)/shard_map/all_to_all | solution.py:22
  68.2 2.9 %reshape_reshape.3 = bf16[2048,576]{1,0:T(8,128)(2,1)} reshape(bf16[16,64,1152]{2,1,0:T(8,128)(2,1)S(1)} %all-to-all-done) | data formatting | bytes 4718592 | tf_op jit(solution)/shard_map/reshape;reshape | solution.py:48
  71.1 4.0 %fusion.38 = (f32[512]{0:T(512)S(1)}, f32[512,2048]{1,0:T(8,128)S(1)}) fusion(bf16[512,576]{1,0:T(8,128)(2,1)} %bitcast.86, bf16[2048,576]{1,0:T(8,128)(2,1)} %reshape_reshape.3, s32[512]{0:T(512)S(1)} %broadcast_bitcast_fusion), kind=kOutput, calls=%fused_computation.67 | convolution fusion | flops 1212153344 | bytes 7147520 | tf_op jit(solution)/shard_map/dot_general | solution.py:87
  75.9 1.0 copy-done.7
  77.0 1.4 fusion.11
  78.4 1.4 multiply_convert_fusion
  79.8 2.1 fusion.37
  82.9 1.4 fusion.8
  84.3 1.4 multiply_convert_fusion.1
  85.7 1.4 fusion.39
  87.1 3.2 %fusion = f32[2048,576]{0,1:T(8,128)S(1)} fusion(f32[2048,576]{0,1:T(8,128)S(1)} %fusion.39, bf16[512,512]{1,0:T(8,128)(2,1)S(1)} %bitcast.82, pred[]{:T(512)} %compare_reduce_fusion, f32[512,2048]{1,0:T(8,128)S(1)} %get-tuple-element.43, f32[512]{0:T(512)S(1)} %log_add_fusion.1), kind=kOutput, calls=%fused_computation.2 | convolution fusion | flops 1077936128 | bytes 13109249 | tf_op jit(solution)/shard_map/dot_general | solution.py:103
  90.4 1.4 convolution_add_fusion
  91.9 2.9 %fusion.1 = f32[2048,576]{0,1:T(8,128)S(1)} fusion(f32[2048,576]{0,1:T(8,128)S(1)} %convolution_add_fusion, bf16[512,512]{1,0:T(8,128)(2,1)S(1)} %bitcast.79, pred[]{:T(512)} %compare_reduce_fusion, f32[512,2048]{1,0:T(8,128)S(1)} %get-tuple-element.45, f32[512]{0:T(512)S(1)} %log_add_fusion), kind=kOutput, calls=%fused_computation.3 | convolution fusion | flops 1077936128 | bytes 13109249 | tf_op jit(solution)/shard_map/dot_general | solution.py:103
  95.1 2.6 %copy.50 = bf16[2048,576]{1,0:T(8,128)(2,1)} copy(bf16[2048,576]{0,1:T(8,128)(2,1)S(1)} %convert_element_type.92) | data formatting | bytes 4718592 | tf_op jit(solution)/shard_map/convert_element_type | solution.py:124
  97.7 4.2 %convert_element_type.93 = bf16[16,64,1152]{2,1,0:T(8,128)(2,1)S(1)} reshape(bf16[2048,576]{1,0:T(8,128)(2,1)} %copy.50) | data formatting | bytes 4718592 | tf_op jit(solution)/shard_map/convert_element_type | solution.py:124
  101.9 61.1 %all_to_all.15 = bf16[16,64,1152]{2,1,0:T(8,128)(2,1)} all-to-all(bf16[16,64,1152]{2,1,0:T(8,128)(2,1)S(1)} %convert_element_type.93), channel_id=1, replica_groups=mesh['seq'=16,'head'=16] {'seq'}, dimensions={0} | all-to-all | bytes 4718592 | tf_op jit(solution)/shard_map/all_to_all | solution.py:36
  163.0 2.0 reduce_sum.64
  165.0 1.7 broadcast_in_dim.11
  166.7 8.9 %all-to-all-start.2 = ((bf16[16,64,1152]{2,1,0:T(8,128)(2,1)}), bf16[16,64,1152]{2,1,0:T(8,128)(2,1)S(1)}, u32[]{:S(2)}, u32[]{:S(2)}) async-start(bf16[16,64,1152]{2,1,0:T(8,128)(2,1)} %broadcast_in_dim.11), calls=%async_computation.2 | async-start | bytes 4718592 | tf_op jit(solution)/shard_map/all_to_all | solution.py:22
  175.6 3.8 %fusion.41 = f32[512,576]{0,1:T(8,128)S(1)} fusion(bf16[512,2048]{1,0:T(8,128)(2,1)} %copy-done.3, bf16[2048,576]{1,0:T(8,128)(2,1)} %reshape_reshape.3), kind=kOutput, calls=%fused_computation.70 | convolution fusion | flops 1207959552 | bytes 5636096 | tf_op jit(solution)/shard_map/dot_general | solution.py:98
  179.4 1.0 copy-done.10
  180.5 0.9 slice.127
  181.4 2.1 %copy.60 = bf16[512,512]{1,0:T(8,128)(2,1)} copy(bf16[512,512]{0,1:T(8,128)(2,1)} %slice.127) | data formatting | bytes 1048576 | tf_op jit(solution)/shard_map/reshape | solution.py:105
  183.4 3.8 %fusion.40 = f32[512,576]{0,1:T(8,128)S(1)} fusion(bf16[512,2048]{1,0:T(8,128)(2,1)} %copy-done.4, bf16[2048,576]{1,0:T(8,128)(2,1)} %reshape_reshape.3), kind=kOutput, calls=%fused_computation.69 | convolution fusion | flops 1207959552 | bytes 5636096 | tf_op jit(solution)/shard_map/dot_general | solution.py:98
  187.3 1.0 copy-done.11
  188.3 0.9 slice.128
  189.1 2.1 copy.59
  191.2 1.5 fusion.16
  192.7 1.5 fusion.17
  194.2 0.7 pad_maximum_fusion.1
  194.9 1.8 copy.56
  196.7 1.0 slice_bitcast_fusion
  197.8 0.8 copy.57
  198.6 8.3 %all-to-all-done.2 = bf16[16,64,1152]{2,1,0:T(8,128)(2,1)S(1)} async-done(((bf16[16,64,1152]{2,1,0:T(8,128)(2,1)}), bf16[16,64,1152]{2,1,0:T(8,128)(2,1)S(1)}, u32[]{:S(2)}, u32[]{:S(2)}) %all-to-all-start.2) | async-done | bytes 2359328 | tf_op jit(solution)/shard_map/all_to_all | solution.py:22
  207.4 0.8 copy.55
  (42 shorter events, 3.7 us)
Async XLA Ops:
  0.6 18.2 %copy-start = (bf16[512,1024]{1,0:T(8,128)(2,1)S(1)}, bf16[512,1024]{1,0:T(8,128)(2,1)}, u32[]{:S(2)}) copy-start(bf16[512,1024]{1,0:T(8,128)(2,1)} %param.18) | copy-start | bytes 3145732
  0.6 13.2 %copy-start.13 = (s32[2]{0:T(128)S(1)}, s32[2]{0:T(128)}, u32[]{:S(2)}) copy-start(s32[2]{0:T(128)} %param.16) | copy-start | bytes 28
  0.7 13.4 %copy-start.12 = (bf16[128,512]{1,0:T(8,128)(2,1)S(1)}, bf16[128,512]{1,0:T(8,128)(2,1)}, u32[]{:S(2)}) copy-start(bf16[128,512]{1,0:T(8,128)(2,1)} %param.14) | copy-start | bytes 393220
  0.7 14.1 %copy-start.14 = (s32[128]{0:T(128)S(1)}, s32[128]{0:T(128)}, u32[]{:S(2)}) copy-start(s32[128]{0:T(128)} %param.15) | copy-start | bytes 1540
  3.7 64.5 %all-to-all-start = ((bf16[16,64,1152]{2,1,0:T(8,128)(2,1)}), bf16[16,64,1152]{2,1,0:T(8,128)(2,1)S(1)}, u32[]{:S(2)}, u32[]{:S(2)}) async-start(bf16[16,64,1152]{2,1,0:T(8,128)(2,1)} %broadcast_in_dim.9), calls=%async_computation | async-start | bytes 4718592 | tf_op jit(solution)/shard_map/all_to_all | solution.py:22
  75.1 1.7 copy-start.7
  75.2 1.8 copy-start.9
  77.0 1.4 copy-start.1
  78.4 1.4 copy-start.6
  79.8 10.6 %copy-start.3 = (bf16[512,2048]{1,0:T(8,128)(2,1)}, bf16[512,2048]{1,0:T(8,128)(2,1)S(1)}, u32[]{:S(2)}) copy-start(bf16[512,2048]{1,0:T(8,128)(2,1)S(1)} %multiply_convert_fusion) | copy-start | bytes 6291460
  81.9 1.0 copy-start.8
  82.9 1.4 copy-start.2
  85.7 1.5 copy-start.4
  87.1 3.3 %copy-start.5 = (bf16[4,128,576]{2,1,0:T(8,128)(2,1)S(1)}, bf16[4,128,576]{2,1,0:T(8,128)(2,1)}, u32[]{:S(2)}) copy-start(bf16[4,128,576]{2,1,0:T(8,128)(2,1)} %get-tuple-element.36) | copy-start | bytes 1769476
  166.7 40.1 %all-to-all-start.2 = ((bf16[16,64,1152]{2,1,0:T(8,128)(2,1)}), bf16[16,64,1152]{2,1,0:T(8,128)(2,1)S(1)}, u32[]{:S(2)}, u32[]{:S(2)}) async-start(bf16[16,64,1152]{2,1,0:T(8,128)(2,1)} %broadcast_in_dim.11), calls=%async_computation.2 | async-start | bytes 4718592 | tf_op jit(solution)/shard_map/all_to_all | solution.py:22
  179.4 1.0 copy-start.10
  187.2 1.0 copy-start.11
where the time goes:
time: 210 us; the launch traced here: 208 us
  blocking collectives  61.1 us (29%)
  waiting for transfers between devices  46.4 us (22%)
  local copies, waits for them, and re-layouts  37.6 us (18%)
  matrix products  34.4 us (16%)
  starting transfers between devices  19 us (9%)
  other arithmetic  8.69 us (4%)
    all_to_all x1, blocking collectives, sum_at_owner(): lax.all_to_all(cut_along(shard, dim, devices), axis, 0, 0, tiled=True)  61.1 us
    all_to_all x2, waiting for transfers between devices, copy_for_each(): return lax.all_to_all(copies, axis, split_axis=0, concat_axis=0, tiled=True)  46.4 us
    all_to_all x2, starting transfers between devices, copy_for_each(): return lax.all_to_all(copies, axis, split_axis=0, concat_axis=0, tiled=True)  19 us
    unnamed x37, local copies, waits for them, and re-layouts  12.1 us
    dot_general x2, matrix products, per_device(): grad_ext = jnp.dot(dscore, whole, preferred_element_type=jnp.float32)  7.59 us
    convert_element_type x2, local copies, waits for them, and re-layouts, per_device(): owned = sum_at_owner(flat.astype(jnp.bfloat16), 'seq', 0)  6.75 us
    dot_general x2, matrix products, per_device(): lax.dot_general(probs_b, back_rows, along_rows, preferred_element_type=jn...  6.16 us
    dot_general x2, matrix products, per_device(): lax.dot_general(ext_rows, whole, along_cols, preferred_element_type=jnp.f...  6.1 us
  transfers between devices with their start and end apart: 2, of which 2 were waited for; matrix products, arithmetic and copies ran while one was open for 18% of the time, Pallas kernels for 0%

commit v1 on v0

v1 whole, which is shorter than its diff:
```python
import jax
import jax.numpy as jnp
from jax import lax
from jax.sharding import Mesh, PartitionSpec as P

LATENT = 512
ROPE = 64
NOPE = 128
QBLOCK = 64
WIDTH = LATENT + ROPE
LANES = 128
ROWS = 16
PACKED = ROWS * WIDTH // LANES
SEQ = ("z", "y_lo")
HEAD = ("x", "y_hi", "core")


def pack_rows(rows):
    latent = rows[:, :LATENT].reshape(ROWS, LATENT // LANES, LANES)
    latent = jnp.transpose(latent, (1, 0, 2)).reshape(-1, LANES)
    rotary = rows[:, LATENT:]
    rotary = jnp.concatenate([rotary[: ROWS // 2], rotary[ROWS // 2 :]], axis=1)
    return jnp.concatenate([latent, rotary], axis=0)


def unpack_rows(packed):
    lead = packed.shape[:-2]
    latent = packed[..., : ROWS * LATENT // LANES, :].reshape(*lead, LATENT // LANES, ROWS, LANES)
    latent = jnp.swapaxes(latent, -3, -2).reshape(*lead, ROWS, LATENT)
    rotary = packed[..., ROWS * LATENT // LANES :, :]
    rotary = jnp.concatenate([rotary[..., :ROPE], rotary[..., ROPE:]], axis=-2)
    return jnp.concatenate([latent, rotary], axis=-1)


def pack_all(rows):
    lead = rows.shape[:-2]
    latent = rows[..., :LATENT].reshape(*lead, ROWS, LATENT // LANES, LANES)
    latent = jnp.swapaxes(latent, -3, -2).reshape(*lead, ROWS * LATENT // LANES, LANES)
    rotary = rows[..., LATENT:]
    rotary = jnp.concatenate([rotary[..., : ROWS // 2, :], rotary[..., ROWS // 2 :, :]], axis=-1)
    return jnp.concatenate([latent, rotary], axis=-2)


def to_each(block, axes):
    copies = jnp.broadcast_to(block, (lax.axis_size(axes), *block.shape))
    return lax.all_to_all(copies, axes, 0, 0, tiled=True)


def swap_core(block):
    return lax.ppermute(block, "core", [(0, 1), (1, 0)])


def add_up(blocks):
    return jnp.sum(blocks.astype(jnp.float32), axis=0).astype(jnp.bfloat16)


def gather_cache(cache):
    own = lax.axis_index(("x", "core"))
    mine = pack_rows(lax.dynamic_slice_in_dim(cache, own * ROWS, ROWS, 0))
    over_seq = to_each(mine, SEQ)
    here = to_each(over_seq, "x")
    there = swap_core(here)
    return here, there


def owned_rows(keep, send):
    half = (keep.astype(jnp.float32) + swap_core(send).astype(jnp.float32)).astype(jnp.bfloat16)
    slices = add_up(lax.all_to_all(half, "x", 0, 0, tiled=True))
    slices = add_up(lax.all_to_all(slices, SEQ, 0, 0, tiled=True))
    parts = to_each(slices, HEAD)
    sizes = [lax.axis_size(axis) for axis in HEAD]
    parts = parts.reshape(*sizes, PACKED, LANES).astype(jnp.float32)
    parts = jnp.sum(parts, axis=1).astype(jnp.bfloat16)
    return unpack_rows(parts).reshape(-1, WIDTH)


def per_device(cache, query_nope, query_rope, scale_exp, offsets, up_key, up_value, grad_out):
    core = lax.axis_index("core")
    here, there = gather_cache(cache)
    both = jnp.stack([jnp.where(core == 0, here, there), jnp.where(core == 0, there, here)])
    whole = jnp.transpose(unpack_rows(both), (2, 1, 0, 3, 4)).reshape(-1, WIDTH)
    keys_total = whole.shape[0]
    queries = query_nope.shape[0]
    heads = up_key.shape[1] // NOPE
    scale = (NOPE + ROPE) ** (-0.5)
    factor = jnp.exp2(scale_exp.astype(jnp.float32))[:, None]
    q_nope = (query_nope.astype(jnp.float32) * factor).astype(jnp.bfloat16).reshape(queries, heads, NOPE)
    q_rope = (query_rope.astype(jnp.float32) * factor).astype(jnp.bfloat16).reshape(queries, heads, ROPE)
    w_key = up_key.reshape(LATENT, heads, NOPE)
    w_value = up_value.reshape(LATENT, heads, NOPE)
    absorbed = jnp.einsum("qhd,chd->hqc", q_nope, w_key, preferred_element_type=jnp.float32).astype(jnp.bfloat16)
    extended = jnp.concatenate([absorbed, jnp.transpose(q_rope, (1, 0, 2))], axis=2)
    back = jnp.einsum("qhd,chd->hqc", grad_out.reshape(queries, heads, NOPE), w_value,
                      preferred_element_type=jnp.float32).astype(jnp.bfloat16)
    positions = (offsets[:, None] + jnp.arange(QBLOCK, dtype=jnp.int32)[None, :]).reshape(-1)
    latent = whole[:, :LATENT]
    visible = jnp.arange(keys_total, dtype=jnp.int32)[None, :] <= jnp.tile(positions, heads)[:, None]
    along_rows = (((0,), (0,)), ((), ()))
    along_cols = (((1,), (1,)), ((), ()))
    ext_rows = extended.reshape(heads * queries, WIDTH)
    back_rows = back.reshape(heads * queries, LATENT)
    raw = lax.dot_general(ext_rows, whole, along_cols, preferred_element_type=jnp.float32) * scale
    scores = jnp.where(visible, raw, -jnp.inf)
    top = jnp.max(scores, axis=1, keepdims=True)
    lse = top + jnp.log(jnp.sum(jnp.exp(scores - top), axis=1, keepdims=True))
    probs = jnp.exp(scores - lse)
    probs_b = probs.astype(jnp.bfloat16)
    dprob = lax.dot_general(back_rows, latent, along_cols, preferred_element_type=jnp.float32)
    delta = jnp.sum(probs_b.astype(jnp.float32) * dprob, axis=1, keepdims=True)
    dscore = (probs * (dprob - delta) * scale).astype(jnp.bfloat16)
    d_cache = lax.dot_general(dscore, ext_rows, along_rows, preferred_element_type=jnp.float32)
    d_cache = d_cache.at[:, :LATENT].add(
        lax.dot_general(probs_b, back_rows, along_rows, preferred_element_type=jnp.float32))
    split = d_cache.astype(jnp.bfloat16).reshape(16, 4, 2, ROWS, WIDTH)
    split = pack_all(jnp.transpose(split, (2, 1, 0, 3, 4)))
    keep = jnp.where(core == 0, split[0], split[1])
    send = jnp.where(core == 0, split[1], split[0])
    mine = owned_rows(keep, send)
    grad_ext = jnp.dot(dscore, whole, preferred_element_type=jnp.float32)
    grad_abs = grad_ext[:, :LATENT].astype(jnp.bfloat16).reshape(heads, queries, LATENT)
    part_nope = jnp.einsum("hqc,chd->qhd", grad_abs, w_key, preferred_element_type=jnp.float32) * factor[:, :, None]
    part_rope = jnp.transpose(grad_ext[:, LATENT:].reshape(heads, queries, ROPE), (1, 0, 2)) * factor[:, :, None]
    d_query_nope = part_nope.astype(jnp.bfloat16).reshape(queries, heads * NOPE)
    d_query_rope = part_rope.astype(jnp.bfloat16).reshape(queries, heads * ROPE)
    return (mine, d_query_nope, d_query_rope)


def solution(mesh):
    names = SEQ + HEAD
    wide = Mesh(mesh.devices.reshape(8, 2, 4, 2, 2), names)
    in_specs = (
        P(SEQ, None),
        P(SEQ, HEAD),
        P(SEQ, HEAD),
        P(SEQ),
        P(SEQ),
        P(None, HEAD),
        P(None, HEAD),
        P(SEQ, HEAD),
    )
    out_specs = (P(SEQ, None), P(SEQ, HEAD), P(SEQ, HEAD))
    return jax.shard_map(per_device, mesh=wide, in_specs=in_specs, out_specs=out_specs, check_vma=False)
```

time: 210 us -> 152 us (0.72)
  waiting for transfers between devices: 46.4 us -> 25.2 us
  blocking collectives: 61.1 us -> 41 us
  matrix products: 34.4 us -> 20.7 us
  local copies, waits for them, and re-layouts: 37.6 us -> 26.9 us
  other arithmetic: 8.69 us -> 16.6 us
    all_to_all x2 -> x3, waiting for transfers between devices: 46.4 us -> 22.3 us  [the longest x2 18.6 us: to_each(): return lax.all_to_all(copies, axes, 0, 0, tiled=True)]
    all_to_all x1 -> x2, blocking collectives: 61.1 us -> 41 us  [the longest x1 21.3 us: to_each(): return lax.all_to_all(copies, axes, 0, 0, tiled=True)]
    unnamed x37, local copies, waits for them, and re-layouts: 12.1 us -> 6.08 us
    convert_element_type x2 -> x4, other arithmetic: 0.37 us -> 5.87 us  [the longest x1 2.5 us: per_device(): dscore = (probs * (dprob - delta) * scale).astype(jnp.bfloat16)]
    dot_general x4 -> x1, matrix products: 5.76 us -> 1.13 us  [per_device(): jnp.einsum('hqc,chd->qhd', grad_abs, w_key, preferred_element_type=jnp.fl...]
    convert_element_type x3 -> x1, local copies, waits for them, and re-layouts: 6.89 us -> 3.08 us  [per_device(): split = d_cache.astype(jnp.bfloat16).reshape(16, 4, 2, ROWS, WIDTH)]
    ppermute x0 -> x2, starting transfers between devices: none -> 3.4 us  [swap_core(): return lax.ppermute(block, 'core', [(0, 1), (1, 0)])]
    dot_general x2 -> x1, matrix products: 7.59 us -> 4.48 us  [per_device(): grad_ext = jnp.dot(dscore, whole, preferred_element_type=jnp.float32)]
  transfers between devices with their start and end apart: 2 -> 5, of which waited for: 2 -> 4; matrix products, arithmetic and copies ran while one was open for 18% -> 9% of each run, Pallas kernels for 0% -> 0%
where the time goes in v1:
time: 152 us; the launch traced here: 151 us
  blocking collectives  41 us (27%)
  local copies, waits for them, and re-layouts  26.9 us (18%)
  waiting for transfers between devices  25.2 us (17%)
  matrix products  20.7 us (14%)
  starting transfers between devices  19.6 us (13%)
  other arithmetic  16.6 us (11%)
    all_to_all x1, blocking collectives, to_each(): return lax.all_to_all(copies, axes, 0, 0, tiled=True)  21.3 us
    all_to_all x1, blocking collectives, owned_rows(): slices = add_up(lax.all_to_all(half, 'x', 0, 0, tiled=True))  19.6 us
    all_to_all x2, waiting for transfers between devices, to_each(): return lax.all_to_all(copies, axes, 0, 0, tiled=True)  18.6 us
    all_to_all x2, starting transfers between devices, to_each(): return lax.all_to_all(copies, axes, 0, 0, tiled=True)  12.6 us
    unnamed x37, local copies, waits for them, and re-layouts  6.08 us
    dot_general x1, matrix products, per_device(): grad_ext = jnp.dot(dscore, whole, preferred_element_type=jnp.float32)  4.48 us
    dot_general x1, matrix products, per_device(): lax.dot_general(probs_b, back_rows, along_rows, preferred_element_type=jn...  4.47 us
    reshape x1, local copies, waits for them, and re-layouts, unpack_rows(): latent = jnp.swapaxes(latent, -3, -2).reshape(*lead, ROWS, LATENT)  4.12 us
  transfers between devices with their start and end apart: 5, of which 4 were waited for; matrix products, arithmetic and copies ran while one was open for 9% of the time, Pallas kernels for 0%

profile of v1, /device:TPU:1, one launch (start us, length us, event | category | flops | bytes accessed | tf_op | source)
XLA Modules:
  0.0 151.0 jit_solution(15965526023830295170)
XLA Ops:
  0.7 1.1 constant_dynamic-slice_fusion
  1.8 0.9 fusion.29
  3.1 21.3 %all_to_all.25 = bf16[16,72,128]{2,1,0:T(8,128)(2,1)S(1)} all-to-all(bf16[16,72,128]{2,1,0:T(8,128)(2,1)S(1)} %broadcast_in_dim.10), channel_id=1, replica_groups=mesh['z'=8,'y_lo'=2,'x'=4,'y_hi'=2,'core'=2] {'z','y_lo'}, dimensions={0} | all-to-all | bytes 589824 | tf_op jit(solution)/shard_map/all_to_all | solution.py:46
  24.4 1.2 broadcast_in_dim.11
  25.6 4.4 %all-to-all-start.1 = ((bf16[4,16,72,128]{3,2,1,0:T(8,128)(2,1)}), bf16[4,16,72,128]{3,2,1,0:T(8,128)(2,1)}, u32[]{:S(2)}, u32[]{:S(2)}) async-start(bf16[4,16,72,128]{3,2,1,0:T(8,128)(2,1)} %broadcast_in_dim.11), calls=%async_computation.1 | async-start | bytes 2359296 | tf_op jit(solution)/shard_map/all_to_all | solution.py:46
  30.2 14.1 %all-to-all-done.1 = bf16[4,16,72,128]{3,2,1,0:T(8,128)(2,1)} async-done(((bf16[4,16,72,128]{3,2,1,0:T(8,128)(2,1)}), bf16[4,16,72,128]{3,2,1,0:T(8,128)(2,1)}, u32[]{:S(2)}, u32[]{:S(2)}) %all-to-all-start.1) | async-done | bytes 1179680 | tf_op jit(solution)/shard_map/all_to_all | solution.py:46
  44.2 3.3 %collective-permute-start = (bf16[4,16,72,128]{3,2,1,0:T(8,128)(2,1)}, bf16[4,16,72,128]{3,2,1,0:T(8,128)(2,1)}, u32[]{:S(2)}, u32[]{:S(2)}) collective-permute-start(bf16[4,16,72,128]{3,2,1,0:T(8,128)(2,1)} %all-to-all-done.1), channel_id=1, source_target_pairs={{0,1},{1,0},{2,3},{3,2},{4,5},{5,4},{6,7},{7,6},{8,9},{9,8},{10,11... | collective-permute-start | bytes 3538952 | tf_op jit(solution)/shard_map/ppermute | solution.py:50
  47.6 0.5 copy.69
  48.5 0.6 compare_reduce_fusion
  49.1 0.5 convolution_convert_fusion.1
  49.6 1.2 pad_maximum_fusion
  50.8 0.4 convolution_convert_fusion
  51.3 1.8 %select_bitcast_fusion.2 = (bf16[1,4,16,72,128]{4,3,2,1,0:T(8,128)(2,1)S(1)}, bf16[1,4,16,72,128]{4,3,2,1,0:T(8,128)(2,1)S(1)}) fusion(bf16[4,16,72,128]{3,2,1,0:T(8,128)(2,1)} %all-to-all-done.1, bf16[4,16,72,128]{3,2,1,0:T(8,128)(2,1)} %collective-permute-done, pred[]{:T(512)S(6)} %eq.2), kind=kLoop, calls=%fused_computation.42 | loop fusion | flops 1179648 | bytes 4718593 | tf_op jit(solution)/shard_map/stack | solution.py:80
  53.2 0.7 fusion.19
  54.0 2.6 %copy.94 = bf16[2,4,16,4,16,128]{5,3,4,2,1,0:T(4,128)(2,1)} copy(bf16[2,4,16,4,16,128]{5,4,3,2,1,0:T(8,128)(2,1)S(1)} %bitcast.102) | data formatting | bytes 4194304 | tf_op jit(solution)/shard_map/reshape | solution.py:28
  56.5 4.1 %reshape.141 = bf16[2,4,16,16,512]{4,3,2,1,0:T(8,128)(2,1)} reshape(bf16[2,4,16,16,4,128]{5,4,3,2,1,0:T(4,128)(2,1)} %bitcast.103) | data formatting | bytes 4194304 | tf_op jit(solution)/shard_map/reshape | solution.py:29
  60.7 1.9 %fusion.10 = bf16[16,4,2,16,576]{4,3,0,1,2:T(8,128)(2,1)S(1)} fusion(bf16[1,4,16,72,128]{4,3,2,1,0:T(8,128)(2,1)S(1)} %get-tuple-element.27, bf16[1,4,16,72,128]{4,3,2,1,0:T(8,128)(2,1)S(1)} %get-tuple-element.26, bf16[2,4,16,8,64]{4,3,2,1,0:T(8,128)(2,1)} %fusion.19, bf16[2,4,16,16,512]{4,3,2,1,0:T(8,128)(2,1)} %reshape.141), kind=kLoop, calls=%fused_computation.23 | loop fusion | flops 17694720 | bytes 6946816 | tf_op jit(solution)/shard_map/transpose | solution.py:81
  62.5 0.3 copy.49
  62.9 1.0 copy-done.7
  63.9 3.9 %fusion.30 = (f32[1024]{0:T(1024)S(1)}, f32[1024,2048]{1,0:T(8,128)S(1)}) fusion(bf16[1024,576]{1,0:T(8,128)(2,1)S(1)} %bitcast.107, bf16[2048,576]{1,0:T(8,128)(2,1)S(1)} %bitcast.99, s32[1024]{0:T(1024)S(1)} %broadcast_bitcast_fusion), kind=kOutput, calls=%fused_computation.70 | convolution fusion | flops 2424306688 | bytes 11935744 | tf_op jit(solution)/shard_map/dot_general | solution.py:102
  67.8 1.3 exponential_reduce_fusion
  69.1 3.0 %multiply_reduce_fusion = (f32[1024]{0:T(1024)S(1)}, f32[1024,2048]{1,0:T(8,128)S(1)}) fusion(f32[1024,2048]{1,0:T(8,128)S(1)} %get-tuple-element.33, f32[1024]{0:T(1024)S(1)} %log_add_fusion, bf16[1024,512]{1,0:T(8,128)(2,1)S(1)} %bitcast.104, bf16[2048,576]{1,0:T(8,128)(2,1)S(1)} %bitcast.100), kind=kOutput, calls=%fused_computation.1 | convolution fusion | flops 2157968384 | bytes 19931136 | tf_op jit(solution)/shard_map/dot_general | solution.py:108
  72.0 2.5 %multiply_convert_fusion = bf16[1024,2048]{1,0:T(8,128)(2,1)S(1)} fusion(f32[1024,2048]{1,0:T(8,128)S(1)} %get-tuple-element.35, f32[1024,2048]{1,0:T(8,128)S(1)} %get-tuple-element.33, f32[1024]{0:T(1024)S(1)} %get-tuple-element.34, f32[1024]{0:T(1024)S(1)} %log_add_fusion), kind=kLoop, calls=%fused_computation | loop fusion | flops 10485760 | bytes 20979712 | tf_op jit(solution)/shard_map/convert_element_type | solution.py:110
  74.6 2.8 %fusion.31 = f32[2048,576]{0,1:T(8,128)S(1)} fusion(bf16[1024,2048]{1,0:T(8,128)(2,1)S(1)} %multiply_convert_fusion, bf16[1024,576]{1,0:T(8,128)(2,1)S(1)} %bitcast.108), kind=kOutput, calls=%fused_computation.71 | convolution fusion | flops 2415919104 | bytes 10092544 | tf_op jit(solution)/shard_map/dot_general | solution.py:111
  77.4 4.5 %fusion.4 = f32[2048,576]{0,1:T(8,128)S(1)} fusion(f32[2048,576]{0,1:T(8,128)S(1)} %fusion.31, bf16[1024,512]{1,0:T(8,128)(2,1)S(1)} %bitcast.105, pred[]{:T(512)} %compare_reduce_fusion, f32[1024,2048]{1,0:T(8,128)S(1)} %get-tuple-element.33, f32[1024]{0:T(1024)S(1)} %log_add_fusion), kind=kOutput, calls=%fused_computation.13 | convolution fusion | flops 2153775104 | bytes 17829888 | tf_op jit(solution)/shard_map/dot_general | solution.py:113
  81.9 1.8 %convert_element_type.74 = bf16[2048,576]{0,1:T(8,128)(2,1)} convert(f32[2048,576]{0,1:T(8,128)S(1)} %fusion.4) | non-fusion elementwise | flops 1179648 | bytes 7077888 | tf_op jit(solution)/shard_map/convert_element_type | solution.py:114
  83.7 3.1 %copy.52 = bf16[2048,576]{1,0:T(8,128)(2,1)S(1)} copy(bf16[2048,576]{0,1:T(8,128)(2,1)} %convert_element_type.74) | data formatting | bytes 4718592 | tf_op jit(solution)/shard_map/convert_element_type | solution.py:114
  86.8 1.7 %slice.109 = bf16[2,4,16,16,512]{4,3,0,1,2:T(8,128)(2,1)} slice(bf16[2,4,16,16,576]{4,3,0,1,2:T(8,128)(2,1)S(1)} %bitcast.95), slice={[0:2], [0:4], [0:16], [0:16], [0:512]} | slice | bytes 4194304 | tf_op jit(solution)/shard_map/slice | solution.py:37
  88.6 2.6 %reshape.147 = bf16[2,4,16,16,4,128]{5,4,3,0,1,2:T(4,128)(2,1)S(1)} reshape(bf16[2,4,16,16,512]{4,3,0,1,2:T(8,128)(2,1)} %slice.109) | data formatting | bytes 4194304 | tf_op jit(solution)/shard_map/reshape | solution.py:37
  91.2 0.6 copy.53
  91.8 0.5 select_bitcast_fusion
  92.4 2.8 %collective-permute-done.1 = bf16[4,16,72,128]{3,2,1,0:T(8,128)(2,1)S(1)} collective-permute-done((bf16[4,16,72,128]{3,2,1,0:T(8,128)(2,1)S(1)}, bf16[4,16,72,128]{3,2,1,0:T(8,128)(2,1)S(1)}, u32[]{:S(2)}, u32[]{:S(2)}) %collective-permute-start.1) | collective-permute-done | bytes 1179680 | tf_op jit(solution)/shard_map/ppermute | solution.py:50
  95.3 0.6 fusion.11
  95.9 19.6 %all_to_all.26 = bf16[4,16,72,128]{3,2,1,0:T(8,128)(2,1)} all-to-all(bf16[4,16,72,128]{3,2,1,0:T(8,128)(2,1)S(1)} %fusion.11), channel_id=1, replica_groups=mesh['z'=8,'y_lo'=2,'x'=4,'y_hi'=2,'core'=2] {'x'}, dimensions={0} | all-to-all | bytes 2359296 | tf_op jit(solution)/shard_map/all_to_all | solution.py:68
  115.5 2.3 %reduce_sum.56 = bf16[16,72,128]{2,1,0:T(8,128)(2,1)} reduce(bf16[4,16,72,128]{3,2,1,0:T(8,128)(2,1)} %all_to_all.26, bf16[]{:T(256)} %constant.57.clone.1), dimensions={0}, to_apply=%region_4.5 | reduce | flops 442368 | bytes 1474562 | tf_op jit(solution)/shard_map/reduce_sum | solution.py:54
  117.7 3.5 %all-to-all-start.3 = ((bf16[16,72,128]{2,1,0:T(8,128)(2,1)}), bf16[16,72,128]{2,1,0:T(8,128)(2,1)S(1)}, u32[]{:S(2)}, u32[]{:S(2)}) async-start(bf16[16,72,128]{2,1,0:T(8,128)(2,1)} %reduce_sum.56), calls=%async_computation.3 | async-start | bytes 589824 | tf_op jit(solution)/shard_map/all_to_all | solution.py:69
  121.3 4.5 %fusion.32 = f32[1024,576]{0,1:T(8,128)S(1)} fusion(bf16[1024,2048]{1,0:T(8,128)(2,1)} %copy-done.6, bf16[2048,576]{1,0:T(8,128)(2,1)S(1)} %bitcast.101), kind=kOutput, calls=%fused_computation.72 | convolution fusion | flops 2415919104 | bytes 8912896 | tf_op jit(solution)/shard_map/dot_general | solution.py:119
  125.8 1.4 copy-done.9
  127.4 0.5 copy.62
  127.9 3.8 %all-to-all-done.3 = bf16[16,72,128]{2,1,0:T(8,128)(2,1)S(1)} async-done(((bf16[16,72,128]{2,1,0:T(8,128)(2,1)}), bf16[16,72,128]{2,1,0:T(8,128)(2,1)S(1)}, u32[]{:S(2)}, u32[]{:S(2)}) %all-to-all-start.3) | async-done | bytes 294944 | tf_op jit(solution)/shard_map/all_to_all | solution.py:69
  131.7 0.8 broadcast_in_dim.23
  132.5 8.2 %all-to-all-start.4 = ((bf16[16,72,128]{2,1,0:T(8,128)(2,1)}), bf16[16,72,128]{2,1,0:T(8,128)(2,1)S(1)}, u32[]{:S(2)}, u32[]{:S(2)}) async-start(bf16[16,72,128]{2,1,0:T(8,128)(2,1)} %broadcast_in_dim.23), calls=%async_computation.4 | async-start | bytes 589824 | tf_op jit(solution)/shard_map/all_to_all | solution.py:46
  140.7 1.1 fusion.15
  141.9 1.8 %copy.60 = bf16[128,1024]{1,0:T(8,128)(2,1)} copy(bf16[128,1024]{0,1:T(8,128)(2,1)} %bitcast.111) | data formatting | bytes 524288
  143.7 1.0 fusion.21
  144.6 0.8 copy.61
  145.4 4.5 %all-to-all-done.4 = bf16[16,72,128]{2,1,0:T(8,128)(2,1)S(1)} async-done(((bf16[16,72,128]{2,1,0:T(8,128)(2,1)}), bf16[16,72,128]{2,1,0:T(8,128)(2,1)S(1)}, u32[]{:S(2)}, u32[]{:S(2)}) %all-to-all-start.4) | async-done | bytes 294944 | tf_op jit(solution)/shard_map/all_to_all | solution.py:46
  150.2 0.8 copy.59
  (54 shorter events, 1.8 us)
Async XLA Ops:
  0.6 50.2 %copy-start = (bf16[512,1024]{1,0:T(8,128)(2,1)S(1)}, bf16[512,1024]{1,0:T(8,128)(2,1)}, u32[]{:S(2)}) copy-start(bf16[512,1024]{1,0:T(8,128)(2,1)} %param.16) | copy-start | bytes 3145732
  3.0 27.0 %copy-start.12 = (bf16[128,512]{1,0:T(8,128)(2,1)S(1)}, bf16[128,512]{1,0:T(8,128)(2,1)}, u32[]{:S(2)}) copy-start(bf16[128,512]{1,0:T(8,128)(2,1)} %param.12) | copy-start | bytes 393220
  3.0 27.1 %copy-start.13 = (s32[128]{0:T(128)S(1)}, s32[128]{0:T(128)}, u32[]{:S(2)}) copy-start(s32[128]{0:T(128)} %param.13) | copy-start | bytes 1540
  3.0 44.5 %copy-start.8 = (bf16[512,1024]{1,0:T(8,128)(2,1)S(1)}, bf16[512,1024]{1,0:T(8,128)(2,1)}, u32[]{:S(2)}) copy-start(bf16[512,1024]{1,0:T(8,128)(2,1)} %param.15) | copy-start | bytes 3145732
  25.6 22.7 %copy-start.14 = (s32[2]{0:T(128)S(1)}, s32[2]{0:T(128)}, u32[]{:S(2)}) copy-start(s32[2]{0:T(128)} %param.14) | copy-start | bytes 28
  25.6 23.5 %copy-start.10 = (bf16[128,1024]{1,0:T(8,128)(2,1)S(1)}, bf16[128,1024]{1,0:T(8,128)(2,1)}, u32[]{:S(2)}) copy-start(bf16[128,1024]{1,0:T(8,128)(2,1)} %param.11) | copy-start | bytes 786436
  25.6 18.6 %all-to-all-start.1 = ((bf16[4,16,72,128]{3,2,1,0:T(8,128)(2,1)}), bf16[4,16,72,128]{3,2,1,0:T(8,128)(2,1)}, u32[]{:S(2)}, u32[]{:S(2)}) async-start(bf16[4,16,72,128]{3,2,1,0:T(8,128)(2,1)} %broadcast_in_dim.11), calls=%async_computation.1 | async-start | bytes 2359296 | tf_op jit(solution)/shard_map/all_to_all | solution.py:46
  44.2 7.0 %collective-permute-start = (bf16[4,16,72,128]{3,2,1,0:T(8,128)(2,1)}, bf16[4,16,72,128]{3,2,1,0:T(8,128)(2,1)}, u32[]{:S(2)}, u32[]{:S(2)}) collective-permute-start(bf16[4,16,72,128]{3,2,1,0:T(8,128)(2,1)} %all-to-all-done.1), channel_id=1, source_target_pairs={{0,1},{1,0},{2,3},{3,2},{4,5},{5,4},{6,7},{7,6},{8,9},{9,8},{10,11... | collective-permute-start | bytes 3538952 | tf_op jit(solution)/shard_map/ppermute | solution.py:50
  48.1 2.7 %copy-start.2 = (bf16[512,1024]{0,1:T(8,128)(2,1)}, bf16[512,1024]{0,1:T(8,128)(2,1)S(1)}, u32[]{:S(2)}) copy-start(bf16[512,1024]{0,1:T(8,128)(2,1)S(1)} %copy.69) | copy-start | bytes 3145732
  49.1 1.7 %copy-start.11 = (bf16[128,1024]{1,0:T(8,128)(2,1)S(1)}, bf16[128,1024]{1,0:T(8,128)(2,1)}, u32[]{:S(2)}) copy-start(bf16[128,1024]{1,0:T(8,128)(2,1)} %param.17) | copy-start | bytes 786436
  62.5 1.3 copy-start.7
  62.9 6.2 %copy-start.4 = (bf16[16,4,2,16,576]{4,3,2,1,0:T(8,128)(2,1)}, bf16[16,4,2,16,576]{4,3,2,1,0:T(8,128)(2,1)S(1)}, u32[]{:S(2)}) copy-start(bf16[16,4,2,16,576]{4,3,2,1,0:T(8,128)(2,1)S(1)} %copy.49) | copy-start | bytes 7077892
  74.6 2.9 %copy-start.6 = (bf16[1024,2048]{1,0:T(8,128)(2,1)}, bf16[1024,2048]{1,0:T(8,128)(2,1)S(1)}, u32[]{:S(2)}) copy-start(bf16[1024,2048]{1,0:T(8,128)(2,1)S(1)} %multiply_convert_fusion) | copy-start | bytes 12582916
  92.3 2.9 %collective-permute-start.1 = (bf16[4,16,72,128]{3,2,1,0:T(8,128)(2,1)S(1)}, bf16[4,16,72,128]{3,2,1,0:T(8,128)(2,1)S(1)}, u32[]{:S(2)}, u32[]{:S(2)}) collective-permute-start(bf16[4,16,72,128]{3,2,1,0:T(8,128)(2,1)S(1)} %select_bitcast_fusion), channel_id=1, source_target_pairs={{0,1},{1,0},{2,3},{3,2},{4,5},{5,4},{6,7},{7,6},{8,9},{9,8},{10,11... | collective-permute-start | bytes 3538952 | tf_op jit(solution)/shard_map/ppermute | solution.py:50
  95.8 25.4 %copy-start.5 = (bf16[16,4,2,16,576]{4,3,2,1,0:T(8,128)(2,1)S(1)}, bf16[16,4,2,16,576]{4,3,2,1,0:T(8,128)(2,1)}, u32[]{:S(2)}) copy-start(bf16[16,4,2,16,576]{4,3,2,1,0:T(8,128)(2,1)} %copy-done.4) | copy-start | bytes 7077892
  117.7 13.9 %all-to-all-start.3 = ((bf16[16,72,128]{2,1,0:T(8,128)(2,1)}), bf16[16,72,128]{2,1,0:T(8,128)(2,1)S(1)}, u32[]{:S(2)}, u32[]{:S(2)}) async-start(bf16[16,72,128]{2,1,0:T(8,128)(2,1)} %reduce_sum.56), calls=%async_computation.3 | async-start | bytes 589824 | tf_op jit(solution)/shard_map/all_to_all | solution.py:69
  125.8 1.4 copy-start.9
  127.2 13.5 %copy-start.3 = (bf16[512,1024]{0,1:T(8,128)(2,1)S(1)}, bf16[512,1024]{0,1:T(8,128)(2,1)}, u32[]{:S(2)}) copy-start(bf16[512,1024]{0,1:T(8,128)(2,1)} %copy-done.2) | copy-start | bytes 3145732
  132.5 17.4 %all-to-all-start.4 = ((bf16[16,72,128]{2,1,0:T(8,128)(2,1)}), bf16[16,72,128]{2,1,0:T(8,128)(2,1)S(1)}, u32[]{:S(2)}, u32[]{:S(2)}) async-start(bf16[16,72,128]{2,1,0:T(8,128)(2,1)} %broadcast_in_dim.23), calls=%async_computation.4 | async-start | bytes 589824 | tf_op jit(solution)/shard_map/all_to_all | solution.py:46
  140.7 10.3 %copy-start.1 = (bf16[512,1024]{1,0:T(8,128)(2,1)S(1)}, bf16[512,1024]{1,0:T(8,128)(2,1)}, u32[]{:S(2)}) copy-start(bf16[512,1024]{1,0:T(8,128)(2,1)} %param.16) | copy-start | bytes 3145732

commit v2 on v1

v2 whole, which is shorter than its diff:
```python
import jax
import jax.numpy as jnp
from jax import lax
from jax.experimental import pallas as pl
from jax.experimental.pallas import tpu as pltpu
from jax.sharding import Mesh, PartitionSpec as P

LATENT = 512
ROPE = 64
NOPE = 128
QBLOCK = 64
WIDTH = LATENT + ROPE
LANES = 128
ROWS = 16
PACKED = ROWS * WIDTH // LANES
PADDED = LATENT + LANES
KTILE = 512
VMEM = 56 * 2**20
LOG2E = 1.4426950408889634
UNSEEN = -1e30
SEQ = ("z", "y_lo")
HEAD = ("x", "y_hi", "core")


def pack_rows(rows):
    latent = rows[:, :LATENT].reshape(ROWS, LATENT // LANES, LANES)
    latent = jnp.transpose(latent, (1, 0, 2)).reshape(-1, LANES)
    rotary = rows[:, LATENT:]
    rotary = jnp.concatenate([rotary[: ROWS // 2], rotary[ROWS // 2 :]], axis=1)
    return jnp.concatenate([latent, rotary], axis=0)


def unpack_rows(packed):
    lead = packed.shape[:-2]
    latent = packed[..., : ROWS * LATENT // LANES, :].reshape(*lead, LATENT // LANES, ROWS, LANES)
    latent = jnp.swapaxes(latent, -3, -2).reshape(*lead, ROWS, LATENT)
    rotary = packed[..., ROWS * LATENT // LANES :, :]
    rotary = jnp.concatenate([rotary[..., :ROPE], rotary[..., ROPE:]], axis=-2)
    return jnp.concatenate([latent, rotary], axis=-1)


def to_each(block, axes):
    copies = jnp.broadcast_to(block, (lax.axis_size(axes), *block.shape))
    return lax.all_to_all(copies, axes, 0, 0, tiled=True)


def swap_core(block):
    return lax.ppermute(block, "core", [(0, 1), (1, 0)])


def add_up(blocks):
    return jnp.sum(blocks.astype(jnp.float32), axis=0).astype(jnp.bfloat16)


def owned_rows(keep, send):
    half = (keep.astype(jnp.float32) + swap_core(send).astype(jnp.float32)).astype(jnp.bfloat16)
    slices = add_up(lax.all_to_all(half, "x", 0, 0, tiled=True))
    slices = add_up(lax.all_to_all(slices, SEQ, 0, 0, tiled=True))
    parts = to_each(slices, HEAD)
    sizes = [lax.axis_size(axis) for axis in HEAD]
    parts = parts.reshape(*sizes, PACKED, LANES).astype(jnp.float32)
    parts = jnp.sum(parts, axis=1).astype(jnp.bfloat16)
    return unpack_rows(parts).reshape(-1, WIDTH)


def project_kernel(scale_ref, nope_ref, rope_ref, key_ref, value_ref, grad_ref, ext_ref, back_ref):
    queries = nope_ref.shape[0]
    heads = key_ref.shape[1] // NOPE
    blocks = queries // QBLOCK
    factor = jnp.exp2(scale_ref[...].astype(jnp.float32))
    cols = (((1,), (1,)), ((), ()))
    for h in range(heads):
        lanes = slice(h * NOPE, (h + 1) * NOPE)
        q_nope = (nope_ref[:, lanes].astype(jnp.float32) * factor).astype(jnp.bfloat16)
        absorbed = lax.dot_general(q_nope, key_ref[:, lanes], cols, preferred_element_type=jnp.float32)
        back = lax.dot_general(grad_ref[:, lanes], value_ref[:, lanes], cols, preferred_element_type=jnp.float32)
        absorbed = absorbed.astype(jnp.bfloat16)
        back = back.astype(jnp.bfloat16)
        pair = slice(h // 2 * LANES, (h // 2 + 1) * LANES)
        rope = rope_ref[:, pair].astype(jnp.float32) * factor
        if h % 2:
            rope = pltpu.roll(rope, ROPE, 1)
        lane = lax.broadcasted_iota(jnp.int32, rope.shape, 1)
        rope = jnp.where(lane < ROPE, rope, 0.0).astype(jnp.bfloat16)
        for b in range(blocks):
            src = slice(b * QBLOCK, (b + 1) * QBLOCK)
            dst = slice(h * QBLOCK, (h + 1) * QBLOCK)
            ext_ref[b, dst, :LATENT] = absorbed[src]
            ext_ref[b, dst, LATENT:] = rope[src]
            back_ref[b, dst, :] = back[src]


def project(scale_exp, query_nope, query_rope, up_key, up_value, grad_out):
    queries = query_nope.shape[0]
    heads = up_key.shape[1] // NOPE
    blocks = queries // QBLOCK
    rows = heads * QBLOCK
    return pl.pallas_call(
        project_kernel,
        out_shape=(
            jax.ShapeDtypeStruct((blocks, rows, PADDED), jnp.bfloat16),
            jax.ShapeDtypeStruct((blocks, rows, LATENT), jnp.bfloat16),
        ),
        compiler_params=pltpu.CompilerParams(vmem_limit_bytes=VMEM),
        cost_estimate=pl.CostEstimate(flops=4 * queries * heads * NOPE * LATENT, bytes_accessed=6_000_000, transcendentals=0),
        name="project",
    )(scale_exp.reshape(queries, 1), query_nope, query_rope, up_key, up_value, grad_out)


def attend_kernel(core_ref, offsets_ref, here_ref, there_ref, ext_ref, back_ref,
                  keep_ref, send_ref, ds_ref, cache_ref, score_buf, dprob_buf, acc_buf):
    slices, owners = here_ref.shape[:2]
    keys_total = cache_ref.shape[0]
    blocks, rows = ext_ref.shape[:2]
    core = core_ref[0]
    scale = (NOPE + ROPE) ** (-0.5)
    lane = lax.broadcasted_iota(jnp.int32, (ROWS // 2, LANES), 1)
    span = 2 * slices * ROWS
    lat_rows = ROWS * LATENT // LANES

    def place(s, x, which):
        return pl.multiple_of(s * span + x * 2 * ROWS + which * ROWS, ROWS)

    for s in range(owners):
        for x in range(slices):
            for src, which in ((here_ref, core), (there_ref, 1 - core)):
                row = place(s, x, which)
                for k in range(LATENT // LANES):
                    cache_ref[pl.ds(row, ROWS), k * LANES : (k + 1) * LANES] = src[x, s, k * ROWS : (k + 1) * ROWS, :]
                rope = src[x, s, lat_rows:, :].astype(jnp.float32)
                low = jnp.where(lane < ROPE, rope, 0.0)
                high = jnp.where(lane < ROPE, pltpu.roll(rope, ROPE, 1), 0.0)
                cache_ref[pl.ds(row, ROWS), LATENT:] = jnp.concatenate([low, high], axis=0).astype(jnp.bfloat16)

    cols = (((1,), (1,)), ((), ()))
    tiles = keys_total // KTILE
    inner = lax.broadcasted_iota(jnp.int32, (KTILE, rows), 1) % QBLOCK
    key = lax.broadcasted_iota(jnp.int32, (KTILE, rows), 0)
    ahead = key - inner

    def fold(values, op):
        return op(values.reshape(-1, 8, rows), axis=0)

    def scores(b, t, top):
        keys = slice(t * KTILE, (t + 1) * KTILE)
        raw = lax.dot_general(cache_ref[keys, :], ext_ref[b], cols, preferred_element_type=jnp.float32)
        dprob_buf[b, keys, :] = lax.dot_general(
            cache_ref[keys, :LATENT], back_ref[b], cols, preferred_element_type=jnp.float32)
        raw = jnp.where(ahead <= offsets_ref[b] - t * KTILE, raw * (scale * LOG2E), UNSEEN)
        score_buf[b, keys, :] = raw
        return jnp.maximum(top, fold(raw, jnp.max))

    def weights(b, t, top, total):
        keys = slice(t * KTILE, (t + 1) * KTILE)
        weight = jnp.exp2(score_buf[b, keys, :] - top)
        score_buf[b, keys, :] = weight
        return total + fold(weight, jnp.sum)

    def values(b, t, inverse, delta):
        keys = slice(t * KTILE, (t + 1) * KTILE)
        probs = (score_buf[b, keys, :] * inverse).astype(jnp.bfloat16)
        part = jnp.dot(probs, back_ref[b], preferred_element_type=jnp.float32)
        if b == 0:
            acc_buf[keys, :LATENT] = part
        else:
            acc_buf[keys, :LATENT] += part
        return delta + fold(probs.astype(jnp.float32) * dprob_buf[b, keys, :], jnp.sum)

    def gradients(b, t, inverse, delta):
        keys = slice(t * KTILE, (t + 1) * KTILE)
        dscore = score_buf[b, keys, :] * inverse * (dprob_buf[b, keys, :] - delta) * scale
        dscore = dscore.astype(jnp.bfloat16)
        ds_ref[b, keys, :] = dscore
        part = jnp.dot(dscore, ext_ref[b], preferred_element_type=jnp.float32)
        acc_buf[keys, :LATENT] += part[:, :LATENT]
        if b == 0:
            acc_buf[keys, LATENT:] = part[:, LATENT:]
        else:
            acc_buf[keys, LATENT:] += part[:, LATENT:]

    low = jnp.full((8, rows), UNSEEN, jnp.float32)
    zero = jnp.zeros((8, rows), jnp.float32)
    tops = [low] * blocks
    totals = [zero] * blocks
    deltas = [zero] * blocks
    for t in range(tiles):
        tops[0] = scores(0, t, tops[0])
    tops[0] = jnp.max(tops[0], axis=0, keepdims=True)
    for t in range(tiles):
        tops[1] = scores(1, t, tops[1])
        totals[0] = weights(0, t, tops[0], totals[0])
    tops[1] = jnp.max(tops[1], axis=0, keepdims=True)
    totals[0] = 1.0 / jnp.sum(totals[0], axis=0, keepdims=True)
    for t in range(tiles):
        deltas[0] = values(0, t, totals[0], deltas[0])
        totals[1] = weights(1, t, tops[1], totals[1])
    deltas[0] = jnp.sum(deltas[0], axis=0, keepdims=True)
    totals[1] = 1.0 / jnp.sum(totals[1], axis=0, keepdims=True)
    for t in range(tiles):
        gradients(0, t, totals[0], deltas[0])
        deltas[1] = values(1, t, totals[1], deltas[1])
    deltas[1] = jnp.sum(deltas[1], axis=0, keepdims=True)
    per_tile = KTILE // span
    for t in range(tiles):
        gradients(1, t, totals[1], deltas[1])
        for s in range(t * per_tile, (t + 1) * per_tile):
            for x in range(slices):
                for dst, which in ((send_ref, 1 - core), (keep_ref, core)):
                    row = place(s, x, which)
                    for k in range(LATENT // LANES):
                        dst[x, s, k * ROWS : (k + 1) * ROWS, :] = acc_buf[
                            pl.ds(row, ROWS), k * LANES : (k + 1) * LANES].astype(jnp.bfloat16)
                    rope = acc_buf[pl.ds(row, ROWS), LATENT:]
                    rope = rope[: ROWS // 2] + pltpu.roll(rope[ROWS // 2 :], ROPE, 1)
                    dst[x, s, lat_rows:, :] = rope.astype(jnp.bfloat16)


def attend(core, offsets, here, there, extended, back):
    blocks, rows = extended.shape[:2]
    slices, owners = here.shape[:2]
    keys_total = 2 * slices * owners * ROWS
    packed = jax.ShapeDtypeStruct(here.shape, jnp.bfloat16)
    smem = pl.BlockSpec(memory_space=pltpu.SMEM)
    vmem = pl.BlockSpec(memory_space=pltpu.VMEM)
    return pl.pallas_call(
        attend_kernel,
        out_shape=(
            packed,
            packed,
            jax.ShapeDtypeStruct((blocks, keys_total, rows), jnp.bfloat16),
            jax.ShapeDtypeStruct((keys_total, PADDED), jnp.bfloat16),
        ),
        in_specs=[smem, smem, vmem, vmem, vmem, vmem],
        out_specs=(vmem, vmem, vmem, vmem),
        scratch_shapes=[
            pltpu.VMEM((blocks, keys_total, rows), jnp.float32),
            pltpu.VMEM((blocks, keys_total, rows), jnp.float32),
            pltpu.VMEM((keys_total, PADDED), jnp.float32),
        ],
        compiler_params=pltpu.CompilerParams(vmem_limit_bytes=VMEM),
        cost_estimate=pl.CostEstimate(
            flops=2 * blocks * rows * keys_total * (2 * PADDED + 2 * LATENT),
            bytes_accessed=12_000_000, transcendentals=blocks * rows * keys_total),
        name="attend",
    )(core.reshape(1), offsets, here, there, extended, back)


def query_kernel(scale_ref, ds_ref, cache_ref, key_ref, nope_ref, rope_ref, grad_buf):
    blocks, _, rows = ds_ref.shape
    heads = rows // QBLOCK
    firsts = (((0,), (0,)), ((), ()))
    factor = jnp.exp2(scale_ref[...].astype(jnp.float32))
    for b in range(blocks):
        grad_buf[b] = lax.dot_general(ds_ref[b], cache_ref[...], firsts, preferred_element_type=jnp.float32)
    for h in range(heads):
        lanes = slice(h * NOPE, (h + 1) * NOPE)
        part = slice(h * QBLOCK, (h + 1) * QBLOCK)
        grad = jnp.concatenate([grad_buf[b, part, :] for b in range(blocks)], axis=0)
        nope = jnp.dot(grad[:, :LATENT].astype(jnp.bfloat16), key_ref[:, lanes], preferred_element_type=jnp.float32)
        nope_ref[:, lanes] = (nope * factor).astype(jnp.bfloat16)
        rope = grad[:, LATENT:] * factor
        if h % 2 == 0:
            even = rope
        else:
            pair = slice(h // 2 * LANES, (h // 2 + 1) * LANES)
            rope_ref[:, pair] = (even + pltpu.roll(rope, ROPE, 1)).astype(jnp.bfloat16)


def query_gradients(scale_exp, dscore, cache, up_key):
    blocks, keys_total, rows = dscore.shape
    heads = rows // QBLOCK
    queries = blocks * QBLOCK
    return pl.pallas_call(
        query_kernel,
        out_shape=(
            jax.ShapeDtypeStruct((queries, heads * NOPE), jnp.bfloat16),
            jax.ShapeDtypeStruct((queries, heads * ROPE), jnp.bfloat16),
        ),
        scratch_shapes=[pltpu.VMEM((blocks, rows, PADDED), jnp.float32)],
        compiler_params=pltpu.CompilerParams(vmem_limit_bytes=VMEM),
        cost_estimate=pl.CostEstimate(
            flops=2 * blocks * rows * keys_total * PADDED, bytes_accessed=9_000_000, transcendentals=0),
        name="query_gradients",
    )(scale_exp.reshape(queries, 1), dscore, cache, up_key)


def per_device(cache, query_nope, query_rope, scale_exp, offsets, up_key, up_value, grad_out):
    core = lax.axis_index("core").astype(jnp.int32)
    own = lax.axis_index(("x", "core"))
    mine = pack_rows(lax.dynamic_slice_in_dim(cache, own * ROWS, ROWS, 0))
    over_seq = to_each(mine, SEQ)
    extended, back = project(scale_exp, query_nope, query_rope, up_key, up_value, grad_out)
    over_seq, extended, back = lax.optimization_barrier((over_seq, extended, back))
    here = to_each(over_seq, "x")
    there = swap_core(here)
    keep, send, dscore, whole = attend(core, offsets, here, there, extended, back)
    d_cache = owned_rows(keep, send)
    d_query_nope, d_query_rope = query_gradients(scale_exp, dscore, whole, up_key)
    return (d_cache, d_query_nope, d_query_rope)


def solution(mesh):
    names = SEQ + HEAD
    wide = Mesh(mesh.devices.reshape(8, 2, 4, 2, 2), names)
    in_specs = (
        P(SEQ, None),
        P(SEQ, HEAD),
        P(SEQ, HEAD),
        P(SEQ),
        P(SEQ),
        P(None, HEAD),
        P(None, HEAD),
        P(SEQ, HEAD),
    )
    out_specs = (P(SEQ, None), P(SEQ, HEAD), P(SEQ, HEAD))
    return jax.shard_map(per_device, mesh=wide, in_specs=in_specs, out_specs=out_specs, check_vma=False)
```

time: 152 us -> 128 us (0.84)
  Pallas kernels: 0 us -> 32.5 us
  matrix products: 20.7 us -> 0 us
  local copies, waits for them, and re-layouts: 26.9 us -> 6.55 us
  other arithmetic: 16.6 us -> 1.98 us
  waiting for transfers between devices: 25.2 us -> 13.1 us
  blocking collectives: 41 us -> 50.1 us
  starting transfers between devices: 19.6 us -> 22.1 us
    pallas_call x0 -> x3, Pallas kernels: none -> 32.5 us  [the longest x1 20.8 us: attend(): pl.pallas_call(attend_kernel, out_shape=(packed, packed, jax.ShapeDtypeSt...]
    dot_general x8 -> x0, matrix products: 20.7 us -> none  [the longest x1 4.48 us: per_device(): grad_ext = jnp.dot(dscore, whole, preferred_element_type=jnp.float32)]
    all_to_all x0 -> x1, blocking collectives: none -> 13.7 us  [owned_rows(): slices = add_up(lax.all_to_all(slices, SEQ, 0, 0, tiled=True))]
    all_to_all x2, waiting for transfers between devices: 18.6 us -> 7.97 us  [to_each(): return lax.all_to_all(copies, axes, 0, 0, tiled=True)]
    reshape x7 -> x1, local copies, waits for them, and re-layouts: 11.1 us -> 0.74 us  [project(): scale_exp.reshape(queries, 1)]
    all_to_all x2, starting transfers between devices: 12.6 us -> 18.2 us  [to_each(): return lax.all_to_all(copies, axes, 0, 0, tiled=True)]
    convert_element_type x4 -> x0, other arithmetic: 5.3 us -> none  [the longest x1 2.5 us: per_device(): dscore = (probs * (dprob - delta) * scale).astype(jnp.bfloat16)]
    unnamed x37 -> x10, local copies, waits for them, and re-layouts: 6.08 us -> 1.97 us
  transfers between devices with their start and end apart: 5 -> 4, of which waited for: 4 -> 4; matrix products, arithmetic and copies ran while one was open for 9% -> 1% of each run, Pallas kernels for 0% -> 9%
where the time goes in v2:
time: 128 us; the launch traced here: 127 us
  blocking collectives  50.1 us (39%)
  Pallas kernels  32.5 us (25%)
  starting transfers between devices  22.1 us (17%)
  waiting for transfers between devices  13.1 us (10%)
  local copies, waits for them, and re-layouts  6.55 us (5%)
  other arithmetic  1.98 us (2%)
    pallas_call x1, Pallas kernels, attend(): pl.pallas_call(attend_kernel, out_shape=(packed, packed, jax.ShapeDtypeSt...  20.8 us
    all_to_all x1, blocking collectives, owned_rows(): slices = add_up(lax.all_to_all(half, 'x', 0, 0, tiled=True))  18.7 us
    all_to_all x2, starting transfers between devices, to_each(): return lax.all_to_all(copies, axes, 0, 0, tiled=True)  18.2 us
    all_to_all x1, blocking collectives, to_each(): return lax.all_to_all(copies, axes, 0, 0, tiled=True)  17.7 us
    all_to_all x1, blocking collectives, owned_rows(): slices = add_up(lax.all_to_all(slices, SEQ, 0, 0, tiled=True))  13.7 us
    all_to_all x2, waiting for transfers between devices, to_each(): return lax.all_to_all(copies, axes, 0, 0, tiled=True)  7.97 us
    pallas_call x1, Pallas kernels, query_gradients(): pl.pallas_call(query_kernel, out_shape=(jax.ShapeDtypeStruct((queries, he...  7.76 us
    ppermute x2, waiting for transfers between devices, swap_core(): return lax.ppermute(block, 'core', [(0, 1), (1, 0)])  5.16 us
  transfers between devices with their start and end apart: 4, of which 4 were waited for; matrix products, arithmetic and copies ran while one was open for 1% of the time, Pallas kernels for 9%

profile of v2, /device:TPU:1, one launch (start us, length us, event | category | flops | bytes accessed | tf_op | source)
XLA Modules:
  0.0 127.1 jit_solution(3400186344214782238)
XLA Ops:
  0.6 0.0 copy-start.1
  0.6 1.0 constant_dynamic-slice_fusion
  1.7 0.9 fusion.1
  2.6 0.1 copy.29
  2.6 0.1 copy.30
  2.7 0.1 copy.22
  2.8 0.1 maximum_maximum_fusion
  2.9 0.8 broadcast_in_dim.9
  3.7 10.1 %all-to-all-start = ((bf16[16,72,128]{2,1,0:T(8,128)(2,1)}), bf16[16,72,128]{2,1,0:T(8,128)(2,1)S(1)}, u32[]{:S(2)}, u32[]{:S(2)}) async-start(bf16[16,72,128]{2,1,0:T(8,128)(2,1)} %broadcast_in_dim.9), calls=%async_computation | async-start | bytes 589824 | tf_op jit(solution)/shard_map/all_to_all | solution.py:44
  13.8 0.0 copy-done.1
  13.8 0.7 copy.23.scale_ref
  14.6 4.0 %project.1 = (bf16[2,512,640]{2,1,0:T(8,128)(2,1)}, bf16[2,512,512]{2,1,0:T(8,128)(2,1)}) custom-call(s32[128,1]{1,0:T(8,128)} %copy.23.scale_ref, bf16[128,1024]{1,0:T(8,128)(2,1)} %nope_ref.1, bf16[128,512]{1,0:T(8,128)(2,1)} %rope_ref.1, bf16[512,1024]{1,0:T(8,128)(2,1)} %key_ref.3, bf16[512,1024]{1,0:T(8,128)(2,1)} %value_ref.1, bf16[128,1024]{1,0:T(8,128)(2,1)} %grad_ref.1), custom_call_target="tpu_custom_call" | custom-call | flops 268435456 | bytes 6000000 | tf_op jit(solution)/shard_map/project/pallas_call | solution.py:98
  18.6 6.5 %all-to-all-done = bf16[16,72,128]{2,1,0:T(8,128)(2,1)S(1)} async-done(((bf16[16,72,128]{2,1,0:T(8,128)(2,1)}), bf16[16,72,128]{2,1,0:T(8,128)(2,1)S(1)}, u32[]{:S(2)}, u32[]{:S(2)}) %all-to-all-start) | async-done | bytes 294944 | tf_op jit(solution)/shard_map/all_to_all | solution.py:44
  25.1 0.2 broadcast_in_dim.10
  25.3 17.7 %all_to_all.25.here_ref = bf16[4,16,72,128]{3,2,1,0:T(8,128)(2,1)S(1)} all-to-all(bf16[4,16,72,128]{3,2,1,0:T(8,128)(2,1)S(1)} %broadcast_in_dim.10), channel_id=1, replica_groups=mesh['z'=8,'y_lo'=2,'x'=4,'y_hi'=2,'core'=2] {'x'}, dimensions={0} | all-to-all | bytes 2359296 | tf_op jit(solution)/shard_map/all_to_all | solution.py:44
  43.0 0.0 copy-start
  43.0 3.5 %collective-permute-start = (bf16[4,16,72,128]{3,2,1,0:T(8,128)(2,1)S(1)}, bf16[4,16,72,128]{3,2,1,0:T(8,128)(2,1)S(1)}, u32[]{:S(2)}, u32[]{:S(2)}) collective-permute-start(bf16[4,16,72,128]{3,2,1,0:T(8,128)(2,1)S(1)} %all_to_all.25.here_ref), channel_id=1, source_target_pairs={{0,1},{1,0},{2,3},{3,2},{4,5},{5,4},{6,7},{7,6},{8,9},{9,8},{10,11... | collective-permute-start | bytes 3538952 | tf_op jit(solution)/shard_map/ppermute | solution.py:48
  46.5 2.5 %collective-permute-done.there_ref = bf16[4,16,72,128]{3,2,1,0:T(8,128)(2,1)S(1)} collective-permute-done((bf16[4,16,72,128]{3,2,1,0:T(8,128)(2,1)S(1)}, bf16[4,16,72,128]{3,2,1,0:T(8,128)(2,1)S(1)}, u32[]{:S(2)}, u32[]{:S(2)}) %collective-permute-start) | collective-permute-done | bytes 1179680 | tf_op jit(solution)/shard_map/ppermute | solution.py:48
  49.0 0.0 copy-start.2
  49.0 0.0 copy-done
  49.0 1.0 copy-done.2
  50.0 20.8 %attend.1 = (bf16[4,16,72,128]{3,2,1,0:T(8,128)(2,1)}, bf16[4,16,72,128]{3,2,1,0:T(8,128)(2,1)}, bf16[2,2048,512]{2,1,0:T(8,128)(2,1)}, bf16[2048,640]{1,0:T(8,128)(2,1)}) custom-call(s32[1]{0:T(128)} %bitcast.core_ref, s32[2]{0:T(128)} %offsets_ref.1, bf16[4,16,72,128]{3,2,1,0:T(8,128)(2,1)} %copy-done, bf16[4,16,72,128]{3,2,1,0:T(8,128)(2,1)} %copy-done.2, ...), custom_call_target="tpu_custom_call" | custom-call | flops 9663676416 | bytes 12000000 | tf_op jit(solution)/shard_map/attend/pallas_call | solution.py:225
  70.8 0.4 collective-permute-start.1
  71.1 2.7 %collective-permute-done.1 = bf16[4,16,72,128]{3,2,1,0:T(8,128)(2,1)S(1)} collective-permute-done((bf16[4,16,72,128]{3,2,1,0:T(8,128)(2,1)}, bf16[4,16,72,128]{3,2,1,0:T(8,128)(2,1)S(1)}, u32[]{:S(2)}, u32[]{:S(2)}) %collective-permute-start.1) | collective-permute-done | bytes 1179680 | tf_op jit(solution)/shard_map/ppermute | solution.py:48
  73.8 1.6 %add_convert_fusion = bf16[4,16,72,128]{3,2,1,0:T(8,128)(2,1)S(1)} fusion(bf16[4,16,72,128]{3,2,1,0:T(8,128)(2,1)S(1)} %collective-permute-done.1, bf16[4,16,72,128]{3,2,1,0:T(8,128)(2,1)} %get-tuple-element.19), kind=kLoop, calls=%fused_computation | loop fusion | flops 2359296 | bytes 3538944 | tf_op jit(solution)/shard_map/convert_element_type | solution.py:56
  75.4 18.7 %all_to_all.26 = bf16[4,16,72,128]{3,2,1,0:T(8,128)(2,1)S(1)} all-to-all(bf16[4,16,72,128]{3,2,1,0:T(8,128)(2,1)S(1)} %add_convert_fusion), channel_id=1, replica_groups=mesh['z'=8,'y_lo'=2,'x'=4,'y_hi'=2,'core'=2] {'x'}, dimensions={0} | all-to-all | bytes 2359296 | tf_op jit(solution)/shard_map/all_to_all | solution.py:57
  94.1 0.2 reduce_sum.36
  94.3 13.7 %all_to_all.27 = bf16[16,72,128]{2,1,0:T(8,128)(2,1)S(1)} all-to-all(bf16[16,72,128]{2,1,0:T(8,128)(2,1)S(1)} %reduce_sum.36), channel_id=1, replica_groups=mesh['z'=8,'y_lo'=2,'x'=4,'y_hi'=2,'core'=2] {'z','y_lo'}, dimensions={0} | all-to-all | bytes 589824 | tf_op jit(solution)/shard_map/all_to_all | solution.py:58
  108.0 0.8 broadcast_in_dim.11
  108.8 8.1 %all-to-all-start.4 = ((bf16[16,72,128]{2,1,0:T(8,128)(2,1)}), bf16[16,72,128]{2,1,0:T(8,128)(2,1)S(1)}, u32[]{:S(2)}, u32[]{:S(2)}) async-start(bf16[16,72,128]{2,1,0:T(8,128)(2,1)} %broadcast_in_dim.11), calls=%async_computation.4 | async-start | bytes 589824 | tf_op jit(solution)/shard_map/all_to_all | solution.py:44
  116.8 7.8 %query_gradients.1 = (bf16[128,1024]{1,0:T(8,128)(2,1)}, bf16[128,512]{1,0:T(8,128)(2,1)}) custom-call(s32[128,1]{1,0:T(8,128)} %copy.23.scale_ref, bf16[2,2048,512]{2,1,0:T(8,128)(2,1)} %get-tuple-element.21.ds_ref, bf16[2048,640]{1,0:T(8,128)(2,1)} %get-tuple-element.22.cache_ref, bf16[512,1024]{1,0:T(8,128)(2,1)} %key_ref.3), custom_call_target="tpu_custom_call" | custom-call | flops 2684354560 | bytes 9000000 | tf_op jit(solution)/shard_map/query_gradients/pallas_call | solution.py:273
  124.6 1.5 %all-to-all-done.4 = bf16[16,72,128]{2,1,0:T(8,128)(2,1)S(1)} async-done(((bf16[16,72,128]{2,1,0:T(8,128)(2,1)}), bf16[16,72,128]{2,1,0:T(8,128)(2,1)S(1)}, u32[]{:S(2)}, u32[]{:S(2)}) %all-to-all-start.4) | async-done | bytes 294944 | tf_op jit(solution)/shard_map/all_to_all | solution.py:44
  126.0 0.1 reduce_sum.38
  126.1 0.1 fusion
  126.2 0.1 copy.24
  126.3 0.8 copy.26
  (5 shorter events, 0.1 us)
Async XLA Ops:
  0.6 13.2 %copy-start.1 = (s32[128]{0:T(128)S(1)}, s32[128]{0:T(128)}, u32[]{:S(2)}) copy-start(s32[128]{0:T(128)} %param.11) | copy-start | bytes 1540
  3.7 21.4 %all-to-all-start = ((bf16[16,72,128]{2,1,0:T(8,128)(2,1)}), bf16[16,72,128]{2,1,0:T(8,128)(2,1)S(1)}, u32[]{:S(2)}, u32[]{:S(2)}) async-start(bf16[16,72,128]{2,1,0:T(8,128)(2,1)} %broadcast_in_dim.9), calls=%async_computation | async-start | bytes 589824 | tf_op jit(solution)/shard_map/all_to_all | solution.py:44
  43.0 6.0 %copy-start = (bf16[4,16,72,128]{3,2,1,0:T(8,128)(2,1)}, bf16[4,16,72,128]{3,2,1,0:T(8,128)(2,1)S(1)}, u32[]{:S(2)}) copy-start(bf16[4,16,72,128]{3,2,1,0:T(8,128)(2,1)S(1)} %all_to_all.25.here_ref) | copy-start | bytes 3538948
  43.0 6.0 %collective-permute-start = (bf16[4,16,72,128]{3,2,1,0:T(8,128)(2,1)S(1)}, bf16[4,16,72,128]{3,2,1,0:T(8,128)(2,1)S(1)}, u32[]{:S(2)}, u32[]{:S(2)}) collective-permute-start(bf16[4,16,72,128]{3,2,1,0:T(8,128)(2,1)S(1)} %all_to_all.25.here_ref), channel_id=1, source_target_pairs={{0,1},{1,0},{2,3},{3,2},{4,5},{5,4},{6,7},{7,6},{8,9},{9,8},{10,11... | collective-permute-start | bytes 3538952 | tf_op jit(solution)/shard_map/ppermute | solution.py:48
  49.0 1.0 copy-start.2
  70.8 3.1 %collective-permute-start.1 = (bf16[4,16,72,128]{3,2,1,0:T(8,128)(2,1)}, bf16[4,16,72,128]{3,2,1,0:T(8,128)(2,1)S(1)}, u32[]{:S(2)}, u32[]{:S(2)}) collective-permute-start(bf16[4,16,72,128]{3,2,1,0:T(8,128)(2,1)} %get-tuple-element.20), channel_id=1, source_target_pairs={{0,1},{1,0},{2,3},{3,2},{4,5},{5,4},{6,7},{7,6},{8,9},{9,8},{10,11... | collective-permute-start | bytes 3538952 | tf_op jit(solution)/shard_map/ppermute | solution.py:48
  108.8 17.3 %all-to-all-start.4 = ((bf16[16,72,128]{2,1,0:T(8,128)(2,1)}), bf16[16,72,128]{2,1,0:T(8,128)(2,1)S(1)}, u32[]{:S(2)}, u32[]{:S(2)}) async-start(bf16[16,72,128]{2,1,0:T(8,128)(2,1)} %broadcast_in_dim.11), calls=%async_computation.4 | async-start | bytes 589824 | tf_op jit(solution)/shard_map/all_to_all | solution.py:44

commit v3 on v1

v3 whole, which is shorter than its diff:
```python
import functools

import jax
import jax.numpy as jnp
from jax import lax
from jax.experimental import pallas as pl
from jax.experimental.pallas import tpu as pltpu
from jax.sharding import Mesh, PartitionSpec as P

LATENT = 512
ROPE = 64
NOPE = 128
QBLOCK = 64
WIDTH = LATENT + ROPE
LANES = 128
PADDED = LATENT + LANES
KTILE = 512
GROUPS = 2
VMEM = 44 * 2**20
LOG2E = 1.4426950408889634
UNSEEN = -1e30
SEQ = ("z", "y_lo")
HEAD = ("x", "y_hi", "core")
COLS = (((1,), (1,)), ((), ()))


def to_each(block, axes):
    copies = jnp.broadcast_to(block, (lax.axis_size(axes), *block.shape))
    return lax.all_to_all(copies, axes, 0, 0, tiled=True)


def swap_core(block):
    return lax.ppermute(block, "core", [(0, 1), (1, 0)])


def add_up(blocks):
    return jnp.sum(blocks.astype(jnp.float32), axis=0).astype(jnp.bfloat16)


def owned_columns(keep, send):
    half = (keep.astype(jnp.float32) + swap_core(send).astype(jnp.float32)).astype(jnp.bfloat16)
    slices = add_up(lax.all_to_all(half, "x", 0, 0, tiled=True))
    slices = add_up(lax.all_to_all(slices, SEQ, 0, 0, tiled=True))
    parts = to_each(slices, HEAD)
    sizes = [lax.axis_size(axis) for axis in HEAD]
    parts = parts.reshape(*sizes, *slices.shape).astype(jnp.float32)
    parts = jnp.sum(parts, axis=1).astype(jnp.bfloat16)
    return parts.reshape(-1, slices.shape[-1]).T


def project_kernel(scale_ref, nope_ref, rope_ref, key_ref, value_ref, grad_ref, ext_ref, back_ref, ext_t_ref, back_t_ref):
    queries = nope_ref.shape[0]
    heads = key_ref.shape[1] // NOPE
    factor = jnp.exp2(scale_ref[...].astype(jnp.float32))
    dot = functools.partial(lax.dot_general, dimension_numbers=COLS, preferred_element_type=jnp.float32)
    lane = lax.broadcasted_iota(jnp.int32, (queries, LANES), 1)
    for h in range(heads):
        lanes = slice(h * NOPE, (h + 1) * NOPE)
        rows = slice(h * queries, (h + 1) * queries)
        q_nope = (nope_ref[:, lanes].astype(jnp.float32) * factor).astype(jnp.bfloat16)
        ext_ref[rows, :LATENT] = dot(q_nope, key_ref[:, lanes]).astype(jnp.bfloat16)
        ext_t_ref[:LATENT, rows] = dot(key_ref[:, lanes], q_nope).astype(jnp.bfloat16)
        back_ref[rows, :] = dot(grad_ref[:, lanes], value_ref[:, lanes]).astype(jnp.bfloat16)
        back_t_ref[:, rows] = dot(value_ref[:, lanes], grad_ref[:, lanes]).astype(jnp.bfloat16)
        pair = slice(h // 2 * LANES, (h // 2 + 1) * LANES)
        rope = rope_ref[:, pair].astype(jnp.float32) * factor
        if h % 2:
            rope = pltpu.roll(rope, ROPE, 1)
        rope = jnp.where(lane < ROPE, rope, 0.0)
        ext_ref[rows, LATENT:] = rope.astype(jnp.bfloat16)
        ext_t_ref[LATENT:, rows] = rope.T[:ROPE].astype(jnp.bfloat16)


def project(scale_exp, query_nope, query_rope, up_key, up_value, grad_out):
    queries = query_nope.shape[0]
    heads = up_key.shape[1] // NOPE
    rows = heads * queries
    return pl.pallas_call(
        project_kernel,
        out_shape=(
            jax.ShapeDtypeStruct((rows, PADDED), jnp.bfloat16),
            jax.ShapeDtypeStruct((rows, LATENT), jnp.bfloat16),
            jax.ShapeDtypeStruct((WIDTH, rows), jnp.bfloat16),
            jax.ShapeDtypeStruct((LATENT, rows), jnp.bfloat16),
        ),
        compiler_params=pltpu.CompilerParams(vmem_limit_bytes=24 * 2**20),
        cost_estimate=pl.CostEstimate(flops=8 * rows * NOPE * LATENT, bytes_accessed=7_500_000, transcendentals=0),
        name="project",
    )(scale_exp.reshape(queries, 1), query_nope, query_rope, up_key, up_value, grad_out)


def lay_out(cache_buf, here, there, core):
    slices, owners, height = here.shape[:3]
    for x in range(slices):
        for s in range(owners):
            mine, other = here[x, s], there[x, s]
            first = jnp.where(core == 0, mine, other)
            second = jnp.where(core == 0, other, mine)
            both = jnp.concatenate([first, second], axis=0)
            cache_buf[2 * height * x : 2 * height * (x + 1), s * LANES : (s + 1) * LANES] = both


def attend_kernel(core_ref, offsets_ref, here_hbm, there_hbm, ext_hbm, back_hbm, ext_t_hbm, back_t_hbm,
                  keep_hbm, send_hbm, ds_hbm,
                  here, there, ext, back, ext_t, back_t, cache, bias, score, dprob, acc, ds, keep, send,
                  in_sems, ds_sems, keep_sems, send_sems):
    slices, owners, height = here.shape[:3]
    keys_total = cache.shape[1]
    rows_total = ext.shape[0]
    core = core_ref[0]
    scale = (NOPE + ROPE) ** (-0.5)
    loads = [
        pltpu.make_async_copy(src, dst, in_sems.at[i])
        for i, (src, dst) in enumerate(
            ((here_hbm, here), (there_hbm, there), (ext_hbm, ext), (back_hbm, back), (back_t_hbm, back_t), (ext_t_hbm, ext_t)))
    ]
    for load in loads:
        load.start()

    queries = bias.shape[0]
    row = lax.broadcasted_iota(jnp.int32, (queries, keys_total), 0)
    key = lax.broadcasted_iota(jnp.int32, (queries, keys_total), 1)
    last = row % QBLOCK + jnp.where(row < QBLOCK, offsets_ref[0], offsets_ref[1])
    bias[...] = jnp.where(key <= last, 0.0, UNSEEN)
    cache[WIDTH:, :] = jnp.zeros((PADDED - WIDTH, keys_total), jnp.bfloat16)
    loads[0].wait()
    loads[1].wait()
    lay_out(cache, here, there, core)
    loads[2].wait()
    loads[3].wait()

    tiles = keys_total // KTILE
    rows = rows_total // GROUPS

    def fold(values, op):
        parts = [values[:, k : k + LANES] for k in range(0, KTILE, LANES)]
        return functools.reduce(op, parts)

    def span(g, t):
        return slice(g * rows, (g + 1) * rows), slice(t * KTILE, (t + 1) * KTILE)

    tops = [jnp.full((rows, LANES), UNSEEN, jnp.float32)] * GROUPS
    totals = [jnp.zeros((rows, LANES), jnp.float32)] * GROUPS
    deltas = [jnp.zeros((rows, LANES), jnp.float32)] * GROUPS

    def scores(g, t):
        own, keys = span(g, t)
        raw = jnp.dot(ext[own, :], cache[:, keys], preferred_element_type=jnp.float32)
        seen = jnp.concatenate([bias[:, keys]] * (rows // queries), axis=0)
        raw = raw * (scale * LOG2E) + seen
        score[own, keys] = raw
        tops[g] = jnp.maximum(tops[g], fold(raw, jnp.maximum))
        dprob[own, keys] = jnp.dot(back[own, :], cache[:LATENT, keys], preferred_element_type=jnp.float32)
        if t == tiles - 1:
            tops[g] = jnp.max(tops[g], axis=1, keepdims=True)

    def weights(g, t):
        own, keys = span(g, t)
        weight = jnp.exp2(score[own, keys] - tops[g])
        score[own, keys] = weight
        totals[g] = totals[g] + fold(weight, jnp.add)
        if t == tiles - 1:
            totals[g] = 1.0 / jnp.sum(totals[g], axis=1, keepdims=True)

    def values(g, t):
        own, keys = span(g, t)
        probs = (score[own, keys] * totals[g]).astype(jnp.bfloat16)
        part = jnp.dot(back_t[:, own], probs, preferred_element_type=jnp.float32)
        if g == 0:
            acc[:LATENT, keys] = part
        else:
            acc[:LATENT, keys] += part
        deltas[g] = deltas[g] + fold(probs.astype(jnp.float32) * dprob[own, keys], jnp.add)
        if t == tiles - 1:
            deltas[g] = jnp.sum(deltas[g], axis=1, keepdims=True)

    stores = []

    def gradients(g, t):
        own, keys = span(g, t)
        dscore = score[own, keys] * (totals[g] * scale) * (dprob[own, keys] - deltas[g])
        dscore = dscore.astype(jnp.bfloat16)
        ds[own, keys] = dscore
        store = pltpu.make_async_copy(ds.at[own, keys], ds_hbm.at[own, keys], ds_sems.at[g, t])
        store.start()
        stores.append(store)
        part = jnp.dot(ext_t[:, own], dscore, preferred_element_type=jnp.float32)
        acc[:LATENT, keys] += part[:LATENT]
        if g == 0:
            acc[LATENT:, keys] = part[LATENT:]
        else:
            acc[LATENT:, keys] += part[LATENT:]

    def put_out(t):
        per_tile = KTILE // LANES
        mine = slice(t * per_tile, (t + 1) * per_tile)
        for dst, hbm, sems, which in ((send, send_hbm, send_sems, 1 - core), (keep, keep_hbm, keep_sems, core)):
            for x in range(slices):
                start = pl.multiple_of((2 * x + which) * height, 8)
                for s in range(t * per_tile, (t + 1) * per_tile):
                    dst[x, s] = acc[pl.ds(start, height), s * LANES : (s + 1) * LANES].astype(jnp.bfloat16)
            store = pltpu.make_async_copy(dst.at[:, mine], hbm.at[:, mine], sems.at[t])
            store.start()
            stores.append(store)

    stages = (scores, weights, values, gradients)
    for step in range(len(stages) + GROUPS - 1):
        if step == 2:
            loads[4].wait()
            loads[5].wait()
        for t in range(tiles):
            for g in range(GROUPS):
                if 0 <= step - g < len(stages):
                    stages[step - g](g, t)
            if step == len(stages) + GROUPS - 2:
                put_out(t)
    for store in stores:
        store.wait()


def attend(core, offsets, here, there, ext, back, ext_t, back_t):
    rows = ext.shape[0]
    slices, owners = here.shape[:2]
    keys_total = owners * LANES
    queries = offsets.shape[0] * QBLOCK
    tiles = keys_total // KTILE
    smem = pl.BlockSpec(memory_space=pltpu.SMEM)
    place = pl.BlockSpec(memory_space=pl.ANY)
    bf16, f32 = jnp.bfloat16, jnp.float32
    return pl.pallas_call(
        attend_kernel,
        out_shape=(
            jax.ShapeDtypeStruct(here.shape, bf16),
            jax.ShapeDtypeStruct(here.shape, bf16),
            jax.ShapeDtypeStruct((rows, keys_total), bf16),
        ),
        in_specs=[smem, smem] + [place] * 6,
        out_specs=(place, place, place),
        scratch_shapes=[
            pltpu.VMEM(here.shape, bf16),
            pltpu.VMEM(here.shape, bf16),
            pltpu.VMEM(ext.shape, bf16),
            pltpu.VMEM(back.shape, bf16),
            pltpu.VMEM(ext_t.shape, bf16),
            pltpu.VMEM(back_t.shape, bf16),
            pltpu.VMEM((PADDED, keys_total), bf16),
            pltpu.VMEM((queries, keys_total), f32),
            pltpu.VMEM((rows, keys_total), f32),
            pltpu.VMEM((rows, keys_total), f32),
            pltpu.VMEM((WIDTH, keys_total), f32),
            pltpu.VMEM((rows, keys_total), bf16),
            pltpu.VMEM(here.shape, bf16),
            pltpu.VMEM(here.shape, bf16),
            pltpu.SemaphoreType.DMA((6,)),
            pltpu.SemaphoreType.DMA((GROUPS, tiles)),
            pltpu.SemaphoreType.DMA((tiles,)),
            pltpu.SemaphoreType.DMA((tiles,)),
        ],
        compiler_params=pltpu.CompilerParams(vmem_limit_bytes=VMEM),
        cost_estimate=pl.CostEstimate(
            flops=2 * rows * keys_total * (2 * PADDED + 2 * LATENT),
            bytes_accessed=14_000_000, transcendentals=rows * keys_total),
        name="attend",
    )(core.reshape(1), offsets, here, there, ext, back, ext_t, back_t)


def query_kernel(core_ref, scale_ref, ds_ref, here_ref, there_ref, key_ref, nope_ref, rope_ref, cache, grad_buf):
    queries = nope_ref.shape[0]
    heads = key_ref.shape[1] // NOPE
    factor = jnp.exp2(scale_ref[...].astype(jnp.float32))
    lay_out(cache, here_ref, there_ref, core_ref[0])
    cache[WIDTH:, :] = jnp.zeros((PADDED - WIDTH, cache.shape[1]), jnp.bfloat16)
    grad_buf[...] = lax.dot_general(ds_ref[...], cache[...], COLS, preferred_element_type=jnp.float32)
    for h in range(heads):
        lanes = slice(h * NOPE, (h + 1) * NOPE)
        grad = grad_buf[h * queries : (h + 1) * queries, :]
        nope = jnp.dot(grad[:, :LATENT].astype(jnp.bfloat16), key_ref[:, lanes], preferred_element_type=jnp.float32)
        nope_ref[:, lanes] = (nope * factor).astype(jnp.bfloat16)
        rope = grad[:, LATENT:] * factor
        if h % 2 == 0:
            even = rope
        else:
            pair = slice(h // 2 * LANES, (h // 2 + 1) * LANES)
            rope_ref[:, pair] = (even + pltpu.roll(rope, ROPE, 1)).astype(jnp.bfloat16)


def query_gradients(core, scale_exp, dscore, here, there, up_key):
    rows, keys_total = dscore.shape
    heads = up_key.shape[1] // NOPE
    queries = rows // heads
    smem = pl.BlockSpec(memory_space=pltpu.SMEM)
    vmem = pl.BlockSpec(memory_space=pltpu.VMEM)
    return pl.pallas_call(
        query_kernel,
        out_shape=(
            jax.ShapeDtypeStruct((queries, heads * NOPE), jnp.bfloat16),
            jax.ShapeDtypeStruct((queries, heads * ROPE), jnp.bfloat16),
        ),
        in_specs=[smem] + [vmem] * 5,
        scratch_shapes=[pltpu.VMEM((PADDED, keys_total), jnp.bfloat16), pltpu.VMEM((rows, PADDED), jnp.float32)],
        compiler_params=pltpu.CompilerParams(vmem_limit_bytes=32 * 2**20),
        cost_estimate=pl.CostEstimate(
            flops=2 * rows * keys_total * PADDED, bytes_accessed=9_000_000, transcendentals=0),
        name="query_gradients",
    )(core.reshape(1), scale_exp.reshape(queries, 1), dscore, here, there, up_key)


def per_device(cache, query_nope, query_rope, scale_exp, offsets, up_key, up_value, grad_out):
    core = lax.axis_index("core").astype(jnp.int32)
    own = lax.axis_index(("x", "core"))
    height = WIDTH // (lax.axis_size("x") * lax.axis_size("core"))
    mine = lax.dynamic_slice_in_dim(cache.T, own * height, height, 0)
    over_seq = to_each(mine, SEQ)
    projected = project(scale_exp, query_nope, query_rope, up_key, up_value, grad_out)
    over_seq, projected = lax.optimization_barrier((over_seq, projected))
    here = to_each(over_seq, "x")
    there = swap_core(here)
    keep, send, dscore = attend(core, offsets, here, there, *projected)
    d_cache = owned_columns(keep, send)
    d_query_nope, d_query_rope = query_gradients(core, scale_exp, dscore, here, there, up_key)
    return (d_cache, d_query_nope, d_query_rope)


def solution(mesh):
    wide = Mesh(mesh.devices.reshape(8, 2, 4, 2, 2), SEQ + HEAD)
    in_specs = (
        P(SEQ, None),
        P(SEQ, HEAD),
        P(SEQ, HEAD),
        P(SEQ),
        P(SEQ),
        P(None, HEAD),
        P(None, HEAD),
        P(SEQ, HEAD),
    )
    out_specs = (P(SEQ, None), P(SEQ, HEAD), P(SEQ, HEAD))
    return jax.shard_map(per_device, mesh=wide, in_specs=in_specs, out_specs=out_specs, check_vma=False)
```

time: 152 us -> 120 us (0.79)
  Pallas kernels: 0 us -> 23.1 us
  matrix products: 20.7 us -> 0 us
  waiting for transfers between devices: 25.2 us -> 9.5 us
  other arithmetic: 16.6 us -> 1.25 us
  local copies, waits for them, and re-layouts: 26.9 us -> 12.2 us
  blocking collectives: 41 us -> 50.8 us
  starting transfers between devices: 19.6 us -> 22.2 us
    pallas_call x0 -> x3, Pallas kernels: none -> 23.1 us  [the longest x1 16.8 us: attend(): pl.pallas_call(attend_kernel, out_shape=(jax.ShapeDtypeStruct(here.shape,...]
    dot_general x8 -> x0, matrix products: 20.7 us -> none  [the longest x1 4.48 us: per_device(): grad_ext = jnp.dot(dscore, whole, preferred_element_type=jnp.float32)]
    all_to_all x2, waiting for transfers between devices: 18.6 us -> 4.55 us  [to_each(): return lax.all_to_all(copies, axes, 0, 0, tiled=True)]
    all_to_all x1 -> x2, blocking collectives: 19.6 us -> 33 us  [the longest x1 18.7 us: owned_columns(): slices = add_up(lax.all_to_all(half, 'x', 0, 0, tiled=True))]
    reshape x8 -> x1, local copies, waits for them, and re-layouts: 11.2 us -> 0.76 us  [project(): scale_exp.reshape(queries, 1)]
    convert_element_type x5 -> x1, other arithmetic: 5.9 us -> 0.31 us  [owned_columns(): (keep.astype(jnp.float32) + swap_core(send).astype(jnp.float32)).astype(j...]
    all_to_all x2, starting transfers between devices: 12.6 us -> 18.2 us  [to_each(): return lax.all_to_all(copies, axes, 0, 0, tiled=True)]
    slice x7 -> x0, local copies, waits for them, and re-layouts: 4.06 us -> none  [the longest x1 1.71 us: pack_all(): latent = rows[..., :LATENT].reshape(*lead, ROWS, LATENT // LANES, LANES)]
  transfers between devices with their start and end apart: 5 -> 4, of which waited for: 4 -> 4; matrix products, arithmetic and copies ran while one was open for 9% -> 1% of each run, Pallas kernels for 0% -> 5%
where the time goes in v3:
time: 120 us
  blocking collectives  50.8 us (42%)
  Pallas kernels  23.1 us (19%)
  starting transfers between devices  22.2 us (18%)
  local copies, waits for them, and re-layouts  12.2 us (10%)
  waiting for transfers between devices  9.5 us (8%)
  other arithmetic  1.25 us (1%)
    all_to_all x1, blocking collectives, owned_columns(): slices = add_up(lax.all_to_all(half, 'x', 0, 0, tiled=True))  18.7 us
    all_to_all x2, starting transfers between devices, to_each(): return lax.all_to_all(copies, axes, 0, 0, tiled=True)  18.2 us
    all_to_all x1, blocking collectives, to_each(): return lax.all_to_all(copies, axes, 0, 0, tiled=True)  17.9 us
    pallas_call x1, Pallas kernels, attend(): pl.pallas_call(attend_kernel, out_shape=(jax.ShapeDtypeStruct(here.shape,...  16.8 us
    all_to_all x1, blocking collectives, owned_columns(): slices = add_up(lax.all_to_all(slices, SEQ, 0, 0, tiled=True))  14.3 us
    unnamed x30, local copies, waits for them, and re-layouts  9.79 us
    ppermute x2, waiting for transfers between devices, swap_core(): return lax.ppermute(block, 'core', [(0, 1), (1, 0)])  4.95 us
    pallas_call x1, Pallas kernels, query_gradients(): pl.pallas_call(query_kernel, out_shape=(jax.ShapeDtypeStruct((queries, he...  4.87 us
  transfers between devices with their start and end apart: 4, of which 4 were waited for; matrix products, arithmetic and copies ran while one was open for 1% of the time, Pallas kernels for 5%

profile of v3, /device:TPU:1, one launch (start us, length us, event | category | flops | bytes accessed | tf_op | source)
XLA Modules:
  0.0 119.9 jit_solution(1223205816450427574)
XLA Ops:
  0.6 0.0 copy-start
  0.6 0.0 copy-start.5
  0.7 0.0 copy-start.4
  0.7 0.9 copy-done
  1.6 0.8 broadcast_in_dim.9
  2.3 10.1 %all-to-all-start = ((bf16[16,72,128]{2,1,0:T(8,128)(2,1)}), bf16[16,72,128]{2,1,0:T(8,128)(2,1)S(1)}, u32[]{:S(2)}, u32[]{:S(2)}) async-start(bf16[16,72,128]{2,1,0:T(8,128)(2,1)} %broadcast_in_dim.9), calls=%async_computation | async-start | bytes 589824 | tf_op jit(solution)/shard_map/all_to_all | solution.py:29
  12.5 0.8 copy.13.scale_ref
  13.2 0.0 copy-done.5
  13.2 0.0 copy-done.4
  13.2 0.0 copy-start.1
  13.2 1.2 %copy-done.1 = bf16[512,1024]{1,0:T(8,128)(2,1)S(1)} copy-done((bf16[512,1024]{1,0:T(8,128)(2,1)S(1)}, bf16[512,1024]{1,0:T(8,128)(2,1)}, u32[]{:S(2)}) %copy-start.1) | copy-done | bytes 1048600
  14.5 0.0 copy-start.2
  14.5 1.2 %copy-done.2 = bf16[512,1024]{1,0:T(8,128)(2,1)S(1)} copy-done((bf16[512,1024]{1,0:T(8,128)(2,1)S(1)}, bf16[512,1024]{1,0:T(8,128)(2,1)}, u32[]{:S(2)}) %copy-start.2) | copy-done | bytes 1048600
  15.7 0.0 copy-start.6
  15.7 0.9 copy-done.6
  16.6 1.4 %project.1 = (bf16[1024,640]{1,0:T(8,128)(2,1)S(1)}, bf16[1024,512]{1,0:T(8,128)(2,1)S(1)}, bf16[576,1024]{1,0:T(8,128)(2,1)S(1)}, bf16[512,1024]{1,0:T(8,128)(2,1)S(1)}) custom-call(s32[128,1]{1,0:T(8,128)S(1)} %copy.13.scale_ref, bf16[128,1024]{1,0:T(8,128)(2,1)S(1)} %copy-done.4, bf16[128,512]{1,0:T(8,128)(2,1)S(1)} %copy-done.6, ...), custom_call_target="tpu_custom_call" | custom-call | flops 536870912 | bytes 7500000 | tf_op jit(solution)/shard_map/project/pallas_call | solution.py:78
  18.0 0.0 copy-start.7
  18.0 1.1 copy-done.7
  19.0 1.0 copy-done.11
  20.0 3.7 %all-to-all-done = bf16[16,72,128]{2,1,0:T(8,128)(2,1)S(1)} async-done(((bf16[16,72,128]{2,1,0:T(8,128)(2,1)}), bf16[16,72,128]{2,1,0:T(8,128)(2,1)S(1)}, u32[]{:S(2)}, u32[]{:S(2)}) %all-to-all-start) | async-done | bytes 294944 | tf_op jit(solution)/shard_map/all_to_all | solution.py:29
  23.7 0.0 copy-start.12
  23.7 0.2 broadcast_in_dim.10
  23.9 0.0 copy-start.8
  23.9 0.0 copy-start.13
  23.9 17.9 %all_to_all.25.here_hbm.here_ref = bf16[4,16,72,128]{3,2,1,0:T(8,128)(2,1)S(1)} all-to-all(bf16[4,16,72,128]{3,2,1,0:T(8,128)(2,1)S(1)} %broadcast_in_dim.10), channel_id=1, replica_groups=mesh['z'=8,'y_lo'=2,'x'=4,'y_hi'=2,'core'=2] {'x'}, dimensions={0} | all-to-all | bytes 2359296 | tf_op jit(solution)/shard_map/all_to_all | solution.py:29
  41.8 3.5 %collective-permute-start = (bf16[4,16,72,128]{3,2,1,0:T(8,128)(2,1)S(1)}, bf16[4,16,72,128]{3,2,1,0:T(8,128)(2,1)S(1)}, u32[]{:S(2)}, u32[]{:S(2)}) collective-permute-start(bf16[4,16,72,128]{3,2,1,0:T(8,128)(2,1)S(1)} %all_to_all.25.here_hbm.here_ref), channel_id=1, source_target_pairs={{0,1},{1,0},{2,3},{3,2},{4,5},{5,4},{6,7},{7,6},{8,9},{9,8},{10,11... | collective-permute-start | bytes 3538952 | tf_op jit(solution)/shard_map/ppermute | solution.py:33
  45.3 2.5 %collective-permute-done.there_hbm.there_ref = bf16[4,16,72,128]{3,2,1,0:T(8,128)(2,1)S(1)} collective-permute-done((bf16[4,16,72,128]{3,2,1,0:T(8,128)(2,1)S(1)}, bf16[4,16,72,128]{3,2,1,0:T(8,128)(2,1)S(1)}, u32[]{:S(2)}, u32[]{:S(2)}) %collective-permute-start) | collective-permute-done | bytes 1179680 | tf_op jit(solution)/shard_map/ppermute | solution.py:33
  47.8 0.0 copy-done.12
  47.8 0.0 copy-done.8
  47.8 0.0 copy-done.13
  47.8 16.8 %attend.1 = (bf16[4,16,72,128]{3,2,1,0:T(8,128)(2,1)S(1)}, bf16[4,16,72,128]{3,2,1,0:T(8,128)(2,1)S(1)}, bf16[1024,2048]{1,0:T(8,128)(2,1)}) custom-call(s32[1]{0:T(128)} %bitcast.core_ref, s32[2]{0:T(128)S(1)} %copy-done.13, bf16[4,16,72,128]{3,2,1,0:T(8,128)(2,1)S(1)} %all_to_all.25.here_hbm.here_ref, ...), custom_call_target="tpu_custom_call" | custom-call | flops 9663676416 | bytes 14000000 | tf_op jit(solution)/shard_map/attend/pallas_call | solution.py:230
  64.6 0.0 copy-done.9
  64.6 0.5 collective-permute-start.1
  65.1 2.5 %collective-permute-done.1 = bf16[4,16,72,128]{3,2,1,0:T(8,128)(2,1)S(1)} collective-permute-done((bf16[4,16,72,128]{3,2,1,0:T(8,128)(2,1)S(1)}, bf16[4,16,72,128]{3,2,1,0:T(8,128)(2,1)S(1)}, u32[]{:S(2)}, u32[]{:S(2)}) %collective-permute-start.1) | collective-permute-done | bytes 1179680 | tf_op jit(solution)/shard_map/ppermute | solution.py:33
  67.6 0.3 add_convert_fusion
  67.9 18.7 %all_to_all.26 = bf16[4,16,72,128]{3,2,1,0:T(8,128)(2,1)S(1)} all-to-all(bf16[4,16,72,128]{3,2,1,0:T(8,128)(2,1)S(1)} %add_convert_fusion), channel_id=1, replica_groups=mesh['z'=8,'y_lo'=2,'x'=4,'y_hi'=2,'core'=2] {'x'}, dimensions={0} | all-to-all | bytes 2359296 | tf_op jit(solution)/shard_map/all_to_all | solution.py:42
  86.6 0.2 reduce_sum.36
  86.8 0.0 copy-start.3
  86.8 14.3 %all_to_all.27 = bf16[16,72,128]{2,1,0:T(8,128)(2,1)S(1)} all-to-all(bf16[16,72,128]{2,1,0:T(8,128)(2,1)S(1)} %reduce_sum.36), channel_id=1, replica_groups=mesh['z'=8,'y_lo'=2,'x'=4,'y_hi'=2,'core'=2] {'z','y_lo'}, dimensions={0} | all-to-all | bytes 589824 | tf_op jit(solution)/shard_map/all_to_all | solution.py:43
  101.1 0.8 broadcast_in_dim.11
  101.9 8.1 %all-to-all-start.4 = ((bf16[16,72,128]{2,1,0:T(8,128)(2,1)}), bf16[16,72,128]{2,1,0:T(8,128)(2,1)S(1)}, u32[]{:S(2)}, u32[]{:S(2)}) async-start(bf16[16,72,128]{2,1,0:T(8,128)(2,1)} %broadcast_in_dim.11), calls=%async_computation.4 | async-start | bytes 589824 | tf_op jit(solution)/shard_map/all_to_all | solution.py:29
  109.9 0.0 copy-done.3
  109.9 0.0 copy-start.10
  109.9 1.3 %copy-done.10 = bf16[4,16,72,128]{3,2,1,0:T(8,128)(2,1)S(1)} copy-done((bf16[4,16,72,128]{3,2,1,0:T(8,128)(2,1)S(1)}, bf16[4,16,72,128]{3,2,1,0:T(8,128)(2,1)}, u32[]{:S(2)}) %copy-start.10) | copy-done | bytes 1179672
  111.2 2.2 %copy-done.14 = bf16[1024,2048]{1,0:T(8,128)(2,1)S(1)} copy-done((bf16[1024,2048]{1,0:T(8,128)(2,1)S(1)}, bf16[1024,2048]{1,0:T(8,128)(2,1)}, u32[]{:S(2)}) %copy-start.14) | copy-done | bytes 4194328
  113.4 4.9 %query_gradients.1 = (bf16[128,1024]{1,0:T(8,128)(2,1)}, bf16[128,512]{1,0:T(8,128)(2,1)}) custom-call(s32[1]{0:T(128)} %bitcast.core_ref, s32[128,1]{1,0:T(8,128)S(1)} %copy.13.scale_ref, bf16[1024,2048]{1,0:T(8,128)(2,1)S(1)} %copy-done.14, bf16[4,16,72,128]{3,2,1,0:T(8,128)(2,1)S(1)} %all_to_all.25.here_hbm.here_ref, ...), custom_call_target="tpu_custom_call" | custom-call | flops 2684354560 | bytes 9000000 | tf_op jit(solution)/shard_map/query_gradients/pallas_call | solution.py:293
  118.3 0.9 all-to-all-done.4
  119.1 0.7 reduce_sum.38
  (5 shorter events, 0.1 us)
Async XLA Ops:
  0.6 0.9 copy-start
  0.6 12.6 %copy-start.5 = (bf16[128,1024]{1,0:T(8,128)(2,1)S(1)}, bf16[128,1024]{1,0:T(8,128)(2,1)}, u32[]{:S(2)}) copy-start(bf16[128,1024]{1,0:T(8,128)(2,1)} %grad_ref.1) | copy-start | bytes 786436
  0.7 12.6 %copy-start.4 = (bf16[128,1024]{1,0:T(8,128)(2,1)S(1)}, bf16[128,1024]{1,0:T(8,128)(2,1)}, u32[]{:S(2)}) copy-start(bf16[128,1024]{1,0:T(8,128)(2,1)} %nope_ref.1) | copy-start | bytes 786436
  2.3 21.4 %all-to-all-start = ((bf16[16,72,128]{2,1,0:T(8,128)(2,1)}), bf16[16,72,128]{2,1,0:T(8,128)(2,1)S(1)}, u32[]{:S(2)}, u32[]{:S(2)}) async-start(bf16[16,72,128]{2,1,0:T(8,128)(2,1)} %broadcast_in_dim.9), calls=%async_computation | async-start | bytes 589824 | tf_op jit(solution)/shard_map/all_to_all | solution.py:29
  13.2 1.2 %copy-start.1 = (bf16[512,1024]{1,0:T(8,128)(2,1)S(1)}, bf16[512,1024]{1,0:T(8,128)(2,1)}, u32[]{:S(2)}) copy-start(bf16[512,1024]{1,0:T(8,128)(2,1)} %value_ref.1) | copy-start | bytes 3145732
  14.5 1.2 %copy-start.2 = (bf16[512,1024]{1,0:T(8,128)(2,1)S(1)}, bf16[512,1024]{1,0:T(8,128)(2,1)}, u32[]{:S(2)}) copy-start(bf16[512,1024]{1,0:T(8,128)(2,1)} %key_ref.3) | copy-start | bytes 3145732
  15.7 0.9 copy-start.6
  18.0 1.1 copy-start.7
  19.0 1.0 copy-start.11
  23.7 24.1 %copy-start.12 = (bf16[576,1024]{1,0:T(8,128)(2,1)S(1)}, bf16[576,1024]{1,0:T(8,128)(2,1)}, u32[]{:S(2)}) copy-start(bf16[576,1024]{1,0:T(8,128)(2,1)} %copy-done.11) | copy-start | bytes 3538948
  23.9 23.9 %copy-start.8 = (bf16[1024,640]{1,0:T(8,128)(2,1)S(1)}, bf16[1024,640]{1,0:T(8,128)(2,1)}, u32[]{:S(2)}) copy-start(bf16[1024,640]{1,0:T(8,128)(2,1)} %copy-done.7) | copy-start | bytes 3932164
  23.9 23.9 %copy-start.13 = (s32[2]{0:T(128)S(1)}, s32[2]{0:T(128)}, u32[]{:S(2)}) copy-start(s32[2]{0:T(128)} %offsets_ref.1) | copy-start | bytes 28
  41.8 6.0 %collective-permute-start = (bf16[4,16,72,128]{3,2,1,0:T(8,128)(2,1)S(1)}, bf16[4,16,72,128]{3,2,1,0:T(8,128)(2,1)S(1)}, u32[]{:S(2)}, u32[]{:S(2)}) collective-permute-start(bf16[4,16,72,128]{3,2,1,0:T(8,128)(2,1)S(1)} %all_to_all.25.here_hbm.here_ref), channel_id=1, source_target_pairs={{0,1},{1,0},{2,3},{3,2},{4,5},{5,4},{6,7},{7,6},{8,9},{9,8},{10,11... | collective-permute-start | bytes 3538952 | tf_op jit(solution)/shard_map/ppermute | solution.py:33
  47.8 16.8 %copy-start.9 = (bf16[4,16,72,128]{3,2,1,0:T(8,128)(2,1)}, bf16[4,16,72,128]{3,2,1,0:T(8,128)(2,1)S(1)}, u32[]{:S(2)}) copy-start(bf16[4,16,72,128]{3,2,1,0:T(8,128)(2,1)S(1)} %collective-permute-done.there_hbm.there_ref) | copy-start | bytes 3538948
  64.6 2.9 %collective-permute-start.1 = (bf16[4,16,72,128]{3,2,1,0:T(8,128)(2,1)S(1)}, bf16[4,16,72,128]{3,2,1,0:T(8,128)(2,1)S(1)}, u32[]{:S(2)}, u32[]{:S(2)}) collective-permute-start(bf16[4,16,72,128]{3,2,1,0:T(8,128)(2,1)S(1)} %get-tuple-element.27), channel_id=1, source_target_pairs={{0,1},{1,0},{2,3},{3,2},{4,5},{5,4},{6,7},{7,6},{8,9},{9,8},{10,11... | collective-permute-start | bytes 3538952 | tf_op jit(solution)/shard_map/ppermute | solution.py:33
  86.8 23.2 %copy-start.3 = (bf16[512,1024]{1,0:T(8,128)(2,1)S(1)}, bf16[512,1024]{1,0:T(8,128)(2,1)}, u32[]{:S(2)}) copy-start(bf16[512,1024]{1,0:T(8,128)(2,1)} %key_ref.3) | copy-start | bytes 3145732
  101.9 17.3 %all-to-all-start.4 = ((bf16[16,72,128]{2,1,0:T(8,128)(2,1)}), bf16[16,72,128]{2,1,0:T(8,128)(2,1)S(1)}, u32[]{:S(2)}, u32[]{:S(2)}) async-start(bf16[16,72,128]{2,1,0:T(8,128)(2,1)} %broadcast_in_dim.11), calls=%async_computation.4 | async-start | bytes 589824 | tf_op jit(solution)/shard_map/all_to_all | solution.py:29
  109.9 1.3 %copy-start.10 = (bf16[4,16,72,128]{3,2,1,0:T(8,128)(2,1)S(1)}, bf16[4,16,72,128]{3,2,1,0:T(8,128)(2,1)}, u32[]{:S(2)}) copy-start(bf16[4,16,72,128]{3,2,1,0:T(8,128)(2,1)} %copy-done.9) | copy-start | bytes 3538948
  111.2 2.2 %copy-start.14 = (bf16[1024,2048]{1,0:T(8,128)(2,1)S(1)}, bf16[1024,2048]{1,0:T(8,128)(2,1)}, u32[]{:S(2)}) copy-start(bf16[1024,2048]{1,0:T(8,128)(2,1)} %get-tuple-element.28.ds_ref) | copy-start | bytes 12582916

commit v4 on v3

v4 whole, which is shorter than its diff:
```python
import functools

import jax
import jax.numpy as jnp
from jax import lax
from jax.experimental import pallas as pl
from jax.experimental.pallas import tpu as pltpu
from jax.sharding import Mesh, PartitionSpec as P

LATENT = 512
ROPE = 64
NOPE = 128
QBLOCK = 64
WIDTH = LATENT + ROPE
LANES = 128
PADDED = LATENT + LANES
KTILE = 1024
GROUPS = 1
VMEM = 44 * 2**20
LOG2E = 1.4426950408889634
UNSEEN = -1e30
SEQ = ("z", "y_lo")
HEAD = ("x", "y_hi", "core")
COLS = (((1,), (1,)), ((), ()))


def to_each(block, axes):
    copies = jnp.broadcast_to(block, (lax.axis_size(axes), *block.shape))
    return lax.all_to_all(copies, axes, 0, 0, tiled=True)


def swap_core(block):
    return lax.ppermute(block, "core", [(0, 1), (1, 0)])


def add_up(blocks):
    return jnp.sum(blocks.astype(jnp.float32), axis=0).astype(jnp.bfloat16)


def to_next(block):
    size = lax.axis_size("x")
    return lax.ppermute(block, "x", [(i, (i + 1) % size) for i in range(size)])


def to_previous(block):
    size = lax.axis_size("x")
    return lax.ppermute(block, "x", [(i, (i - 1) % size) for i in range(size)])


def gather_over_x(block):
    half = block.shape[0] // 2
    low, high = block[:half], block[half:]
    after_low, before_high = to_previous(low), to_next(high)
    after_high, before_low = to_previous(high), to_next(low)
    far_low, far_high = to_previous(after_low), to_next(before_high)
    return [low, high, after_low, after_high, far_low, far_high, before_low, before_high]


def reduce_over_x(own, after, far, before):
    def send(shift, block):
        return shift(block.astype(jnp.bfloat16)).astype(jnp.float32)

    low = send(to_next, far[0])
    high = send(to_previous, far[1])
    from_before_high = send(to_next, after[1])
    from_after_low = send(to_previous, before[0])
    from_before_low = send(to_next, after[0] + low)
    from_after_high = send(to_previous, before[1] + high)
    return [
        (own[0] + from_before_low + from_after_low).astype(jnp.bfloat16),
        (own[1] + from_before_high + from_after_high).astype(jnp.bfloat16),
    ]


def core_sums(keeps, sends):
    half = keeps[0].shape[0] // 2
    sums = [None] * 4
    for i in (2, 1, 3, 0):
        other = swap_core(sends[i])
        sums[i] = [
            keeps[i][part].astype(jnp.float32) + other[part].astype(jnp.float32)
            for part in (slice(0, half), slice(half, None))
        ]
    return sums


def owned_columns(slices):
    parts = to_each(slices, HEAD)
    sizes = [lax.axis_size(axis) for axis in HEAD]
    parts = parts.reshape(*sizes, *slices.shape).astype(jnp.float32)
    parts = jnp.sum(parts, axis=1).astype(jnp.bfloat16)
    return parts.reshape(-1, slices.shape[-1]).T


def project_kernel(scale_ref, nope_hbm, rope_hbm, key_hbm, value_hbm, grad_hbm, ext_ref, back_ref, ext_t_ref, back_t_ref,
                   nope, rope_in, up_key, up_value, grad, sems):
    queries = nope.shape[0]
    heads = up_key.shape[1] // NOPE
    loads = [
        pltpu.make_async_copy(src, dst, sems.at[i])
        for i, (src, dst) in enumerate(
            ((nope_hbm, nope), (key_hbm, up_key), (rope_hbm, rope_in), (grad_hbm, grad), (value_hbm, up_value)))
    ]
    for load in loads:
        load.start()
    factor = jnp.exp2(scale_ref[...].astype(jnp.float32))
    dot = functools.partial(lax.dot_general, dimension_numbers=COLS, preferred_element_type=jnp.float32)
    lane = lax.broadcasted_iota(jnp.int32, (queries, LANES), 1)
    for load in loads[:3]:
        load.wait()
    for h in range(heads):
        lanes = slice(h * NOPE, (h + 1) * NOPE)
        rows = slice(h * queries, (h + 1) * queries)
        q_nope = (nope[:, lanes].astype(jnp.float32) * factor).astype(jnp.bfloat16)
        ext_ref[rows, :LATENT] = dot(q_nope, up_key[:, lanes]).astype(jnp.bfloat16)
        ext_t_ref[:LATENT, rows] = dot(up_key[:, lanes], q_nope).astype(jnp.bfloat16)
        pair = slice(h // 2 * LANES, (h // 2 + 1) * LANES)
        rope = rope_in[:, pair].astype(jnp.float32) * factor
        if h % 2:
            rope = pltpu.roll(rope, ROPE, 1)
        rope = jnp.where(lane < ROPE, rope, 0.0)
        ext_ref[rows, LATENT:] = rope.astype(jnp.bfloat16)
        ext_t_ref[LATENT:, rows] = rope.T[:ROPE].astype(jnp.bfloat16)
    for load in loads[3:]:
        load.wait()
    for h in range(heads):
        lanes = slice(h * NOPE, (h + 1) * NOPE)
        rows = slice(h * queries, (h + 1) * queries)
        back_ref[rows, :] = dot(grad[:, lanes], up_value[:, lanes]).astype(jnp.bfloat16)
        back_t_ref[:, rows] = dot(up_value[:, lanes], grad[:, lanes]).astype(jnp.bfloat16)


def project(scales, query_nope, query_rope, up_key, up_value, grad_out):
    queries = query_nope.shape[0]
    heads = up_key.shape[1] // NOPE
    rows = heads * queries
    vmem = pl.BlockSpec(memory_space=pltpu.VMEM)
    any_place = pl.BlockSpec(memory_space=pl.ANY)
    operands = (query_nope, query_rope, up_key, up_value, grad_out)
    return pl.pallas_call(
        project_kernel,
        out_shape=(
            jax.ShapeDtypeStruct((rows, PADDED), jnp.bfloat16),
            jax.ShapeDtypeStruct((rows, LATENT), jnp.bfloat16),
            jax.ShapeDtypeStruct((WIDTH, rows), jnp.bfloat16),
            jax.ShapeDtypeStruct((LATENT, rows), jnp.bfloat16),
        ),
        in_specs=[vmem] + [any_place] * len(operands),
        scratch_shapes=[pltpu.VMEM(array.shape, array.dtype) for array in operands]
        + [pltpu.SemaphoreType.DMA((len(operands),))],
        compiler_params=pltpu.CompilerParams(vmem_limit_bytes=58 * 2**20),
        cost_estimate=pl.CostEstimate(flops=8 * rows * NOPE * LATENT, bytes_accessed=7_500_000, transcendentals=0),
        name="project",
    )(scales, *operands)


def fill_cache(cache, blocks, place, core, sems):
    slices = len(blocks) // 4
    half, height = blocks[0].shape[:2]
    copies = []
    for i, block in enumerate(blocks):
        which = core if i < 2 * slices else 1 - core
        x = (place + i % (2 * slices) // 2) % slices
        start = pl.multiple_of((2 * x + which) * height, 8)
        owners = pl.ds(i % 2 * half, half)
        copy = pltpu.make_async_copy(block, cache.at[owners, pl.ds(start, height), :], sems.at[i])
        copy.start()
        copies.append(copy)
    return copies


def keys_of(cache, first, count, features):
    return jnp.concatenate([cache[s, :features, :] for s in range(first, first + count)], axis=1)


def attend_kernel(place_ref, offsets_ref, *refs):
    blocks_hbm, refs = refs[:16], refs[16:]
    (ext_hbm, back_hbm, ext_t_hbm, back_t_hbm), outs_hbm, (ds_hbm, cache_hbm), refs = refs[:4], refs[4:12], refs[12:14], refs[14:]
    (ext, back, ext_t, back_t, cache, bias, score, dprob, acc, ds, outs,
     block_sems, in_sems, ds_sems, out_sems) = refs
    slices = len(outs_hbm) // 2
    height = outs_hbm[0].shape[1]
    place, core = place_ref[0], place_ref[1]
    owners = cache.shape[0]
    keys_total = owners * LANES
    rows_total = ext.shape[0]
    scale = (NOPE + ROPE) ** (-0.5)
    block_loads = fill_cache(cache, blocks_hbm, place, core, block_sems)
    loads = [
        pltpu.make_async_copy(src, dst, in_sems.at[i])
        for i, (src, dst) in enumerate(
            ((ext_hbm, ext), (back_hbm, back), (back_t_hbm, back_t), (ext_t_hbm, ext_t)))
    ]
    loads[0].start()

    queries = bias.shape[0]
    row = lax.broadcasted_iota(jnp.int32, (queries, keys_total), 0)
    key = lax.broadcasted_iota(jnp.int32, (queries, keys_total), 1)
    last = row % QBLOCK + jnp.where(row < QBLOCK, offsets_ref[0], offsets_ref[1])
    bias[...] = jnp.where(key <= last, 0.0, UNSEEN)
    cache[:, WIDTH:, :] = jnp.zeros((owners, PADDED - WIDTH, LANES), jnp.bfloat16)
    for load in block_loads:
        load.wait()
    loads[0].wait()
    for load in loads[1:]:
        load.start()

    tiles = keys_total // KTILE
    per_tile = KTILE // LANES
    rows = rows_total // GROUPS

    def fold(values, op):
        parts = [values[:, k : k + LANES] for k in range(0, KTILE, LANES)]
        return functools.reduce(op, parts)

    def span(g, t):
        return slice(g * rows, (g + 1) * rows), slice(t * KTILE, (t + 1) * KTILE)

    tops = [jnp.full((rows, LANES), UNSEEN, jnp.float32)] * GROUPS
    totals = [jnp.zeros((rows, LANES), jnp.float32)] * GROUPS
    deltas = [jnp.zeros((rows, LANES), jnp.float32)] * GROUPS

    def scores(g, t):
        own, keys = span(g, t)
        mine = keys_of(cache, t * per_tile, per_tile, PADDED)
        raw = jnp.dot(ext[own, :], mine, preferred_element_type=jnp.float32)
        seen = jnp.concatenate([bias[:, keys]] * (rows // queries), axis=0)
        raw = raw * (scale * LOG2E) + seen
        score[own, keys] = raw
        tops[g] = jnp.maximum(tops[g], fold(raw, jnp.maximum))
        if g == 0 and t == 0:
            loads[1].wait()
        dprob[own, keys] = jnp.dot(back[own, :], mine[:LATENT], preferred_element_type=jnp.float32)
        if t == tiles - 1:
            tops[g] = jnp.max(tops[g], axis=1, keepdims=True)

    def weights(g, t):
        own, keys = span(g, t)
        weight = jnp.exp2(score[own, keys] - tops[g])
        score[own, keys] = weight
        totals[g] = totals[g] + fold(weight, jnp.add)
        if t == tiles - 1:
            totals[g] = 1.0 / jnp.sum(totals[g], axis=1, keepdims=True)

    def values(g, t):
        own, keys = span(g, t)
        probs = (score[own, keys] * totals[g]).astype(jnp.bfloat16)
        part = jnp.dot(back_t[:, own], probs, preferred_element_type=jnp.float32)
        if g == 0:
            acc[:LATENT, keys] = part
        else:
            acc[:LATENT, keys] += part
        deltas[g] = deltas[g] + fold(probs.astype(jnp.float32) * dprob[own, keys], jnp.add)
        if t == tiles - 1:
            deltas[g] = jnp.sum(deltas[g], axis=1, keepdims=True)

    stores = [pltpu.make_async_copy(cache, cache_hbm, block_sems.at[len(blocks_hbm)])]
    stores[0].start()

    def gradients(g, t):
        own, keys = span(g, t)
        dscore = score[own, keys] * (totals[g] * scale) * (dprob[own, keys] - deltas[g])
        dscore = dscore.astype(jnp.bfloat16)
        ds[own, keys] = dscore
        store = pltpu.make_async_copy(ds.at[own, keys], ds_hbm.at[own, keys], ds_sems.at[g, t])
        store.start()
        stores.append(store)
        part = jnp.dot(ext_t[:, own], dscore, preferred_element_type=jnp.float32)
        acc[:LATENT, keys] += part[:LATENT]
        if g == 0:
            acc[LATENT:, keys] = part[LATENT:]
        else:
            acc[LATENT:, keys] += part[LATENT:]

    def put_out(t):
        mine = slice(t * per_tile, (t + 1) * per_tile)
        for s in range(t * per_tile, (t + 1) * per_tile):
            outs[s] = acc[:, s * LANES : (s + 1) * LANES].astype(jnp.bfloat16)
        for i, out in enumerate(outs_hbm):
            which = core if i < slices else 1 - core
            start = pl.multiple_of((2 * ((place + i) % slices) + which) * height, 8)
            store = pltpu.make_async_copy(outs.at[mine, pl.ds(start, height), :], out.at[mine], out_sems.at[i, t])
            store.start()
            stores.append(store)

    stages = (scores, weights, values, gradients)
    for step in range(len(stages) + GROUPS - 1):
        if step == stages.index(values):
            loads[2].wait()
            loads[3].wait()
        for t in range(tiles):
            for g in range(GROUPS):
                if 0 <= step - g < len(stages):
                    stages[step - g](g, t)
            if step == len(stages) + GROUPS - 2:
                put_out(t)
    for store in stores:
        store.wait()


def attend(place, offsets, blocks, ext, back, ext_t, back_t):
    rows = ext.shape[0]
    half, height = blocks[0].shape[:2]
    owners = 2 * half
    keys_total = owners * LANES
    queries = offsets.shape[0] * QBLOCK
    tiles = keys_total // KTILE
    smem = pl.BlockSpec(memory_space=pltpu.SMEM)
    any_place = pl.BlockSpec(memory_space=pl.ANY)
    bf16, f32 = jnp.bfloat16, jnp.float32
    sums = len(blocks) // 2
    *outs, dscore, whole = pl.pallas_call(
        attend_kernel,
        out_shape=[jax.ShapeDtypeStruct((owners, height, LANES), bf16)] * sums
        + [jax.ShapeDtypeStruct((rows, keys_total), bf16), jax.ShapeDtypeStruct((owners, PADDED, LANES), bf16)],
        in_specs=[smem, smem] + [any_place] * (len(blocks) + 4),
        out_specs=[any_place] * (sums + 2),
        scratch_shapes=[
            pltpu.VMEM(ext.shape, bf16),
            pltpu.VMEM(back.shape, bf16),
            pltpu.VMEM(ext_t.shape, bf16),
            pltpu.VMEM(back_t.shape, bf16),
            pltpu.VMEM((owners, PADDED, LANES), bf16),
            pltpu.VMEM((queries, keys_total), f32),
            pltpu.VMEM((rows, keys_total), f32),
            pltpu.VMEM((rows, keys_total), f32),
            pltpu.VMEM((WIDTH, keys_total), f32),
            pltpu.VMEM((rows, keys_total), bf16),
            pltpu.VMEM((owners, WIDTH, LANES), bf16),
            pltpu.SemaphoreType.DMA((len(blocks) + 1,)),
            pltpu.SemaphoreType.DMA((4,)),
            pltpu.SemaphoreType.DMA((GROUPS, tiles)),
            pltpu.SemaphoreType.DMA((sums, tiles)),
        ],
        compiler_params=pltpu.CompilerParams(vmem_limit_bytes=VMEM),
        cost_estimate=pl.CostEstimate(
            flops=2 * rows * keys_total * (2 * PADDED + 2 * LATENT),
            bytes_accessed=14_000_000, transcendentals=rows * keys_total),
        name="attend",
    )(place, offsets, *blocks, ext, back, ext_t, back_t)
    return outs[: sums // 2], outs[sums // 2 :], dscore, whole


def query_kernel(first, ready, place_ref, scale_ref, ds_hbm, cache_hbm, key_hbm, *refs):
    nope_hbm, rope_hbm, ds, up_key, parts, cache, grad_buf, nope, rope_out, sems = refs[2 * ready :]
    queries = nope.shape[0]
    heads = up_key.shape[1] // NOPE
    loads = [
        pltpu.make_async_copy(cache_hbm, parts, sems.at[0]),
        pltpu.make_async_copy(ds_hbm.at[first * queries : (first + heads) * queries], ds, sems.at[1]),
        pltpu.make_async_copy(key_hbm.at[:, first * NOPE : (first + heads) * NOPE], up_key, sems.at[2]),
    ]
    for load in loads:
        load.start()
    factor = jnp.exp2(scale_ref[...].astype(jnp.float32))
    loads[0].wait()
    cache[...] = keys_of(parts, 0, parts.shape[0], PADDED)
    loads[1].wait()
    grad_buf[...] = lax.dot_general(ds[...], cache[...], COLS, preferred_element_type=jnp.float32)
    loads[2].wait()
    for h in range(heads):
        lanes = slice(h * NOPE, (h + 1) * NOPE)
        grad = grad_buf[h * queries : (h + 1) * queries, :]
        part = jnp.dot(grad[:, :LATENT].astype(jnp.bfloat16), up_key[:, lanes], preferred_element_type=jnp.float32)
        nope[:, lanes] = (part * factor).astype(jnp.bfloat16)
        rope = grad[:, LATENT:] * factor
        if h % 2 == 0:
            even = rope
        else:
            pair = slice(h // 2 * LANES, (h // 2 + 1) * LANES)
            rope_out[:, pair] = (even + pltpu.roll(rope, ROPE, 1)).astype(jnp.bfloat16)
    stores = [
        pltpu.make_async_copy(nope, nope_hbm.at[:, first * NOPE : (first + heads) * NOPE], sems.at[3]),
        pltpu.make_async_copy(rope_out, rope_hbm.at[:, first * ROPE : (first + heads) * ROPE], sems.at[4]),
    ]
    for store in stores:
        store.start()
    for store in stores:
        store.wait()


def query_gradients(first, count, place, scales, dscore, whole, up_key, ready=()):
    keys_total = dscore.shape[1]
    heads = up_key.shape[1] // NOPE
    queries = scales.shape[0]
    rows = count * queries
    smem = pl.BlockSpec(memory_space=pltpu.SMEM)
    vmem = pl.BlockSpec(memory_space=pltpu.VMEM)
    any_place = pl.BlockSpec(memory_space=pl.ANY)
    bf16, f32 = jnp.bfloat16, jnp.float32
    return pl.pallas_call(
        functools.partial(query_kernel, first, len(ready) // 2),
        out_shape=(
            jax.ShapeDtypeStruct((queries, heads * NOPE), bf16),
            jax.ShapeDtypeStruct((queries, heads * ROPE), bf16),
        ),
        in_specs=[smem, vmem] + [any_place] * (3 + len(ready)),
        out_specs=(any_place, any_place),
        scratch_shapes=[
            pltpu.VMEM((rows, keys_total), bf16),
            pltpu.VMEM((up_key.shape[0], count * NOPE), bf16),
            pltpu.VMEM(whole.shape, bf16),
            pltpu.VMEM((PADDED, keys_total), bf16),
            pltpu.VMEM((rows, PADDED), f32),
            pltpu.VMEM((queries, count * NOPE), bf16),
            pltpu.VMEM((queries, count * ROPE), bf16),
            pltpu.SemaphoreType.DMA((5,)),
        ],
        input_output_aliases={5 + i: i for i in range(len(ready))},
        compiler_params=pltpu.CompilerParams(vmem_limit_bytes=58 * 2**20),
        cost_estimate=pl.CostEstimate(
            flops=2 * rows * keys_total * PADDED, bytes_accessed=9_000_000, transcendentals=0),
        name=f"query_gradients_{first}",
    )(place, scales, dscore, whole, up_key, *ready)


def per_device(cache, query_nope, query_rope, scale_exp, offsets, up_key, up_value, grad_out):
    place = jnp.stack([lax.axis_index("x"), lax.axis_index("core")]).astype(jnp.int32)
    own = lax.axis_index(("x", "core"))
    height = WIDTH // (lax.axis_size("x") * lax.axis_size("core"))
    mine = lax.dynamic_slice_in_dim(cache.T, own * height, height, 0)
    scales = scale_exp.reshape(-1, 1)
    heads = up_key.shape[1] // NOPE
    projected = project(scales, query_nope, query_rope, up_key, up_value, grad_out)
    over_seq, projected = lax.optimization_barrier((to_each(mine, SEQ), projected))
    here = gather_over_x(over_seq)
    blocks = here + [swap_core(block) for block in here]
    keeps, sends, dscore, whole = attend(place, offsets, blocks, *projected)
    slices = jnp.concatenate(reduce_over_x(*core_sums(keeps, sends)))
    early = query_gradients(0, heads // 2, place, scales, dscore, whole, up_key)
    slices = add_up(lax.all_to_all(slices, SEQ, 0, 0, tiled=True))
    slices, early = lax.optimization_barrier((slices, early))
    query_grads = query_gradients(heads // 2, heads // 2, place, scales, dscore, whole, up_key, early)
    return (owned_columns(slices), *query_grads)


def solution(mesh):
    wide = Mesh(mesh.devices.reshape(8, 2, 4, 2, 2), SEQ + HEAD)
    in_specs = (
        P(SEQ, None),
        P(SEQ, HEAD),
        P(SEQ, HEAD),
        P(SEQ),
        P(SEQ),
        P(None, HEAD),
        P(None, HEAD),
        P(SEQ, HEAD),
    )
    out_specs = (P(SEQ, None), P(SEQ, HEAD), P(SEQ, HEAD))
    return jax.shard_map(per_device, mesh=wide, in_specs=in_specs, out_specs=out_specs, check_vma=False)
```

time: 120 us -> 119 us (level)
  blocking collectives: 50.8 us -> 0 us
  starting transfers between devices: 22.2 us -> 47.9 us
  waiting for transfers between devices: 9.5 us -> 24.7 us
  Pallas kernels: 23.1 us -> 33.5 us
  local copies, waits for them, and re-layouts: 12.2 us -> 8.86 us
    all_to_all x3 -> x0, blocking collectives: 50.8 us -> none  [the longest x1 18.7 us: owned_columns(): slices = add_up(lax.all_to_all(half, 'x', 0, 0, tiled=True))]
    ppermute x0 -> x12, starting transfers between devices: none -> 14.8 us  [the longest x6 12.1 us: to_previous(): return lax.ppermute(block, 'x', [(i, (i - 1) % size) for i in range(size)])]
    ppermute x0 -> x12, waiting for transfers between devices: none -> 11.6 us  [the longest x6 9.62 us: to_next(): return lax.ppermute(block, 'x', [(i, (i + 1) % size) for i in range(size)])]
    pallas_call x2 -> x3, Pallas kernels: 21.7 us -> 28.1 us  [the longest x1 15.5 us: attend(): pl.pallas_call(attend_kernel, out_shape=[jax.ShapeDtypeStruct((owners, he...]
    ppermute x2 -> x12, starting transfers between devices: 4 us -> 9.34 us  [swap_core(): return lax.ppermute(block, 'core', [(0, 1), (1, 0)])]
    pallas_call x1, Pallas kernels: 1.36 us -> 5.37 us  [project(): pl.pallas_call(project_kernel, out_shape=(jax.ShapeDtypeStruct((rows, PAD...]
    unnamed x30 -> x14, local copies, waits for them, and re-layouts: 9.79 us -> 5.93 us
    all_to_all x0 -> x1, waiting for transfers between devices: none -> 3.76 us  [per_device(): slices = add_up(lax.all_to_all(slices, SEQ, 0, 0, tiled=True))]
  transfers between devices with their start and end apart: 4 -> 27, of which waited for: 4 -> 12; matrix products, arithmetic and copies ran while one was open for 1% -> 1% of each run, Pallas kernels for 5% -> 15%
where the time goes in v4:
time: 119 us; the launch traced here: 118 us
  starting transfers between devices  47.9 us (40%)
  Pallas kernels  33.5 us (28%)
  waiting for transfers between devices  24.7 us (21%)
  local copies, waits for them, and re-layouts  8.86 us (7%)
  other arithmetic  2.01 us (2%)
    all_to_all x2, starting transfers between devices, to_each(): return lax.all_to_all(copies, axes, 0, 0, tiled=True)  20.2 us
    pallas_call x1, Pallas kernels, attend(): pl.pallas_call(attend_kernel, out_shape=[jax.ShapeDtypeStruct((owners, he...  15.5 us
    pallas_call x2, Pallas kernels, query_gradients(): pl.pallas_call(functools.partial(query_kernel, first, len(ready) // 2), o...  12.6 us
    ppermute x6, starting transfers between devices, to_previous(): return lax.ppermute(block, 'x', [(i, (i - 1) % size) for i in range(size)])  12.1 us
    ppermute x6, waiting for transfers between devices, to_next(): return lax.ppermute(block, 'x', [(i, (i + 1) % size) for i in range(size)])  9.62 us
    ppermute x12, starting transfers between devices, swap_core(): return lax.ppermute(block, 'core', [(0, 1), (1, 0)])  9.34 us
    all_to_all x2, waiting for transfers between devices, to_each(): return lax.all_to_all(copies, axes, 0, 0, tiled=True)  7.38 us
    unnamed x14, local copies, waits for them, and re-layouts  5.93 us
  transfers between devices with their start and end apart: 27, of which 12 were waited for; matrix products, arithmetic and copies ran while one was open for 1% of the time, Pallas kernels for 15%

profile of v4, /device:TPU:1, one launch (start us, length us, event | category | flops | bytes accessed | tf_op | source)
XLA Modules:
  0.0 117.8 jit_solution(16421738961417984174)
XLA Ops:
  0.7 0.9 copy-done
  1.5 0.8 broadcast_in_dim.6
  2.3 10.1 %all-to-all-start = ((bf16[16,72,128]{2,1,0:T(8,128)(2,1)}), bf16[16,72,128]{2,1,0:T(8,128)(2,1)S(1)}, u32[]{:S(2)}, u32[]{:S(2)}) async-start(bf16[16,72,128]{2,1,0:T(8,128)(2,1)} %broadcast_in_dim.6), calls=%async_computation | async-start | bytes 589824 | tf_op jit(solution)/shard_map/all_to_all | solution.py:29
  12.5 1.4 %copy.16.scale_ref = s32[128,1]{1,0:T(8,128)} copy(s32[128,1]{0,1:T(1,128)} %bitcast.11) | data formatting | bytes 1024 | tf_op jit(solution)/shard_map/reshape | solution.py:422
  13.8 5.4 %project.1 = (bf16[1024,640]{1,0:T(8,128)(2,1)}, bf16[1024,512]{1,0:T(8,128)(2,1)}, bf16[576,1024]{1,0:T(8,128)(2,1)}, bf16[512,1024]{1,0:T(8,128)(2,1)}) custom-call(s32[128,1]{1,0:T(8,128)} %copy.16.scale_ref, bf16[128,1024]{1,0:T(8,128)(2,1)} %nope_hbm.1, bf16[128,512]{1,0:T(8,128)(2,1)} %rope_hbm.1, bf16[512,1024]{1,0:T(8,128)(2,1)} %key_hbm.5, ...), custom_call_target="tpu_custom_call" | custom-call | flops 536870912 | bytes 7500000 | tf_op jit(solution)/shard_map/project/pallas_call | solution.py:140
  19.2 4.5 %all-to-all-done = bf16[16,72,128]{2,1,0:T(8,128)(2,1)S(1)} async-done(((bf16[16,72,128]{2,1,0:T(8,128)(2,1)}), bf16[16,72,128]{2,1,0:T(8,128)(2,1)S(1)}, u32[]{:S(2)}, u32[]{:S(2)}) %all-to-all-start) | async-done | bytes 294944 | tf_op jit(solution)/shard_map/all_to_all | solution.py:29
  23.8 2.4 %collective-permute-start.7 = (bf16[8,72,128]{2,1,0:T(8,128)(2,1)S(1)}, bf16[8,72,128]{2,1,0:T(8,128)(2,1)S(1)}, u32[]{:S(2)}, u32[]{:S(2)}) collective-permute-start(bf16[8,72,128]{2,1,0:T(8,128)(2,1)S(1)} %get-tuple-element.63.refs_1_), channel_id=1, source_target_pairs={{0,1},{1,0},{2,3},{3,2},{4,5},{5,4},{6,7},{7,6},{8,9},{9,8},{10,11... | collective-permute-start | bytes 442376 | tf_op jit(solution)/shard_map/ppermute | solution.py:33
  26.2 1.2 %collective-permute-start.3 = (bf16[8,72,128]{2,1,0:T(8,128)(2,1)S(1)}, bf16[8,72,128]{2,1,0:T(8,128)(2,1)S(1)}, u32[]{:S(2)}, u32[]{:S(2)}) collective-permute-start(bf16[8,72,128]{2,1,0:T(8,128)(2,1)S(1)} %get-tuple-element.63.refs_1_), channel_id=1, source_target_pairs={{0,4},{4,8},{8,12},{12,0},{1,5},{5,9},{9,13},{13,1},{2,6},{6,10},{... | collective-permute-start | bytes 442376 | tf_op jit(solution)/shard_map/ppermute | solution.py:42
  27.4 1.5 %collective-permute-start.1 = (bf16[8,72,128]{2,1,0:T(8,128)(2,1)S(1)}, bf16[8,72,128]{2,1,0:T(8,128)(2,1)S(1)}, u32[]{:S(2)}, u32[]{:S(2)}) collective-permute-start(bf16[8,72,128]{2,1,0:T(8,128)(2,1)S(1)} %get-tuple-element.63.refs_1_), channel_id=1, source_target_pairs={{0,12},{4,0},{8,4},{12,8},{1,13},{5,1},{9,5},{13,9},{2,14},{6,2},{... | collective-permute-start | bytes 442376 | tf_op jit(solution)/shard_map/ppermute | solution.py:47
  28.9 1.3 %collective-permute-start = (bf16[8,72,128]{2,1,0:T(8,128)(2,1)S(1)}, bf16[8,72,128]{2,1,0:T(8,128)(2,1)S(1)}, u32[]{:S(2)}, u32[]{:S(2)}) collective-permute-start(bf16[8,72,128]{2,1,0:T(8,128)(2,1)S(1)} %get-tuple-element.64.refs_0_), channel_id=1, source_target_pairs={{0,12},{4,0},{8,4},{12,8},{1,13},{5,1},{9,5},{13,9},{2,14},{6,2},{... | collective-permute-start | bytes 442376 | tf_op jit(solution)/shard_map/ppermute | solution.py:47
  30.1 0.9 collective-permute-start.6
  31.0 0.2 collective-permute-start.5
  31.2 1.5 %collective-permute-done.3.refs_7_ = bf16[8,72,128]{2,1,0:T(8,128)(2,1)S(1)} collective-permute-done((bf16[8,72,128]{2,1,0:T(8,128)(2,1)S(1)}, bf16[8,72,128]{2,1,0:T(8,128)(2,1)S(1)}, u32[]{:S(2)}, u32[]{:S(2)}) %collective-permute-start.3) | collective-permute-done | bytes 147488 | tf_op jit(solution)/shard_map/ppermute | solution.py:42
  32.8 0.9 collective-permute-start.13
  33.7 1.9 %collective-permute-done.refs_2_ = bf16[8,72,128]{2,1,0:T(8,128)(2,1)S(1)} collective-permute-done((bf16[8,72,128]{2,1,0:T(8,128)(2,1)S(1)}, bf16[8,72,128]{2,1,0:T(8,128)(2,1)S(1)}, u32[]{:S(2)}, u32[]{:S(2)}) %collective-permute-start) | collective-permute-done | bytes 147488 | tf_op jit(solution)/shard_map/ppermute | solution.py:47
  35.6 2.7 %collective-permute-start.2 = (bf16[8,72,128]{2,1,0:T(8,128)(2,1)S(1)}, bf16[8,72,128]{2,1,0:T(8,128)(2,1)S(1)}, u32[]{:S(2)}, u32[]{:S(2)}) collective-permute-start(bf16[8,72,128]{2,1,0:T(8,128)(2,1)S(1)} %collective-permute-done.refs_2_), channel_id=1, source_target_pairs={{0,12},{4,0},{8,4},{12,8},{1,13},{5,1},{9,5},{13,9},{2,14},{6,2},{... | collective-permute-start | bytes 442376 | tf_op jit(solution)/shard_map/ppermute | solution.py:47
  38.3 1.5 %collective-permute-start.8 = (bf16[8,72,128]{2,1,0:T(8,128)(2,1)S(1)}, bf16[8,72,128]{2,1,0:T(8,128)(2,1)S(1)}, u32[]{:S(2)}, u32[]{:S(2)}) collective-permute-start(bf16[8,72,128]{2,1,0:T(8,128)(2,1)S(1)} %collective-permute-done.refs_2_), channel_id=1, source_target_pairs={{0,1},{1,0},{2,3},{3,2},{4,5},{5,4},{6,7},{7,6},{8,9},{9,8},{10,11... | collective-permute-start | bytes 442376 | tf_op jit(solution)/shard_map/ppermute | solution.py:33
  39.9 0.4 collective-permute-start.12
  40.3 0.2 collective-permute-done.4.refs_5_
  40.5 1.2 collective-permute-start.11
  41.7 0.8 collective-permute-start.10
  42.7 0.8 collective-permute-done.10.refs_12_
  43.5 1.3 %copy-done.2 = bf16[1024,640]{1,0:T(8,128)(2,1)S(1)} copy-done((bf16[1024,640]{1,0:T(8,128)(2,1)S(1)}, bf16[1024,640]{1,0:T(8,128)(2,1)}, u32[]{:S(2)}) %copy-start.2) | copy-done | bytes 1310744
  44.8 1.3 %copy-done.3 = bf16[576,1024]{1,0:T(8,128)(2,1)S(1)} copy-done((bf16[576,1024]{1,0:T(8,128)(2,1)S(1)}, bf16[576,1024]{1,0:T(8,128)(2,1)}, u32[]{:S(2)}) %copy-start.3) | copy-done | bytes 1179672
  46.0 1.2 %copy-done.4 = bf16[1024,512]{1,0:T(8,128)(2,1)S(1)} copy-done((bf16[1024,512]{1,0:T(8,128)(2,1)S(1)}, bf16[1024,512]{1,0:T(8,128)(2,1)}, u32[]{:S(2)}) %copy-start.4) | copy-done | bytes 1048600
  47.3 1.2 %copy-done.5 = bf16[512,1024]{1,0:T(8,128)(2,1)S(1)} copy-done((bf16[512,1024]{1,0:T(8,128)(2,1)S(1)}, bf16[512,1024]{1,0:T(8,128)(2,1)}, u32[]{:S(2)}) %copy-start.5) | copy-done | bytes 1048600
  48.5 15.5 %attend.1 = (bf16[16,72,128]{2,1,0:T(8,128)(2,1)S(1)}, bf16[16,72,128]{2,1,0:T(8,128)(2,1)S(1)}, bf16[16,72,128]{2,1,0:T(8,128)(2,1)S(1)}, bf16[16,72,128]{2,1,0...) custom-call(s32[2]{0:T(128)S(1)} %pad_add_fusion.place_ref, ...), custom_call_target="tpu_custom_call" | custom-call | flops 9663676416 | bytes 14000000 | tf_op jit(solution)/shard_map/attend/pallas_call | solution.py:312
  64.0 0.5 collective-permute-start.16
  64.5 0.1 collective-permute-start.15
  64.6 1.1 collective-permute-done.16
  65.8 1.0 collective-permute-start.17
  66.8 0.6 collective-permute-start.19
  67.4 2.6 %collective-permute-start.22 = (bf16[8,72,128]{2,1,0:T(8,128)(2,1)S(1)}, bf16[8,72,128]{2,1,0:T(8,128)(2,1)S(1)}, u32[]{:S(2)}, u32[]{:S(2)}) collective-permute-start(bf16[8,72,128]{2,1,0:T(8,128)(2,1)S(1)} %get-tuple-element.60), channel_id=1, source_target_pairs={{0,12},{4,0},{8,4},{12,8},{1,13},{5,1},{9,5},{13,9},{2,14},{6,2},{... | collective-permute-start | bytes 442376 | tf_op jit(solution)/shard_map/ppermute | solution.py:47
  70.1 3.3 %collective-permute-done.17 = bf16[8,72,128]{2,1,0:T(8,128)(2,1)S(1)} collective-permute-done((bf16[8,72,128]{2,1,0:T(8,128)(2,1)S(1)}, bf16[8,72,128]{2,1,0:T(8,128)(2,1)S(1)}, u32[]{:S(2)}, u32[]{:S(2)}) %collective-permute-start.17) | collective-permute-done | bytes 147488 | tf_op jit(solution)/shard_map/ppermute | solution.py:42
  73.8 2.7 %collective-permute-start.20 = (bf16[8,72,128]{2,1,0:T(8,128)(2,1)S(1)}, bf16[8,72,128]{2,1,0:T(8,128)(2,1)S(1)}, u32[]{:S(2)}, u32[]{:S(2)}) collective-permute-start(bf16[8,72,128]{2,1,0:T(8,128)(2,1)S(1)} %get-tuple-element.61), channel_id=1, source_target_pairs={{0,12},{4,0},{8,4},{12,8},{1,13},{5,1},{9,5},{13,9},{2,14},{6,2},{... | collective-permute-start | bytes 442376 | tf_op jit(solution)/shard_map/ppermute | solution.py:47
  76.6 1.4 %collective-permute-start.23 = (bf16[8,72,128]{2,1,0:T(8,128)(2,1)S(1)}, bf16[8,72,128]{2,1,0:T(8,128)(2,1)S(1)}, u32[]{:S(2)}, u32[]{:S(2)}) collective-permute-start(bf16[8,72,128]{2,1,0:T(8,128)(2,1)S(1)} %get-tuple-element.62), channel_id=1, source_target_pairs={{0,12},{4,0},{8,4},{12,8},{1,13},{5,1},{9,5},{13,9},{2,14},{6,2},{... | collective-permute-start | bytes 442376 | tf_op jit(solution)/shard_map/ppermute | solution.py:47
  77.9 1.4 %collective-permute-done.18 = bf16[8,72,128]{2,1,0:T(8,128)(2,1)S(1)} collective-permute-done((bf16[8,72,128]{2,1,0:T(8,128)(2,1)S(1)}, bf16[8,72,128]{2,1,0:T(8,128)(2,1)S(1)}, u32[]{:S(2)}, u32[]{:S(2)}) %collective-permute-start.18) | collective-permute-done | bytes 147488 | tf_op jit(solution)/shard_map/ppermute | solution.py:42
  79.3 3.2 %collective-permute-done.21 = bf16[8,72,128]{2,1,0:T(8,128)(2,1)S(1)} collective-permute-done((bf16[8,72,128]{2,1,0:T(8,128)(2,1)S(1)}, bf16[8,72,128]{2,1,0:T(8,128)(2,1)S(1)}, u32[]{:S(2)}, u32[]{:S(2)}) %collective-permute-start.21) | collective-permute-done | bytes 147488 | tf_op jit(solution)/shard_map/ppermute | solution.py:42
  82.5 0.2 add_convert_fusion.4
  82.6 0.7 pad_maximum_fusion
  83.4 3.5 %all-to-all-start.1 = ((bf16[16,72,128]{2,1,0:T(8,128)(2,1)}), bf16[16,72,128]{2,1,0:T(8,128)(2,1)S(1)}, u32[]{:S(2)}, u32[]{:S(2)}) async-start(bf16[16,72,128]{2,1,0:T(8,128)(2,1)} %pad_maximum_fusion), calls=%async_computation.1 | async-start | bytes 589824 | tf_op jit(solution)/shard_map/all_to_all | solution.py:431
  86.9 6.3 %query_gradients_0.1 = (bf16[128,1024]{1,0:T(8,128)(2,1)}, bf16[128,512]{1,0:T(8,128)(2,1)}) custom-call(s32[2]{0:T(128)} %copy-done.1, s32[128,1]{1,0:T(8,128)} %copy.16.scale_ref, bf16[1024,2048]{1,0:T(8,128)(2,1)} %get-tuple-element.46.ds_hbm, bf16[16,640,128]{2,1,0:T(8,128)(2,1)} %get-tuple-element.47.cache_hbm, bf16[512,1024]{1,0:T(8,128)(2,1)} %key_hbm.5), custom_call_target="tpu_custom_call" | custom-call | flops 1342177280 | bytes 9000000 | tf_op jit(solution)/shard_map/query_gradients_0/pallas_call | solution.py:391
  93.2 3.8 %all-to-all-done.1 = bf16[16,72,128]{2,1,0:T(8,128)(2,1)S(1)} async-done(((bf16[16,72,128]{2,1,0:T(8,128)(2,1)}), bf16[16,72,128]{2,1,0:T(8,128)(2,1)S(1)}, u32[]{:S(2)}, u32[]{:S(2)}) %all-to-all-start.1) | async-done | bytes 294944 | tf_op jit(solution)/shard_map/all_to_all | solution.py:431
  97.0 0.7 broadcast_in_dim.7
  97.8 10.1 %all-to-all-start.2 = ((bf16[16,72,128]{2,1,0:T(8,128)(2,1)}), bf16[16,72,128]{2,1,0:T(8,128)(2,1)S(1)}, u32[]{:S(2)}, u32[]{:S(2)}) async-start(bf16[16,72,128]{2,1,0:T(8,128)(2,1)} %broadcast_in_dim.7), calls=%async_computation.2 | async-start | bytes 589824 | tf_op jit(solution)/shard_map/all_to_all | solution.py:29
  107.9 6.3 %query_gradients_4.1 = (bf16[128,1024]{1,0:T(8,128)(2,1)}, bf16[128,512]{1,0:T(8,128)(2,1)}) custom-call(s32[2]{0:T(128)} %copy-done.1, s32[128,1]{1,0:T(8,128)} %copy.16.scale_ref, bf16[1024,2048]{1,0:T(8,128)(2,1)} %get-tuple-element.46.ds_hbm, bf16[16,640,128]{2,1,0:T(8,128)(2,1)} %get-tuple-element.47.cache_hbm, ...), custom_call_target="tpu_custom_call", output_to_operand_aliasing={{0}: (5, {}), {1}: (6, {})} | custom-call | flops 1342177280 | bytes 9000000 | tf_op jit(solution)/shard_map/query_gradients_4/pallas_call | solution.py:391
  114.2 2.9 %all-to-all-done.2 = bf16[16,72,128]{2,1,0:T(8,128)(2,1)S(1)} async-done(((bf16[16,72,128]{2,1,0:T(8,128)(2,1)}), bf16[16,72,128]{2,1,0:T(8,128)(2,1)S(1)}, u32[]{:S(2)}, u32[]{:S(2)}) %all-to-all-start.2) | async-done | bytes 294944 | tf_op jit(solution)/shard_map/all_to_all | solution.py:29
  117.1 0.7 reduce_sum.25
  (37 shorter events, 0.9 us)
Async XLA Ops:
  0.6 0.9 copy-start
  0.6 42.8 %copy-start.6 = (s32[2]{0:T(128)S(1)}, s32[2]{0:T(128)}, u32[]{:S(2)}) copy-start(s32[2]{0:T(128)} %offsets_ref.1) | copy-start | bytes 28
  2.3 21.4 %all-to-all-start = ((bf16[16,72,128]{2,1,0:T(8,128)(2,1)}), bf16[16,72,128]{2,1,0:T(8,128)(2,1)S(1)}, u32[]{:S(2)}, u32[]{:S(2)}) async-start(bf16[16,72,128]{2,1,0:T(8,128)(2,1)} %broadcast_in_dim.6), calls=%async_computation | async-start | bytes 589824 | tf_op jit(solution)/shard_map/all_to_all | solution.py:29
  23.8 7.3 %collective-permute-start.7 = (bf16[8,72,128]{2,1,0:T(8,128)(2,1)S(1)}, bf16[8,72,128]{2,1,0:T(8,128)(2,1)S(1)}, u32[]{:S(2)}, u32[]{:S(2)}) collective-permute-start(bf16[8,72,128]{2,1,0:T(8,128)(2,1)S(1)} %get-tuple-element.63.refs_1_), channel_id=1, source_target_pairs={{0,1},{1,0},{2,3},{3,2},{4,5},{5,4},{6,7},{7,6},{8,9},{9,8},{10,11... | collective-permute-start | bytes 442376 | tf_op jit(solution)/shard_map/ppermute | solution.py:33
  26.2 6.6 %collective-permute-start.3 = (bf16[8,72,128]{2,1,0:T(8,128)(2,1)S(1)}, bf16[8,72,128]{2,1,0:T(8,128)(2,1)S(1)}, u32[]{:S(2)}, u32[]{:S(2)}) collective-permute-start(bf16[8,72,128]{2,1,0:T(8,128)(2,1)S(1)} %get-tuple-element.63.refs_1_), channel_id=1, source_target_pairs={{0,4},{4,8},{8,12},{12,0},{1,5},{5,9},{9,13},{13,1},{2,6},{6,10},{... | collective-permute-start | bytes 442376 | tf_op jit(solution)/shard_map/ppermute | solution.py:42
  27.4 6.3 %collective-permute-start.1 = (bf16[8,72,128]{2,1,0:T(8,128)(2,1)S(1)}, bf16[8,72,128]{2,1,0:T(8,128)(2,1)S(1)}, u32[]{:S(2)}, u32[]{:S(2)}) collective-permute-start(bf16[8,72,128]{2,1,0:T(8,128)(2,1)S(1)} %get-tuple-element.63.refs_1_), channel_id=1, source_target_pairs={{0,12},{4,0},{8,4},{12,8},{1,13},{5,1},{9,5},{13,9},{2,14},{6,2},{... | collective-permute-start | bytes 442376 | tf_op jit(solution)/shard_map/ppermute | solution.py:47
  28.9 6.8 %collective-permute-start = (bf16[8,72,128]{2,1,0:T(8,128)(2,1)S(1)}, bf16[8,72,128]{2,1,0:T(8,128)(2,1)S(1)}, u32[]{:S(2)}, u32[]{:S(2)}) collective-permute-start(bf16[8,72,128]{2,1,0:T(8,128)(2,1)S(1)} %get-tuple-element.64.refs_0_), channel_id=1, source_target_pairs={{0,12},{4,0},{8,4},{12,8},{1,13},{5,1},{9,5},{13,9},{2,14},{6,2},{... | collective-permute-start | bytes 442376 | tf_op jit(solution)/shard_map/ppermute | solution.py:47
  30.1 8.2 %collective-permute-start.6 = (bf16[8,72,128]{2,1,0:T(8,128)(2,1)S(1)}, bf16[8,72,128]{2,1,0:T(8,128)(2,1)S(1)}, u32[]{:S(2)}, u32[]{:S(2)}) collective-permute-start(bf16[8,72,128]{2,1,0:T(8,128)(2,1)S(1)} %get-tuple-element.64.refs_0_), channel_id=1, source_target_pairs={{0,1},{1,0},{2,3},{3,2},{4,5},{5,4},{6,7},{7,6},{8,9},{9,8},{10,11... | collective-permute-start | bytes 442376 | tf_op jit(solution)/shard_map/ppermute | solution.py:33
  31.0 8.7 %collective-permute-start.5 = (bf16[8,72,128]{2,1,0:T(8,128)(2,1)S(1)}, bf16[8,72,128]{2,1,0:T(8,128)(2,1)S(1)}, u32[]{:S(2)}, u32[]{:S(2)}) collective-permute-start(bf16[8,72,128]{2,1,0:T(8,128)(2,1)S(1)} %get-tuple-element.64.refs_0_), channel_id=1, source_target_pairs={{0,4},{4,8},{8,12},{12,0},{1,5},{5,9},{9,13},{13,1},{2,6},{6,10},{... | collective-permute-start | bytes 442376 | tf_op jit(solution)/shard_map/ppermute | solution.py:42
  32.8 7.1 %collective-permute-start.13 = (bf16[8,72,128]{2,1,0:T(8,128)(2,1)S(1)}, bf16[8,72,128]{2,1,0:T(8,128)(2,1)S(1)}, u32[]{:S(2)}, u32[]{:S(2)}) collective-permute-start(bf16[8,72,128]{2,1,0:T(8,128)(2,1)S(1)} %collective-permute-done.3.refs_7_), channel_id=1, source_target_pairs={{0,1},{1,0},{2,3},{3,2},{4,5},{5,4},{6,7},{7,6},{8,9},{9,8},{10,11... | collective-permute-start | bytes 442376 | tf_op jit(solution)/shard_map/ppermute | solution.py:33
  33.7 6.9 %collective-permute-start.4 = (bf16[8,72,128]{2,1,0:T(8,128)(2,1)S(1)}, bf16[8,72,128]{2,1,0:T(8,128)(2,1)S(1)}, u32[]{:S(2)}, u32[]{:S(2)}) collective-permute-start(bf16[8,72,128]{2,1,0:T(8,128)(2,1)S(1)} %collective-permute-done.3.refs_7_), channel_id=1, source_target_pairs={{0,4},{4,8},{8,12},{12,0},{1,5},{5,9},{9,13},{13,1},{2,6},{6,10},{... | collective-permute-start | bytes 442376 | tf_op jit(solution)/shard_map/ppermute | solution.py:42
  35.6 6.1 %collective-permute-start.2 = (bf16[8,72,128]{2,1,0:T(8,128)(2,1)S(1)}, bf16[8,72,128]{2,1,0:T(8,128)(2,1)S(1)}, u32[]{:S(2)}, u32[]{:S(2)}) collective-permute-start(bf16[8,72,128]{2,1,0:T(8,128)(2,1)S(1)} %collective-permute-done.refs_2_), channel_id=1, source_target_pairs={{0,12},{4,0},{8,4},{12,8},{1,13},{5,1},{9,5},{13,9},{2,14},{6,2},{... | collective-permute-start | bytes 442376 | tf_op jit(solution)/shard_map/ppermute | solution.py:47
  38.3 4.2 %collective-permute-start.8 = (bf16[8,72,128]{2,1,0:T(8,128)(2,1)S(1)}, bf16[8,72,128]{2,1,0:T(8,128)(2,1)S(1)}, u32[]{:S(2)}, u32[]{:S(2)}) collective-permute-start(bf16[8,72,128]{2,1,0:T(8,128)(2,1)S(1)} %collective-permute-done.refs_2_), channel_id=1, source_target_pairs={{0,1},{1,0},{2,3},{3,2},{4,5},{5,4},{6,7},{7,6},{8,9},{9,8},{10,11... | collective-permute-start | bytes 442376 | tf_op jit(solution)/shard_map/ppermute | solution.py:33
  39.8 2.8 %collective-permute-start.9 = (bf16[8,72,128]{2,1,0:T(8,128)(2,1)S(1)}, bf16[8,72,128]{2,1,0:T(8,128)(2,1)S(1)}, u32[]{:S(2)}, u32[]{:S(2)}) collective-permute-start(bf16[8,72,128]{2,1,0:T(8,128)(2,1)S(1)} %collective-permute-done.1.refs_3_), channel_id=1, source_target_pairs={{0,1},{1,0},{2,3},{3,2},{4,5},{5,4},{6,7},{7,6},{8,9},{9,8},{10,11... | collective-permute-start | bytes 442376 | tf_op jit(solution)/shard_map/ppermute | solution.py:33
  39.9 2.7 %collective-permute-start.12 = (bf16[8,72,128]{2,1,0:T(8,128)(2,1)S(1)}, bf16[8,72,128]{2,1,0:T(8,128)(2,1)S(1)}, u32[]{:S(2)}, u32[]{:S(2)}) collective-permute-start(bf16[8,72,128]{2,1,0:T(8,128)(2,1)S(1)} %collective-permute-done.5.refs_6_), channel_id=1, source_target_pairs={{0,1},{1,0},{2,3},{3,2},{4,5},{5,4},{6,7},{7,6},{8,9},{9,8},{10,11... | collective-permute-start | bytes 442376 | tf_op jit(solution)/shard_map/ppermute | solution.py:33
  40.5 2.2 %collective-permute-start.11 = (bf16[8,72,128]{2,1,0:T(8,128)(2,1)S(1)}, bf16[8,72,128]{2,1,0:T(8,128)(2,1)S(1)}, u32[]{:S(2)}, u32[]{:S(2)}) collective-permute-start(bf16[8,72,128]{2,1,0:T(8,128)(2,1)S(1)} %collective-permute-done.4.refs_5_), channel_id=1, source_target_pairs={{0,1},{1,0},{2,3},{3,2},{4,5},{5,4},{6,7},{7,6},{8,9},{9,8},{10,11... | collective-permute-start | bytes 442376 | tf_op jit(solution)/shard_map/ppermute | solution.py:33
  41.7 1.8 %collective-permute-start.10 = (bf16[8,72,128]{2,1,0:T(8,128)(2,1)S(1)}, bf16[8,72,128]{2,1,0:T(8,128)(2,1)S(1)}, u32[]{:S(2)}, u32[]{:S(2)}) collective-permute-start(bf16[8,72,128]{2,1,0:T(8,128)(2,1)S(1)} %collective-permute-done.2.refs_4_), channel_id=1, source_target_pairs={{0,1},{1,0},{2,3},{3,2},{4,5},{5,4},{6,7},{7,6},{8,9},{9,8},{10,11... | collective-permute-start | bytes 442376 | tf_op jit(solution)/shard_map/ppermute | solution.py:33
  42.5 21.5 %copy-start.1 = (s32[2]{0:T(128)}, s32[2]{0:T(128)S(1)}, u32[]{:S(2)}) copy-start(s32[2]{0:T(128)S(1)} %pad_add_fusion.place_ref) | copy-start | bytes 28
  43.5 1.3 %copy-start.2 = (bf16[1024,640]{1,0:T(8,128)(2,1)S(1)}, bf16[1024,640]{1,0:T(8,128)(2,1)}, u32[]{:S(2)}) copy-start(bf16[1024,640]{1,0:T(8,128)(2,1)} %get-tuple-element.34.refs_16_) | copy-start | bytes 3932164
  44.8 1.3 %copy-start.3 = (bf16[576,1024]{1,0:T(8,128)(2,1)S(1)}, bf16[576,1024]{1,0:T(8,128)(2,1)}, u32[]{:S(2)}) copy-start(bf16[576,1024]{1,0:T(8,128)(2,1)} %get-tuple-element.36.refs_18_) | copy-start | bytes 3538948
  46.0 1.2 %copy-start.4 = (bf16[1024,512]{1,0:T(8,128)(2,1)S(1)}, bf16[1024,512]{1,0:T(8,128)(2,1)}, u32[]{:S(2)}) copy-start(bf16[1024,512]{1,0:T(8,128)(2,1)} %get-tuple-element.35.refs_17_) | copy-start | bytes 3145732
  47.3 1.2 %copy-start.5 = (bf16[512,1024]{1,0:T(8,128)(2,1)S(1)}, bf16[512,1024]{1,0:T(8,128)(2,1)}, u32[]{:S(2)}) copy-start(bf16[512,1024]{1,0:T(8,128)(2,1)} %get-tuple-element.37.refs_19_) | copy-start | bytes 3145732
  64.0 1.7 %collective-permute-start.16 = (bf16[16,72,128]{2,1,0:T(8,128)(2,1)S(1)}, bf16[16,72,128]{2,1,0:T(8,128)(2,1)S(1)}, u32[]{:S(2)}, u32[]{:S(2)}) collective-permute-start(bf16[16,72,128]{2,1,0:T(8,128)(2,1)S(1)} %get-tuple-element.43), channel_id=1, source_target_pairs={{0,1},{1,0},{2,3},{3,2},{4,5},{5,4},{6,7},{7,6},{8,9},{9,8},{10,11... | collective-permute-start | bytes 884744 | tf_op jit(solution)/shard_map/ppermute | solution.py:33
  64.5 5.6 %collective-permute-start.15 = (bf16[16,72,128]{2,1,0:T(8,128)(2,1)S(1)}, bf16[16,72,128]{2,1,0:T(8,128)(2,1)S(1)}, u32[]{:S(2)}, u32[]{:S(2)}) collective-permute-start(bf16[16,72,128]{2,1,0:T(8,128)(2,1)S(1)} %get-tuple-element.41), channel_id=1, source_target_pairs={{0,1},{1,0},{2,3},{3,2},{4,5},{5,4},{6,7},{7,6},{8,9},{9,8},{10,11... | collective-permute-start | bytes 884744 | tf_op jit(solution)/shard_map/ppermute | solution.py:33
  65.8 7.6 %collective-permute-start.17 = (bf16[8,72,128]{2,1,0:T(8,128)(2,1)S(1)}, bf16[8,72,128]{2,1,0:T(8,128)(2,1)S(1)}, u32[]{:S(2)}, u32[]{:S(2)}) collective-permute-start(bf16[8,72,128]{2,1,0:T(8,128)(2,1)S(1)} %get-tuple-element.59), channel_id=1, source_target_pairs={{0,4},{4,8},{8,12},{12,0},{1,5},{5,9},{9,13},{13,1},{2,6},{6,10},{... | collective-permute-start | bytes 442376 | tf_op jit(solution)/shard_map/ppermute | solution.py:42
  66.8 6.9 %collective-permute-start.19 = (bf16[16,72,128]{2,1,0:T(8,128)(2,1)S(1)}, bf16[16,72,128]{2,1,0:T(8,128)(2,1)S(1)}, u32[]{:S(2)}, u32[]{:S(2)}) collective-permute-start(bf16[16,72,128]{2,1,0:T(8,128)(2,1)S(1)} %get-tuple-element.45), channel_id=1, source_target_pairs={{0,1},{1,0},{2,3},{3,2},{4,5},{5,4},{6,7},{7,6},{8,9},{9,8},{10,11... | collective-permute-start | bytes 884744 | tf_op jit(solution)/shard_map/ppermute | solution.py:33
  67.4 10.5 %collective-permute-start.14 = (bf16[16,72,128]{2,1,0:T(8,128)(2,1)S(1)}, bf16[16,72,128]{2,1,0:T(8,128)(2,1)S(1)}, u32[]{:S(2)}, u32[]{:S(2)}) collective-permute-start(bf16[16,72,128]{2,1,0:T(8,128)(2,1)S(1)} %get-tuple-element.39), channel_id=1, source_target_pairs={{0,1},{1,0},{2,3},{3,2},{4,5},{5,4},{6,7},{7,6},{8,9},{9,8},{10,11... | collective-permute-start | bytes 884744 | tf_op jit(solution)/shard_map/ppermute | solution.py:33
  67.4 6.3 %collective-permute-start.22 = (bf16[8,72,128]{2,1,0:T(8,128)(2,1)S(1)}, bf16[8,72,128]{2,1,0:T(8,128)(2,1)S(1)}, u32[]{:S(2)}, u32[]{:S(2)}) collective-permute-start(bf16[8,72,128]{2,1,0:T(8,128)(2,1)S(1)} %get-tuple-element.60), channel_id=1, source_target_pairs={{0,12},{4,0},{8,4},{12,8},{1,13},{5,1},{9,5},{13,9},{2,14},{6,2},{... | collective-permute-start | bytes 442376 | tf_op jit(solution)/shard_map/ppermute | solution.py:47
  73.5 5.8 %collective-permute-start.18 = (bf16[8,72,128]{2,1,0:T(8,128)(2,1)S(1)}, bf16[8,72,128]{2,1,0:T(8,128)(2,1)S(1)}, u32[]{:S(2)}, u32[]{:S(2)}) collective-permute-start(bf16[8,72,128]{2,1,0:T(8,128)(2,1)S(1)} %get-tuple-element.57), channel_id=1, source_target_pairs={{0,4},{4,8},{8,12},{12,0},{1,5},{5,9},{9,13},{13,1},{2,6},{6,10},{... | collective-permute-start | bytes 442376 | tf_op jit(solution)/shard_map/ppermute | solution.py:42
  73.6 8.8 %collective-permute-start.21 = (bf16[8,72,128]{2,1,0:T(8,128)(2,1)S(1)}, bf16[8,72,128]{2,1,0:T(8,128)(2,1)S(1)}, u32[]{:S(2)}, u32[]{:S(2)}) collective-permute-start(bf16[8,72,128]{2,1,0:T(8,128)(2,1)S(1)} %get-tuple-element.58), channel_id=1, source_target_pairs={{0,4},{4,8},{8,12},{12,0},{1,5},{5,9},{9,13},{13,1},{2,6},{6,10},{... | collective-permute-start | bytes 442376 | tf_op jit(solution)/shard_map/ppermute | solution.py:42
  73.8 8.6 %collective-permute-start.20 = (bf16[8,72,128]{2,1,0:T(8,128)(2,1)S(1)}, bf16[8,72,128]{2,1,0:T(8,128)(2,1)S(1)}, u32[]{:S(2)}, u32[]{:S(2)}) collective-permute-start(bf16[8,72,128]{2,1,0:T(8,128)(2,1)S(1)} %get-tuple-element.61), channel_id=1, source_target_pairs={{0,12},{4,0},{8,4},{12,8},{1,13},{5,1},{9,5},{13,9},{2,14},{6,2},{... | collective-permute-start | bytes 442376 | tf_op jit(solution)/shard_map/ppermute | solution.py:47
  76.6 5.9 %collective-permute-start.23 = (bf16[8,72,128]{2,1,0:T(8,128)(2,1)S(1)}, bf16[8,72,128]{2,1,0:T(8,128)(2,1)S(1)}, u32[]{:S(2)}, u32[]{:S(2)}) collective-permute-start(bf16[8,72,128]{2,1,0:T(8,128)(2,1)S(1)} %get-tuple-element.62), channel_id=1, source_target_pairs={{0,12},{4,0},{8,4},{12,8},{1,13},{5,1},{9,5},{13,9},{2,14},{6,2},{... | collective-permute-start | bytes 442376 | tf_op jit(solution)/shard_map/ppermute | solution.py:47
  83.4 13.6 %all-to-all-start.1 = ((bf16[16,72,128]{2,1,0:T(8,128)(2,1)}), bf16[16,72,128]{2,1,0:T(8,128)(2,1)S(1)}, u32[]{:S(2)}, u32[]{:S(2)}) async-start(bf16[16,72,128]{2,1,0:T(8,128)(2,1)} %pad_maximum_fusion), calls=%async_computation.1 | async-start | bytes 589824 | tf_op jit(solution)/shard_map/all_to_all | solution.py:431
  97.8 19.3 %all-to-all-start.2 = ((bf16[16,72,128]{2,1,0:T(8,128)(2,1)}), bf16[16,72,128]{2,1,0:T(8,128)(2,1)S(1)}, u32[]{:S(2)}, u32[]{:S(2)}) async-start(bf16[16,72,128]{2,1,0:T(8,128)(2,1)} %broadcast_in_dim.7), calls=%async_computation.2 | async-start | bytes 589824 | tf_op jit(solution)/shard_map/all_to_all | solution.py:29

commit v5 on v4

--- a/solution.py
+++ b/solution.py
@@ -16,7 +16,7 @@
 PADDED = LATENT + LANES
 KTILE = 1024
 GROUPS = 1
-VMEM = 44 * 2**20
+VMEM = 60 * 2**20
 LOG2E = 1.4426950408889634
 UNSEEN = -1e30
 SEQ = ("z", "y_lo")
@@ -47,40 +47,36 @@
     return lax.ppermute(block, "x", [(i, (i - 1) % size) for i in range(size)])
 
 
+def to_side(block):
+    size = lax.axis_size("x")
+    pairs = [(2 * i + c, 2 * ((i + (1 if c else -1)) % size) + c) for i in range(size) for c in range(2)]
+    return lax.ppermute(block, ("x", "core"), pairs)
+
+
+def to_other_side(block):
+    size = lax.axis_size("x")
+    pairs = [(2 * i + c, 2 * ((i + (-1 if c else 1)) % size) + c) for i in range(size) for c in range(2)]
+    return lax.ppermute(block, ("x", "core"), pairs)
+
+
 def gather_over_x(block):
-    half = block.shape[0] // 2
-    low, high = block[:half], block[half:]
-    after_low, before_high = to_previous(low), to_next(high)
-    after_high, before_low = to_previous(high), to_next(low)
-    far_low, far_high = to_previous(after_low), to_next(before_high)
-    return [low, high, after_low, after_high, far_low, far_high, before_low, before_high]
+    after, before = to_previous(block), to_next(block)
+    far = to_side(jnp.where(lax.axis_index("core") == 0, after, before))
+    return [block, after, far, before]
 
 
 def reduce_over_x(own, after, far, before):
-    def send(shift, block):
-        return shift(block.astype(jnp.bfloat16)).astype(jnp.float32)
-
-    low = send(to_next, far[0])
-    high = send(to_previous, far[1])
-    from_before_high = send(to_next, after[1])
-    from_after_low = send(to_previous, before[0])
-    from_before_low = send(to_next, after[0] + low)
-    from_after_high = send(to_previous, before[1] + high)
-    return [
-        (own[0] + from_before_low + from_after_low).astype(jnp.bfloat16),
-        (own[1] + from_before_high + from_after_high).astype(jnp.bfloat16),
-    ]
+    first = lax.axis_index("core") == 0
+    passed = to_other_side(far.astype(jnp.bfloat16)).astype(jnp.float32)
+    after = to_next((after + jnp.where(first, passed, 0.0)).astype(jnp.bfloat16))
+    before = to_previous((before + jnp.where(first, 0.0, passed)).astype(jnp.bfloat16))
+    return (own + after.astype(jnp.float32) + before.astype(jnp.float32)).astype(jnp.bfloat16)
 
 
 def core_sums(keeps, sends):
-    half = keeps[0].shape[0] // 2
     sums = [None] * 4
     for i in (2, 1, 3, 0):
-        other = swap_core(sends[i])
-        sums[i] = [
-            keeps[i][part].astype(jnp.float32) + other[part].astype(jnp.float32)
-            for part in (slice(0, half), slice(half, None))
-        ]
+        sums[i] = keeps[i].astype(jnp.float32) + swap_core(sends[i]).astype(jnp.float32)
     return sums
 
 
@@ -155,15 +151,13 @@
 
 
 def fill_cache(cache, blocks, place, core, sems):
-    slices = len(blocks) // 4
-    half, height = blocks[0].shape[:2]
+    slices = len(blocks) // 2
+    height = blocks[0].shape[1]
     copies = []
     for i, block in enumerate(blocks):
-        which = core if i < 2 * slices else 1 - core
-        x = (place + i % (2 * slices) // 2) % slices
-        start = pl.multiple_of((2 * x + which) * height, 8)
-        owners = pl.ds(i % 2 * half, half)
-        copy = pltpu.make_async_copy(block, cache.at[owners, pl.ds(start, height), :], sems.at[i])
+        which = core if i < slices else 1 - core
+        start = pl.multiple_of((2 * ((place + i) % slices) + which) * height, 8)
+        copy = pltpu.make_async_copy(block, cache.at[:, pl.ds(start, height), :], sems.at[i])
         copy.start()
         copies.append(copy)
     return copies
@@ -174,10 +168,10 @@
 
 
 def attend_kernel(place_ref, offsets_ref, *refs):
-    blocks_hbm, refs = refs[:16], refs[16:]
+    blocks_hbm, refs = refs[:8], refs[8:]
     (ext_hbm, back_hbm, ext_t_hbm, back_t_hbm), outs_hbm, (ds_hbm, cache_hbm), refs = refs[:4], refs[4:12], refs[12:14], refs[14:]
     (ext, back, ext_t, back_t, cache, bias, score, dprob, acc, ds, outs,
-     block_sems, in_sems, ds_sems, out_sems) = refs
+     block_sems, in_sems, ds_sems, out_sems, cache_sems) = refs
     slices = len(outs_hbm) // 2
     height = outs_hbm[0].shape[1]
     place, core = place_ref[0], place_ref[1]
@@ -254,8 +248,12 @@
         if t == tiles - 1:
             deltas[g] = jnp.sum(deltas[g], axis=1, keepdims=True)
 
-    stores = [pltpu.make_async_copy(cache, cache_hbm, block_sems.at[len(blocks_hbm)])]
-    stores[0].start()
+    stores = [
+        pltpu.make_async_copy(cache.at[s], cache_hbm.at[:, s * LANES : (s + 1) * LANES], cache_sems.at[s])
+        for s in range(owners)
+    ]
+    for store in stores:
+        store.start()
 
     def gradients(g, t):
         own, keys = span(g, t)
@@ -300,19 +298,18 @@
 
 def attend(place, offsets, blocks, ext, back, ext_t, back_t):
     rows = ext.shape[0]
-    half, height = blocks[0].shape[:2]
-    owners = 2 * half
+    owners, height = blocks[0].shape[:2]
     keys_total = owners * LANES
     queries = offsets.shape[0] * QBLOCK
     tiles = keys_total // KTILE
     smem = pl.BlockSpec(memory_space=pltpu.SMEM)
     any_place = pl.BlockSpec(memory_space=pl.ANY)
     bf16, f32 = jnp.bfloat16, jnp.float32
-    sums = len(blocks) // 2
+    sums = len(blocks)
     *outs, dscore, whole = pl.pallas_call(
         attend_kernel,
         out_shape=[jax.ShapeDtypeStruct((owners, height, LANES), bf16)] * sums
-        + [jax.ShapeDtypeStruct((rows, keys_total), bf16), jax.ShapeDtypeStruct((owners, PADDED, LANES), bf16)],
+        + [jax.ShapeDtypeStruct((rows, keys_total), bf16), jax.ShapeDtypeStruct((PADDED, keys_total), bf16)],
         in_specs=[smem, smem] + [any_place] * (len(blocks) + 4),
         out_specs=[any_place] * (sums + 2),
         scratch_shapes=[
@@ -327,10 +324,11 @@
             pltpu.VMEM((WIDTH, keys_total), f32),
             pltpu.VMEM((rows, keys_total), bf16),
             pltpu.VMEM((owners, WIDTH, LANES), bf16),
-            pltpu.SemaphoreType.DMA((len(blocks) + 1,)),
+            pltpu.SemaphoreType.DMA((len(blocks),)),
             pltpu.SemaphoreType.DMA((4,)),
             pltpu.SemaphoreType.DMA((GROUPS, tiles)),
             pltpu.SemaphoreType.DMA((sums, tiles)),
+            pltpu.SemaphoreType.DMA((owners,)),
         ],
         compiler_params=pltpu.CompilerParams(vmem_limit_bytes=VMEM),
         cost_estimate=pl.CostEstimate(
@@ -342,11 +340,11 @@
 
 
 def query_kernel(first, ready, place_ref, scale_ref, ds_hbm, cache_hbm, key_hbm, *refs):
-    nope_hbm, rope_hbm, ds, up_key, parts, cache, grad_buf, nope, rope_out, sems = refs[2 * ready :]
+    nope_hbm, rope_hbm, ds, up_key, cache, grad_buf, nope, rope_out, sems = refs[2 * ready :]
     queries = nope.shape[0]
     heads = up_key.shape[1] // NOPE
     loads = [
-        pltpu.make_async_copy(cache_hbm, parts, sems.at[0]),
+        pltpu.make_async_copy(cache_hbm, cache, sems.at[0]),
         pltpu.make_async_copy(ds_hbm.at[first * queries : (first + heads) * queries], ds, sems.at[1]),
         pltpu.make_async_copy(key_hbm.at[:, first * NOPE : (first + heads) * NOPE], up_key, sems.at[2]),
     ]
@@ -354,7 +352,6 @@
         load.start()
     factor = jnp.exp2(scale_ref[...].astype(jnp.float32))
     loads[0].wait()
-    cache[...] = keys_of(parts, 0, parts.shape[0], PADDED)
     loads[1].wait()
     grad_buf[...] = lax.dot_general(ds[...], cache[...], COLS, preferred_element_type=jnp.float32)
     loads[2].wait()
@@ -400,7 +397,6 @@
             pltpu.VMEM((rows, keys_total), bf16),
             pltpu.VMEM((up_key.shape[0], count * NOPE), bf16),
             pltpu.VMEM(whole.shape, bf16),
-            pltpu.VMEM((PADDED, keys_total), bf16),
             pltpu.VMEM((rows, PADDED), f32),
             pltpu.VMEM((queries, count * NOPE), bf16),
             pltpu.VMEM((queries, count * ROPE), bf16),
@@ -426,11 +422,12 @@
     here = gather_over_x(over_seq)
     blocks = here + [swap_core(block) for block in here]
     keeps, sends, dscore, whole = attend(place, offsets, blocks, *projected)
-    slices = jnp.concatenate(reduce_over_x(*core_sums(keeps, sends)))
+    slices = reduce_over_x(*core_sums(keeps, sends))
     early = query_gradients(0, heads // 2, place, scales, dscore, whole, up_key)
-    slices = add_up(lax.all_to_all(slices, SEQ, 0, 0, tiled=True))
     slices, early = lax.optimization_barrier((slices, early))
     query_grads = query_gradients(heads // 2, heads // 2, place, scales, dscore, whole, up_key, early)
+    slices = add_up(lax.all_to_all(slices, SEQ, 0, 0, tiled=True))
+    slices, query_grads = lax.optimization_barrier((slices, query_grads))
     return (owned_columns(slices), *query_grads)
 
 

time: 119 us -> 117 us (0.983)
  blocking collectives: 0 us -> 19.4 us
  starting transfers between devices: 47.9 us -> 34.2 us
  waiting for transfers between devices: 24.7 us -> 18.5 us
  local copies, waits for them, and re-layouts: 8.86 us -> 4.22 us
  other arithmetic: 2.01 us -> 4.68 us
  Pallas kernels: 33.5 us -> 35.1 us
    all_to_all x0 -> x1, blocking collectives: none -> 19.4 us  [to_each(): return lax.all_to_all(copies, axes, 0, 0, tiled=True)]
    all_to_all x2 -> x1, starting transfers between devices: 20.2 us -> 10.1 us  [to_each(): return lax.all_to_all(copies, axes, 0, 0, tiled=True)]
    ppermute x6 -> x2, starting transfers between devices: 12.1 us -> 4.66 us  [to_previous(): return lax.ppermute(block, 'x', [(i, (i - 1) % size) for i in range(size)])]
    ppermute x6 -> x2, waiting for transfers between devices: 9.62 us -> 4.71 us  [to_next(): return lax.ppermute(block, 'x', [(i, (i + 1) % size) for i in range(size)])]
    ppermute x0 -> x2, starting transfers between devices: none -> 4.49 us  [the longest x1 3.48 us: to_other_side(): return lax.ppermute(block, ('x', 'core'), pairs)]
    unnamed x14 -> x20, local copies, waits for them, and re-layouts: 5.93 us -> 2.04 us
    ppermute x0 -> x2, waiting for transfers between devices: none -> 3.73 us  [the longest x1 3.66 us: to_other_side(): return lax.ppermute(block, ('x', 'core'), pairs)]
    all_to_all x2 -> x1, waiting for transfers between devices: 7.38 us -> 4.43 us  [to_each(): return lax.all_to_all(copies, axes, 0, 0, tiled=True)]
  transfers between devices with their start and end apart: 27 -> 16, of which waited for: 12 -> 7; matrix products, arithmetic and copies ran while one was open for 1% -> 4% of each run, Pallas kernels for 15% -> 16%
where the time goes in v5:
time: 117 us
  Pallas kernels  35.1 us (30%)
  starting transfers between devices  34.2 us (29%)
  blocking collectives  19.4 us (17%)
  waiting for transfers between devices  18.5 us (16%)
  other arithmetic  4.68 us (4%)
  local copies, waits for them, and re-layouts  4.22 us (4%)
    all_to_all x1, blocking collectives, to_each(): return lax.all_to_all(copies, axes, 0, 0, tiled=True)  19.4 us
    pallas_call x1, Pallas kernels, attend(): pl.pallas_call(attend_kernel, out_shape=[jax.ShapeDtypeStruct((owners, he...  16.9 us
    pallas_call x2, Pallas kernels, query_gradients(): pl.pallas_call(functools.partial(query_kernel, first, len(ready) // 2), o...  12.7 us
    ppermute x8, starting transfers between devices, swap_core(): return lax.ppermute(block, 'core', [(0, 1), (1, 0)])  10.1 us
    all_to_all x1, starting transfers between devices, to_each(): return lax.all_to_all(copies, axes, 0, 0, tiled=True)  10.1 us
    pallas_call x1, Pallas kernels, project(): pl.pallas_call(project_kernel, out_shape=(jax.ShapeDtypeStruct((rows, PAD...  5.44 us
    ppermute x2, waiting for transfers between devices, to_next(): return lax.ppermute(block, 'x', [(i, (i + 1) % size) for i in range(size)])  4.71 us
    ppermute x2, starting transfers between devices, to_previous(): return lax.ppermute(block, 'x', [(i, (i - 1) % size) for i in range(size)])  4.66 us
  transfers between devices with their start and end apart: 16, of which 7 were waited for; matrix products, arithmetic and copies ran while one was open for 4% of the time, Pallas kernels for 16%

profile of v5, /device:TPU:1, one launch (start us, length us, event | category | flops | bytes accessed | tf_op | source)
XLA Modules:
  0.0 116.9 jit_solution(90812749668272709)
XLA Ops:
  0.6 0.0 copy-start
  0.7 0.9 copy-done
  1.5 0.8 broadcast_in_dim.12
  2.3 10.1 %all-to-all-start = ((bf16[16,72,128]{2,1,0:T(8,128)(2,1)}), bf16[16,72,128]{2,1,0:T(8,128)(2,1)S(1)}, u32[]{:S(2)}, u32[]{:S(2)}) async-start(bf16[16,72,128]{2,1,0:T(8,128)(2,1)} %broadcast_in_dim.12), calls=%async_computation | async-start | bytes 589824 | tf_op jit(solution)/shard_map/all_to_all | solution.py:29
  12.4 1.4 %copy.16.scale_ref = s32[128,1]{1,0:T(8,128)} copy(s32[128,1]{0,1:T(1,128)} %bitcast.11) | data formatting | bytes 1024 | tf_op jit(solution)/shard_map/reshape | solution.py:418
  13.8 5.4 %project.1 = (bf16[1024,640]{1,0:T(8,128)(2,1)}, bf16[1024,512]{1,0:T(8,128)(2,1)}, bf16[576,1024]{1,0:T(8,128)(2,1)}, bf16[512,1024]{1,0:T(8,128)(2,1)}) custom-call(s32[128,1]{1,0:T(8,128)} %copy.16.scale_ref, bf16[128,1024]{1,0:T(8,128)(2,1)} %nope_hbm.1, bf16[128,512]{1,0:T(8,128)(2,1)} %rope_hbm.1, bf16[512,1024]{1,0:T(8,128)(2,1)} %key_hbm.5, ...), custom_call_target="tpu_custom_call" | custom-call | flops 536870912 | bytes 7500000 | tf_op jit(solution)/shard_map/project/pallas_call | solution.py:136
  19.3 4.4 %all-to-all-done.refs_0_ = bf16[16,72,128]{2,1,0:T(8,128)(2,1)S(1)} async-done(((bf16[16,72,128]{2,1,0:T(8,128)(2,1)}), bf16[16,72,128]{2,1,0:T(8,128)(2,1)S(1)}, u32[]{:S(2)}, u32[]{:S(2)}) %all-to-all-start) | async-done | bytes 294944 | tf_op jit(solution)/shard_map/all_to_all | solution.py:29
  23.7 1.2 %collective-permute-start.1 = (bf16[16,72,128]{2,1,0:T(8,128)(2,1)S(1)}, bf16[16,72,128]{2,1,0:T(8,128)(2,1)S(1)}, u32[]{:S(2)}, u32[]{:S(2)}) collective-permute-start(bf16[16,72,128]{2,1,0:T(8,128)(2,1)S(1)} %all-to-all-done.refs_0_), channel_id=1, source_target_pairs={{0,4},{4,8},{8,12},{12,0},{1,5},{5,9},{9,13},{13,1},{2,6},{6,10},{... | collective-permute-start | bytes 884744 | tf_op jit(solution)/shard_map/ppermute | solution.py:42
  24.9 1.5 %collective-permute-start = (bf16[16,72,128]{2,1,0:T(8,128)(2,1)S(1)}, bf16[16,72,128]{2,1,0:T(8,128)(2,1)S(1)}, u32[]{:S(2)}, u32[]{:S(2)}) collective-permute-start(bf16[16,72,128]{2,1,0:T(8,128)(2,1)S(1)} %all-to-all-done.refs_0_), channel_id=1, source_target_pairs={{0,12},{4,0},{8,4},{12,8},{1,13},{5,1},{9,5},{13,9},{2,14},{6,2},{... | collective-permute-start | bytes 884744 | tf_op jit(solution)/shard_map/ppermute | solution.py:47
  26.4 4.7 %collective-permute-done.1.refs_3_ = bf16[16,72,128]{2,1,0:T(8,128)(2,1)S(1)} collective-permute-done((bf16[16,72,128]{2,1,0:T(8,128)(2,1)S(1)}, bf16[16,72,128]{2,1,0:T(8,128)(2,1)S(1)}, u32[]{:S(2)}, u32[]{:S(2)}) %collective-permute-start.1) | collective-permute-done | bytes 294944 | tf_op jit(solution)/shard_map/ppermute | solution.py:42
  31.1 0.0 collective-permute-done.refs_1_
  31.1 1.0 collective-permute-start.2
  32.1 5.3 %collective-permute-start.3 = (bf16[16,72,128]{2,1,0:T(8,128)(2,1)S(1)}, bf16[16,72,128]{2,1,0:T(8,128)(2,1)S(1)}, u32[]{:S(2)}, u32[]{:S(2)}) collective-permute-start(bf16[16,72,128]{2,1,0:T(8,128)(2,1)S(1)} %all-to-all-done.refs_0_), channel_id=1, source_target_pairs={{0,1},{1,0},{2,3},{3,2},{4,5},{5,4},{6,7},{7,6},{8,9},{9,8},{10,11... | collective-permute-start | bytes 884744 | tf_op jit(solution)/shard_map/ppermute | solution.py:33
  37.4 0.0 collective-permute-start.6
  37.4 0.5 collective-permute-start.4
  37.9 0.1 collective-permute-done.2.refs_2_
  38.0 3.7 %collective-permute-start.5 = (bf16[16,72,128]{2,1,0:T(8,128)(2,1)S(1)}, bf16[16,72,128]{2,1,0:T(8,128)(2,1)S(1)}, u32[]{:S(2)}, u32[]{:S(2)}) collective-permute-start(bf16[16,72,128]{2,1,0:T(8,128)(2,1)S(1)} %collective-permute-done.2.refs_2_), channel_id=1, source_target_pairs={{0,1},{1,0},{2,3},{3,2},{4,5},{5,4},{6,7},{7,6},{8,9},{9,8},{10,11... | collective-permute-start | bytes 884744 | tf_op jit(solution)/shard_map/ppermute | solution.py:33
  41.7 0.7 pad_add_fusion.place_ref
  42.3 0.0 collective-permute-done.6.refs_7_
  42.3 0.0 collective-permute-done.4.refs_5_
  42.4 0.5 collective-permute-done.5.refs_6_
  42.9 0.2 copy-done.6
  43.1 0.1 copy-done.7
  43.1 0.1 copy-done.8
  43.3 0.7 copy-done.9
  44.0 16.9 %attend.1 = (bf16[16,72,128]{2,1,0:T(8,128)(2,1)}, bf16[16,72,128]{2,1,0:T(8,128)(2,1)}, bf16[16,72,128]{2,1,0:T(8,128)(2,1)}, bf16[16,72,128]{2,1,0:T(8,128)(2,...) custom-call(s32[2]{0:T(128)} %pad_add_fusion.place_ref, ...), custom_call_target="tpu_custom_call" | custom-call | flops 9663676416 | bytes 14000000 | tf_op jit(solution)/shard_map/attend/pallas_call | solution.py:309
  60.9 0.1 collective-permute-start.9
  61.1 0.5 collective-permute-start.8
  61.5 0.1 collective-permute-start.12
  61.6 1.2 %collective-permute-done.9 = bf16[16,72,128]{2,1,0:T(8,128)(2,1)S(1)} collective-permute-done((bf16[16,72,128]{2,1,0:T(8,128)(2,1)}, bf16[16,72,128]{2,1,0:T(8,128)(2,1)S(1)}, u32[]{:S(2)}, u32[]{:S(2)}) %collective-permute-start.9) | collective-permute-done | bytes 294944 | tf_op jit(solution)/shard_map/ppermute | solution.py:33
  62.8 1.1 add_convert_fusion.1
  63.9 3.5 %collective-permute-start.10 = (bf16[16,72,128]{2,1,0:T(8,128)(2,1)S(1)}, bf16[16,72,128]{2,1,0:T(8,128)(2,1)S(1)}, u32[]{:S(2)}, u32[]{:S(2)}) collective-permute-start(bf16[16,72,128]{2,1,0:T(8,128)(2,1)S(1)} %add_convert_fusion.1), channel_id=1, source_target_pairs={{0,4},{1,13},{4,8},{5,1},{8,12},{9,5},{12,0},{13,9},{2,6},{3,15},{... | collective-permute-start | bytes 884744 | tf_op jit(solution)/shard_map/ppermute | solution.py:59
  67.3 0.0 collective-permute-start.7
  67.4 0.0 collective-permute-done.8
  67.4 0.0 collective-permute-done.12
  67.4 3.7 %collective-permute-done.10 = bf16[16,72,128]{2,1,0:T(8,128)(2,1)S(1)} collective-permute-done((bf16[16,72,128]{2,1,0:T(8,128)(2,1)S(1)}, bf16[16,72,128]{2,1,0:T(8,128)(2,1)S(1)}, u32[]{:S(2)}, u32[]{:S(2)}) %collective-permute-start.10) | collective-permute-done | bytes 294944 | tf_op jit(solution)/shard_map/ppermute | solution.py:59
  71.0 1.3 %fusion.1 = (bf16[16,72,128]{2,1,0:T(8,128)(2,1)S(1)}, bf16[16,72,128]{2,1,0:T(8,128)(2,1)S(1)}) fusion(bf16[16,72,128]{2,1,0:T(8,128)(2,1)S(1)} %collective-permute-done.10, bf16[16,72,128]{2,1,0:T(8,128)(2,1)S(1)} %collective-permute-done.8, bf16[16,72,128]{2,1,0:T(8,128)(2,1)} %get-tuple-element.43, pred[]{:T(512)S(6)} %eq.4, ...), kind=kLoop, calls=%fused_computation.3 | loop fusion | flops 1916928 | bytes 2064385 | tf_op jit(solution)/shard_map/convert_element_type | solution.py:71
  72.3 0.1 collective-permute-start.11
  72.4 3.2 %collective-permute-start.13 = (bf16[16,72,128]{2,1,0:T(8,128)(2,1)S(1)}, bf16[16,72,128]{2,1,0:T(8,128)(2,1)S(1)}, u32[]{:S(2)}, u32[]{:S(2)}) collective-permute-start(bf16[16,72,128]{2,1,0:T(8,128)(2,1)S(1)} %get-tuple-element.62), channel_id=1, source_target_pairs={{0,12},{4,0},{8,4},{12,8},{1,13},{5,1},{9,5},{13,9},{2,14},{6,2},{... | collective-permute-start | bytes 884744 | tf_op jit(solution)/shard_map/ppermute | solution.py:47
  75.6 6.4 %query_gradients_0.1 = (bf16[128,1024]{1,0:T(8,128)(2,1)}, bf16[128,512]{1,0:T(8,128)(2,1)}) custom-call(s32[2]{0:T(128)} %pad_add_fusion.place_ref, s32[128,1]{1,0:T(8,128)} %copy.16.scale_ref, bf16[1024,2048]{1,0:T(8,128)(2,1)} %get-tuple-element.49.ds_hbm, bf16[640,2048]{1,0:T(8,128)(2,1)} %get-tuple-element.50.cache_hbm, bf16[512,1024]{1,0:T(8,128)(2,1)} %key_hbm.5), custom_call_target="tpu_custom_call" | custom-call | flops 1342177280 | bytes 9000000 | tf_op jit(solution)/shard_map/query_gradients_0/pallas_call | solution.py:388
  82.0 0.0 collective-permute-done.7
  82.0 0.0 collective-permute-done.13
  82.0 0.9 add_convert_fusion
  82.9 3.5 %all-to-all-start.1 = ((bf16[16,72,128]{2,1,0:T(8,128)(2,1)}), bf16[16,72,128]{2,1,0:T(8,128)(2,1)S(1)}, u32[]{:S(2)}, u32[]{:S(2)}) async-start(bf16[16,72,128]{2,1,0:T(8,128)(2,1)} %add_convert_fusion), calls=%async_computation.1 | async-start | bytes 589824 | tf_op jit(solution)/shard_map/all_to_all | solution.py:429
  86.4 6.3 %query_gradients_4.1 = (bf16[128,1024]{1,0:T(8,128)(2,1)}, bf16[128,512]{1,0:T(8,128)(2,1)}) custom-call(s32[2]{0:T(128)} %pad_add_fusion.place_ref, s32[128,1]{1,0:T(8,128)} %copy.16.scale_ref, bf16[1024,2048]{1,0:T(8,128)(2,1)} %get-tuple-element.49.ds_hbm, ...), custom_call_target="tpu_custom_call", output_to_operand_aliasing={{0}: (5, {}), {1}: (6, {})} | custom-call | flops 1342177280 | bytes 9000000 | tf_op jit(solution)/shard_map/query_gradients_4/pallas_call | solution.py:388
  92.8 3.9 %all-to-all-done.1 = bf16[16,72,128]{2,1,0:T(8,128)(2,1)S(1)} async-done(((bf16[16,72,128]{2,1,0:T(8,128)(2,1)}), bf16[16,72,128]{2,1,0:T(8,128)(2,1)S(1)}, u32[]{:S(2)}, u32[]{:S(2)}) %all-to-all-start.1) | async-done | bytes 294944 | tf_op jit(solution)/shard_map/all_to_all | solution.py:429
  96.7 19.4 %all_to_all.15 = bf16[16,72,128]{2,1,0:T(8,128)(2,1)S(1)} all-to-all(bf16[16,72,128]{2,1,0:T(8,128)(2,1)S(1)} %broadcast_in_dim.14), channel_id=1, replica_groups=mesh['z'=8,'y_lo'=2,'x'=4,'y_hi'=2,'core'=2] {'x','y_hi','core'}, dimensions={0} | all-to-all | bytes 589824 | tf_op jit(solution)/shard_map/all_to_all | solution.py:29
  116.2 0.7 reduce_sum.25
  (20 shorter events, 0.2 us)
Async XLA Ops:
  0.6 0.9 copy-start
  2.3 21.4 %all-to-all-start = ((bf16[16,72,128]{2,1,0:T(8,128)(2,1)}), bf16[16,72,128]{2,1,0:T(8,128)(2,1)S(1)}, u32[]{:S(2)}, u32[]{:S(2)}) async-start(bf16[16,72,128]{2,1,0:T(8,128)(2,1)} %broadcast_in_dim.12), calls=%async_computation | async-start | bytes 589824 | tf_op jit(solution)/shard_map/all_to_all | solution.py:29
  23.7 19.2 %copy-start.3 = (bf16[16,72,128]{2,1,0:T(8,128)(2,1)}, bf16[16,72,128]{2,1,0:T(8,128)(2,1)S(1)}, u32[]{:S(2)}) copy-start(bf16[16,72,128]{2,1,0:T(8,128)(2,1)S(1)} %all-to-all-done.refs_0_) | copy-start | bytes 884740
  23.7 7.4 %collective-permute-start.1 = (bf16[16,72,128]{2,1,0:T(8,128)(2,1)S(1)}, bf16[16,72,128]{2,1,0:T(8,128)(2,1)S(1)}, u32[]{:S(2)}, u32[]{:S(2)}) collective-permute-start(bf16[16,72,128]{2,1,0:T(8,128)(2,1)S(1)} %all-to-all-done.refs_0_), channel_id=1, source_target_pairs={{0,4},{4,8},{8,12},{12,0},{1,5},{5,9},{9,13},{13,1},{2,6},{6,10},{... | collective-permute-start | bytes 884744 | tf_op jit(solution)/shard_map/ppermute | solution.py:42
  24.9 6.2 %collective-permute-start = (bf16[16,72,128]{2,1,0:T(8,128)(2,1)S(1)}, bf16[16,72,128]{2,1,0:T(8,128)(2,1)S(1)}, u32[]{:S(2)}, u32[]{:S(2)}) collective-permute-start(bf16[16,72,128]{2,1,0:T(8,128)(2,1)S(1)} %all-to-all-done.refs_0_), channel_id=1, source_target_pairs={{0,12},{4,0},{8,4},{12,8},{1,13},{5,1},{9,5},{13,9},{2,14},{6,2},{... | collective-permute-start | bytes 884744 | tf_op jit(solution)/shard_map/ppermute | solution.py:47
  31.1 11.8 %copy-start.1 = (bf16[16,72,128]{2,1,0:T(8,128)(2,1)}, bf16[16,72,128]{2,1,0:T(8,128)(2,1)S(1)}, u32[]{:S(2)}) copy-start(bf16[16,72,128]{2,1,0:T(8,128)(2,1)S(1)} %collective-permute-done.1.refs_3_) | copy-start | bytes 884740
  31.1 11.8 %copy-start.2 = (bf16[16,72,128]{2,1,0:T(8,128)(2,1)}, bf16[16,72,128]{2,1,0:T(8,128)(2,1)S(1)}, u32[]{:S(2)}) copy-start(bf16[16,72,128]{2,1,0:T(8,128)(2,1)S(1)} %collective-permute-done.refs_1_) | copy-start | bytes 884740
  31.1 6.9 %collective-permute-start.2 = (bf16[16,72,128]{2,1,0:T(8,128)(2,1)S(1)}, bf16[16,72,128]{2,1,0:T(8,128)(2,1)S(1)}, u32[]{:S(2)}, u32[]{:S(2)}) collective-permute-start(bf16[16,72,128]{2,1,0:T(8,128)(2,1)S(1)} %broadcast_select_fusion), channel_id=1, source_target_pairs={{0,12},{1,5},{4,0},{5,9},{8,4},{9,13},{12,8},{13,1},{2,14},{3,7},{... | collective-permute-start | bytes 884744 | tf_op jit(solution)/shard_map/ppermute | solution.py:53
  32.1 10.2 %collective-permute-start.3 = (bf16[16,72,128]{2,1,0:T(8,128)(2,1)S(1)}, bf16[16,72,128]{2,1,0:T(8,128)(2,1)S(1)}, u32[]{:S(2)}, u32[]{:S(2)}) collective-permute-start(bf16[16,72,128]{2,1,0:T(8,128)(2,1)S(1)} %all-to-all-done.refs_0_), channel_id=1, source_target_pairs={{0,1},{1,0},{2,3},{3,2},{4,5},{5,4},{6,7},{7,6},{8,9},{9,8},{10,11... | collective-permute-start | bytes 884744 | tf_op jit(solution)/shard_map/ppermute | solution.py:33
  37.4 4.9 %collective-permute-start.6 = (bf16[16,72,128]{2,1,0:T(8,128)(2,1)S(1)}, bf16[16,72,128]{2,1,0:T(8,128)(2,1)S(1)}, u32[]{:S(2)}, u32[]{:S(2)}) collective-permute-start(bf16[16,72,128]{2,1,0:T(8,128)(2,1)S(1)} %collective-permute-done.1.refs_3_), channel_id=1, source_target_pairs={{0,1},{1,0},{2,3},{3,2},{4,5},{5,4},{6,7},{7,6},{8,9},{9,8},{10,11... | collective-permute-start | bytes 884744 | tf_op jit(solution)/shard_map/ppermute | solution.py:33
  37.4 4.9 %collective-permute-start.4 = (bf16[16,72,128]{2,1,0:T(8,128)(2,1)S(1)}, bf16[16,72,128]{2,1,0:T(8,128)(2,1)S(1)}, u32[]{:S(2)}, u32[]{:S(2)}) collective-permute-start(bf16[16,72,128]{2,1,0:T(8,128)(2,1)S(1)} %collective-permute-done.refs_1_), channel_id=1, source_target_pairs={{0,1},{1,0},{2,3},{3,2},{4,5},{5,4},{6,7},{7,6},{8,9},{9,8},{10,11... | collective-permute-start | bytes 884744 | tf_op jit(solution)/shard_map/ppermute | solution.py:33
  38.0 4.9 %copy-start.5 = (bf16[16,72,128]{2,1,0:T(8,128)(2,1)}, bf16[16,72,128]{2,1,0:T(8,128)(2,1)S(1)}, u32[]{:S(2)}) copy-start(bf16[16,72,128]{2,1,0:T(8,128)(2,1)S(1)} %collective-permute-done.2.refs_2_) | copy-start | bytes 884740
  38.0 4.9 %collective-permute-start.5 = (bf16[16,72,128]{2,1,0:T(8,128)(2,1)S(1)}, bf16[16,72,128]{2,1,0:T(8,128)(2,1)S(1)}, u32[]{:S(2)}, u32[]{:S(2)}) collective-permute-start(bf16[16,72,128]{2,1,0:T(8,128)(2,1)S(1)} %collective-permute-done.2.refs_2_), channel_id=1, source_target_pairs={{0,1},{1,0},{2,3},{3,2},{4,5},{5,4},{6,7},{7,6},{8,9},{9,8},{10,11... | collective-permute-start | bytes 884744 | tf_op jit(solution)/shard_map/ppermute | solution.py:33
  42.3 0.7 copy-start.6
  42.3 0.8 copy-start.7
  42.3 0.9 copy-start.8
  43.3 0.7 copy-start.9
  60.9 1.9 %collective-permute-start.9 = (bf16[16,72,128]{2,1,0:T(8,128)(2,1)}, bf16[16,72,128]{2,1,0:T(8,128)(2,1)S(1)}, u32[]{:S(2)}, u32[]{:S(2)}) collective-permute-start(bf16[16,72,128]{2,1,0:T(8,128)(2,1)} %get-tuple-element.46), channel_id=1, source_target_pairs={{0,1},{1,0},{2,3},{3,2},{4,5},{5,4},{6,7},{7,6},{8,9},{9,8},{10,11... | collective-permute-start | bytes 884744 | tf_op jit(solution)/shard_map/ppermute | solution.py:33
  61.1 6.3 %collective-permute-start.8 = (bf16[16,72,128]{2,1,0:T(8,128)(2,1)}, bf16[16,72,128]{2,1,0:T(8,128)(2,1)S(1)}, u32[]{:S(2)}, u32[]{:S(2)}) collective-permute-start(bf16[16,72,128]{2,1,0:T(8,128)(2,1)} %get-tuple-element.44), channel_id=1, source_target_pairs={{0,1},{1,0},{2,3},{3,2},{4,5},{5,4},{6,7},{7,6},{8,9},{9,8},{10,11... | collective-permute-start | bytes 884744 | tf_op jit(solution)/shard_map/ppermute | solution.py:33
  61.5 5.8 %collective-permute-start.12 = (bf16[16,72,128]{2,1,0:T(8,128)(2,1)}, bf16[16,72,128]{2,1,0:T(8,128)(2,1)S(1)}, u32[]{:S(2)}, u32[]{:S(2)}) collective-permute-start(bf16[16,72,128]{2,1,0:T(8,128)(2,1)} %get-tuple-element.48), channel_id=1, source_target_pairs={{0,1},{1,0},{2,3},{3,2},{4,5},{5,4},{6,7},{7,6},{8,9},{9,8},{10,11... | collective-permute-start | bytes 884744 | tf_op jit(solution)/shard_map/ppermute | solution.py:33
  63.9 7.2 %collective-permute-start.10 = (bf16[16,72,128]{2,1,0:T(8,128)(2,1)S(1)}, bf16[16,72,128]{2,1,0:T(8,128)(2,1)S(1)}, u32[]{:S(2)}, u32[]{:S(2)}) collective-permute-start(bf16[16,72,128]{2,1,0:T(8,128)(2,1)S(1)} %add_convert_fusion.1), channel_id=1, source_target_pairs={{0,4},{1,13},{4,8},{5,1},{8,12},{9,5},{12,0},{13,9},{2,6},{3,15},{... | collective-permute-start | bytes 884744 | tf_op jit(solution)/shard_map/ppermute | solution.py:59
  67.3 14.6 %collective-permute-start.7 = (bf16[16,72,128]{2,1,0:T(8,128)(2,1)}, bf16[16,72,128]{2,1,0:T(8,128)(2,1)S(1)}, u32[]{:S(2)}, u32[]{:S(2)}) collective-permute-start(bf16[16,72,128]{2,1,0:T(8,128)(2,1)} %get-tuple-element.42), channel_id=1, source_target_pairs={{0,1},{1,0},{2,3},{3,2},{4,5},{5,4},{6,7},{7,6},{8,9},{9,8},{10,11... | collective-permute-start | bytes 884744 | tf_op jit(solution)/shard_map/ppermute | solution.py:33
  72.3 9.7 %collective-permute-start.11 = (bf16[16,72,128]{2,1,0:T(8,128)(2,1)S(1)}, bf16[16,72,128]{2,1,0:T(8,128)(2,1)S(1)}, u32[]{:S(2)}, u32[]{:S(2)}) collective-permute-start(bf16[16,72,128]{2,1,0:T(8,128)(2,1)S(1)} %get-tuple-element.61), channel_id=1, source_target_pairs={{0,4},{4,8},{8,12},{12,0},{1,5},{5,9},{9,13},{13,1},{2,6},{6,10},{... | collective-permute-start | bytes 884744 | tf_op jit(solution)/shard_map/ppermute | solution.py:42
  72.4 9.6 %collective-permute-start.13 = (bf16[16,72,128]{2,1,0:T(8,128)(2,1)S(1)}, bf16[16,72,128]{2,1,0:T(8,128)(2,1)S(1)}, u32[]{:S(2)}, u32[]{:S(2)}) collective-permute-start(bf16[16,72,128]{2,1,0:T(8,128)(2,1)S(1)} %get-tuple-element.62), channel_id=1, source_target_pairs={{0,12},{4,0},{8,4},{12,8},{1,13},{5,1},{9,5},{13,9},{2,14},{6,2},{... | collective-permute-start | bytes 884744 | tf_op jit(solution)/shard_map/ppermute | solution.py:47
  75.6 6.4 %copy-start.4 = (bf16[16,72,128]{2,1,0:T(8,128)(2,1)S(1)}, bf16[16,72,128]{2,1,0:T(8,128)(2,1)}, u32[]{:S(2)}) copy-start(bf16[16,72,128]{2,1,0:T(8,128)(2,1)} %get-tuple-element.41) | copy-start | bytes 884740
  82.9 13.8 %all-to-all-start.1 = ((bf16[16,72,128]{2,1,0:T(8,128)(2,1)}), bf16[16,72,128]{2,1,0:T(8,128)(2,1)S(1)}, u32[]{:S(2)}, u32[]{:S(2)}) async-start(bf16[16,72,128]{2,1,0:T(8,128)(2,1)} %add_convert_fusion), calls=%async_computation.1 | async-start | bytes 589824 | tf_op jit(solution)/shard_map/all_to_all | solution.py:429

commit v6 on v5

--- a/solution.py
+++ b/solution.py
@@ -49,25 +49,18 @@
 
 def to_side(block):
     size = lax.axis_size("x")
-    pairs = [(2 * i + c, 2 * ((i + (1 if c else -1)) % size) + c) for i in range(size) for c in range(2)]
-    return lax.ppermute(block, ("x", "core"), pairs)
-
-
-def to_other_side(block):
-    size = lax.axis_size("x")
     pairs = [(2 * i + c, 2 * ((i + (-1 if c else 1)) % size) + c) for i in range(size) for c in range(2)]
     return lax.ppermute(block, ("x", "core"), pairs)
 
 
 def gather_over_x(block):
-    after, before = to_previous(block), to_next(block)
-    far = to_side(jnp.where(lax.axis_index("core") == 0, after, before))
-    return [block, after, far, before]
+    half = block.shape[0] // 2
+    return [block, to_previous(block[:half]), to_next(block[half:])]
 
 
 def reduce_over_x(own, after, far, before):
     first = lax.axis_index("core") == 0
-    passed = to_other_side(far.astype(jnp.bfloat16)).astype(jnp.float32)
+    passed = to_side(far.astype(jnp.bfloat16)).astype(jnp.float32)
     after = to_next((after + jnp.where(first, passed, 0.0)).astype(jnp.bfloat16))
     before = to_previous((before + jnp.where(first, 0.0, passed)).astype(jnp.bfloat16))
     return (own + after.astype(jnp.float32) + before.astype(jnp.float32)).astype(jnp.bfloat16)
@@ -151,13 +144,15 @@
 
 
 def fill_cache(cache, blocks, place, core, sems):
-    slices = len(blocks) // 2
-    height = blocks[0].shape[1]
+    parts = len(blocks) // 2
+    half, height = blocks[1].shape[:2]
     copies = []
     for i, block in enumerate(blocks):
-        which = core if i < slices else 1 - core
-        start = pl.multiple_of((2 * ((place + i) % slices) + which) * height, 8)
-        copy = pltpu.make_async_copy(block, cache.at[:, pl.ds(start, height), :], sems.at[i])
+        which = core if i < parts else 1 - core
+        parity = (place + (i % parts > 0)) % 2
+        owners = ((0, 2 * half), (0, half), (half, half))[i % parts]
+        start = pl.multiple_of((2 * parity + which) * height, 16)
+        copy = pltpu.make_async_copy(block, cache.at[pl.ds(*owners), pl.ds(start, height), :], sems.at[i])
         copy.start()
         copies.append(copy)
     return copies
@@ -168,10 +163,10 @@
 
 
 def attend_kernel(place_ref, offsets_ref, *refs):
-    blocks_hbm, refs = refs[:8], refs[8:]
+    blocks_hbm, refs = refs[:6], refs[6:]
     (ext_hbm, back_hbm, ext_t_hbm, back_t_hbm), outs_hbm, (ds_hbm, cache_hbm), refs = refs[:4], refs[4:12], refs[12:14], refs[14:]
     (ext, back, ext_t, back_t, cache, bias, score, dprob, acc, ds, outs,
-     block_sems, in_sems, ds_sems, out_sems, cache_sems) = refs
+     block_sems, in_sems, ds_sems, out_sems) = refs
     slices = len(outs_hbm) // 2
     height = outs_hbm[0].shape[1]
     place, core = place_ref[0], place_ref[1]
@@ -248,12 +243,8 @@
         if t == tiles - 1:
             deltas[g] = jnp.sum(deltas[g], axis=1, keepdims=True)
 
-    stores = [
-        pltpu.make_async_copy(cache.at[s], cache_hbm.at[:, s * LANES : (s + 1) * LANES], cache_sems.at[s])
-        for s in range(owners)
-    ]
-    for store in stores:
-        store.start()
+    stores = [pltpu.make_async_copy(cache, cache_hbm, block_sems.at[len(blocks_hbm)])]
+    stores[0].start()
 
     def gradients(g, t):
         own, keys = span(g, t)
@@ -296,20 +287,21 @@
         store.wait()
 
 
-def attend(place, offsets, blocks, ext, back, ext_t, back_t):
+def attend(slices, place, offsets, blocks, ext, back, ext_t, back_t):
     rows = ext.shape[0]
-    owners, height = blocks[0].shape[:2]
+    owners = blocks[0].shape[0]
+    height = WIDTH // (2 * slices)
     keys_total = owners * LANES
     queries = offsets.shape[0] * QBLOCK
     tiles = keys_total // KTILE
     smem = pl.BlockSpec(memory_space=pltpu.SMEM)
     any_place = pl.BlockSpec(memory_space=pl.ANY)
     bf16, f32 = jnp.bfloat16, jnp.float32
-    sums = len(blocks)
+    sums = 2 * slices
     *outs, dscore, whole = pl.pallas_call(
         attend_kernel,
         out_shape=[jax.ShapeDtypeStruct((owners, height, LANES), bf16)] * sums
-        + [jax.ShapeDtypeStruct((rows, keys_total), bf16), jax.ShapeDtypeStruct((PADDED, keys_total), bf16)],
+        + [jax.ShapeDtypeStruct((rows, keys_total), bf16), jax.ShapeDtypeStruct((owners, PADDED, LANES), bf16)],
         in_specs=[smem, smem] + [any_place] * (len(blocks) + 4),
         out_specs=[any_place] * (sums + 2),
         scratch_shapes=[
@@ -324,11 +316,10 @@
             pltpu.VMEM((WIDTH, keys_total), f32),
             pltpu.VMEM((rows, keys_total), bf16),
             pltpu.VMEM((owners, WIDTH, LANES), bf16),
-            pltpu.SemaphoreType.DMA((len(blocks),)),
+            pltpu.SemaphoreType.DMA((len(blocks) + 1,)),
             pltpu.SemaphoreType.DMA((4,)),
             pltpu.SemaphoreType.DMA((GROUPS, tiles)),
             pltpu.SemaphoreType.DMA((sums, tiles)),
-            pltpu.SemaphoreType.DMA((owners,)),
         ],
         compiler_params=pltpu.CompilerParams(vmem_limit_bytes=VMEM),
         cost_estimate=pl.CostEstimate(
@@ -339,93 +330,82 @@
     return outs[: sums // 2], outs[sums // 2 :], dscore, whole
 
 
-def query_kernel(first, ready, place_ref, scale_ref, ds_hbm, cache_hbm, key_hbm, *refs):
-    nope_hbm, rope_hbm, ds, up_key, cache, grad_buf, nope, rope_out, sems = refs[2 * ready :]
-    queries = nope.shape[0]
+def query_kernel(scale_ref, ds_hbm, cache_hbm, key_hbm, *refs):
+    nope_ref, rope_ref, ds, up_key, parts, cache, grad_buf, sems = refs
+    queries = nope_ref.shape[0]
+    half = ds.shape[0] // 2
     heads = up_key.shape[1] // NOPE
     loads = [
-        pltpu.make_async_copy(cache_hbm, cache, sems.at[0]),
-        pltpu.make_async_copy(ds_hbm.at[first * queries : (first + heads) * queries], ds, sems.at[1]),
-        pltpu.make_async_copy(key_hbm.at[:, first * NOPE : (first + heads) * NOPE], up_key, sems.at[2]),
+        pltpu.make_async_copy(cache_hbm, parts, sems.at[0]),
+        pltpu.make_async_copy(ds_hbm.at[:half], ds.at[:half], sems.at[1]),
+        pltpu.make_async_copy(ds_hbm.at[half:], ds.at[half:], sems.at[2]),
+        pltpu.make_async_copy(key_hbm, up_key, sems.at[3]),
     ]
     for load in loads:
         load.start()
     factor = jnp.exp2(scale_ref[...].astype(jnp.float32))
     loads[0].wait()
-    loads[1].wait()
-    grad_buf[...] = lax.dot_general(ds[...], cache[...], COLS, preferred_element_type=jnp.float32)
-    loads[2].wait()
+    cache[...] = keys_of(parts, 0, parts.shape[0], PADDED)
+    for i in range(2):
+        own = slice(i * half, (i + 1) * half)
+        loads[1 + i].wait()
+        grad_buf[own, :] = lax.dot_general(ds[own, :], cache[...], COLS, preferred_element_type=jnp.float32)
+    loads[3].wait()
     for h in range(heads):
         lanes = slice(h * NOPE, (h + 1) * NOPE)
         grad = grad_buf[h * queries : (h + 1) * queries, :]
         part = jnp.dot(grad[:, :LATENT].astype(jnp.bfloat16), up_key[:, lanes], preferred_element_type=jnp.float32)
-        nope[:, lanes] = (part * factor).astype(jnp.bfloat16)
+        nope_ref[:, lanes] = (part * factor).astype(jnp.bfloat16)
         rope = grad[:, LATENT:] * factor
         if h % 2 == 0:
             even = rope
         else:
             pair = slice(h // 2 * LANES, (h // 2 + 1) * LANES)
-            rope_out[:, pair] = (even + pltpu.roll(rope, ROPE, 1)).astype(jnp.bfloat16)
-    stores = [
-        pltpu.make_async_copy(nope, nope_hbm.at[:, first * NOPE : (first + heads) * NOPE], sems.at[3]),
-        pltpu.make_async_copy(rope_out, rope_hbm.at[:, first * ROPE : (first + heads) * ROPE], sems.at[4]),
-    ]
-    for store in stores:
-        store.start()
-    for store in stores:
-        store.wait()
-
-
-def query_gradients(first, count, place, scales, dscore, whole, up_key, ready=()):
-    keys_total = dscore.shape[1]
+            rope_ref[:, pair] = (even + pltpu.roll(rope, ROPE, 1)).astype(jnp.bfloat16)
+
+
+def query_gradients(scales, dscore, whole, up_key):
+    rows, keys_total = dscore.shape
     heads = up_key.shape[1] // NOPE
     queries = scales.shape[0]
-    rows = count * queries
-    smem = pl.BlockSpec(memory_space=pltpu.SMEM)
     vmem = pl.BlockSpec(memory_space=pltpu.VMEM)
     any_place = pl.BlockSpec(memory_space=pl.ANY)
     bf16, f32 = jnp.bfloat16, jnp.float32
     return pl.pallas_call(
-        functools.partial(query_kernel, first, len(ready) // 2),
+        query_kernel,
         out_shape=(
             jax.ShapeDtypeStruct((queries, heads * NOPE), bf16),
             jax.ShapeDtypeStruct((queries, heads * ROPE), bf16),
         ),
-        in_specs=[smem, vmem] + [any_place] * (3 + len(ready)),
-        out_specs=(any_place, any_place),
+        in_specs=[vmem] + [any_place] * 3,
         scratch_shapes=[
-            pltpu.VMEM((rows, keys_total), bf16),
-            pltpu.VMEM((up_key.shape[0], count * NOPE), bf16),
+            pltpu.VMEM(dscore.shape, bf16),
+            pltpu.VMEM(up_key.shape, bf16),
             pltpu.VMEM(whole.shape, bf16),
+            pltpu.VMEM((PADDED, keys_total), bf16),
             pltpu.VMEM((rows, PADDED), f32),
-            pltpu.VMEM((queries, count * NOPE), bf16),
-            pltpu.VMEM((queries, count * ROPE), bf16),
-            pltpu.SemaphoreType.DMA((5,)),
+            pltpu.SemaphoreType.DMA((4,)),
         ],
-        input_output_aliases={5 + i: i for i in range(len(ready))},
         compiler_params=pltpu.CompilerParams(vmem_limit_bytes=58 * 2**20),
         cost_estimate=pl.CostEstimate(
             flops=2 * rows * keys_total * PADDED, bytes_accessed=9_000_000, transcendentals=0),
-        name=f"query_gradients_{first}",
-    )(place, scales, dscore, whole, up_key, *ready)
+        name="query_gradients",
+    )(scales, dscore, whole, up_key)
 
 
 def per_device(cache, query_nope, query_rope, scale_exp, offsets, up_key, up_value, grad_out):
     place = jnp.stack([lax.axis_index("x"), lax.axis_index("core")]).astype(jnp.int32)
-    own = lax.axis_index(("x", "core"))
-    height = WIDTH // (lax.axis_size("x") * lax.axis_size("core"))
+    own = place[0] % 2 * 2 + place[1]
+    height = WIDTH // 4
     mine = lax.dynamic_slice_in_dim(cache.T, own * height, height, 0)
     scales = scale_exp.reshape(-1, 1)
-    heads = up_key.shape[1] // NOPE
     projected = project(scales, query_nope, query_rope, up_key, up_value, grad_out)
     over_seq, projected = lax.optimization_barrier((to_each(mine, SEQ), projected))
     here = gather_over_x(over_seq)
     blocks = here + [swap_core(block) for block in here]
-    keeps, sends, dscore, whole = attend(place, offsets, blocks, *projected)
+    keeps, sends, dscore, whole = attend(lax.axis_size("x"), place, offsets, blocks, *projected)
     slices = reduce_over_x(*core_sums(keeps, sends))
-    early = query_gradients(0, heads // 2, place, scales, dscore, whole, up_key)
-    slices, early = lax.optimization_barrier((slices, early))
-    query_grads = query_gradients(heads // 2, heads // 2, place, scales, dscore, whole, up_key, early)
+    query_grads = query_gradients(scales, dscore, whole, up_key)
     slices = add_up(lax.all_to_all(slices, SEQ, 0, 0, tiled=True))
     slices, query_grads = lax.optimization_barrier((slices, query_grads))
     return (owned_columns(slices), *query_grads)

time: 117 us -> 117 us (level)
  Pallas kernels: 35.1 us -> 31.3 us
  waiting for transfers between devices: 18.5 us -> 22.2 us
  starting transfers between devices: 34.2 us -> 31.8 us
  blocking collectives: 19.4 us -> 20.7 us
    all_to_all x1, waiting for transfers between devices: 4.43 us -> 10.1 us  [to_each(): return lax.all_to_all(copies, axes, 0, 0, tiled=True)]
    ppermute x1 -> x0, waiting for transfers between devices: 3.66 us -> none  [to_other_side(): return lax.ppermute(block, ('x', 'core'), pairs)]
    ppermute x1, waiting for transfers between devices: 0.07 us -> 3.66 us  [to_side(): return lax.ppermute(block, ('x', 'core'), pairs)]
    pallas_call x2 -> x1, Pallas kernels: 12.7 us -> 9.2 us  [query_gradients(): pl.pallas_call(query_kernel, out_shape=(jax.ShapeDtypeStruct((queries, he...]
    ppermute x1 -> x0, starting transfers between devices: 3.48 us -> none  [to_other_side(): return lax.ppermute(block, ('x', 'core'), pairs)]
    all_to_all x1, waiting for transfers between devices: 3.87 us -> 0.76 us  [per_device(): slices = add_up(lax.all_to_all(slices, SEQ, 0, 0, tiled=True))]
    ppermute x1, starting transfers between devices: 1 us -> 2.84 us  [to_side(): return lax.ppermute(block, ('x', 'core'), pairs)]
    ppermute x8 -> x7, starting transfers between devices: 10.1 us -> 8.6 us  [swap_core(): return lax.ppermute(block, 'core', [(0, 1), (1, 0)])]
  transfers between devices with their start and end apart: 16 -> 14, of which waited for: 7 -> 8; matrix products, arithmetic and copies ran while one was open for 4% -> 4% of each run, Pallas kernels for 16% -> 13%
where the time goes in v6:
time: 117 us; the launch traced here: 116 us
  starting transfers between devices  31.8 us (27%)
  Pallas kernels  31.3 us (27%)
  waiting for transfers between devices  22.2 us (19%)
  blocking collectives  20.7 us (18%)
  local copies, waits for them, and re-layouts  4.82 us (4%)
  other arithmetic  4.55 us (4%)
    all_to_all x1, blocking collectives, to_each(): return lax.all_to_all(copies, axes, 0, 0, tiled=True)  20.7 us
    pallas_call x1, Pallas kernels, attend(): pl.pallas_call(attend_kernel, out_shape=[jax.ShapeDtypeStruct((owners, he...  16.7 us
    all_to_all x1, starting transfers between devices, to_each(): return lax.all_to_all(copies, axes, 0, 0, tiled=True)  10.1 us
    all_to_all x1, waiting for transfers between devices, to_each(): return lax.all_to_all(copies, axes, 0, 0, tiled=True)  10.1 us
    pallas_call x1, Pallas kernels, query_gradients(): pl.pallas_call(query_kernel, out_shape=(jax.ShapeDtypeStruct((queries, he...  9.2 us
    ppermute x7, starting transfers between devices, swap_core(): return lax.ppermute(block, 'core', [(0, 1), (1, 0)])  8.6 us
    ppermute x2, waiting for transfers between devices, to_next(): return lax.ppermute(block, 'x', [(i, (i + 1) % size) for i in range(size)])  6.02 us
    pallas_call x1, Pallas kernels, project(): pl.pallas_call(project_kernel, out_shape=(jax.ShapeDtypeStruct((rows, PAD...  5.44 us
  transfers between devices with their start and end apart: 14, of which 8 were waited for; matrix products, arithmetic and copies ran while one was open for 4% of the time, Pallas kernels for 13%

profile of v6, /device:TPU:1, one launch (start us, length us, event | category | flops | bytes accessed | tf_op | source)
XLA Modules:
  0.0 116.2 jit_solution(6986538197050606097)
XLA Ops:
  0.6 0.0 copy-start
  0.7 0.9 copy-done
  1.6 0.9 broadcast_in_dim.12
  2.5 10.1 %all-to-all-start = ((bf16[16,144,128]{2,1,0:T(8,128)(2,1)}), bf16[16,144,128]{2,1,0:T(8,128)(2,1)S(1)}, u32[]{:S(2)}, u32[]{:S(2)}) async-start(bf16[16,144,128]{2,1,0:T(8,128)(2,1)} %broadcast_in_dim.12), calls=%async_computation | async-start | bytes 1179648 | tf_op jit(solution)/shard_map/all_to_all | solution.py:29
  12.6 1.4 %copy.13.scale_ref = s32[128,1]{1,0:T(8,128)} copy(s32[128,1]{0,1:T(1,128)} %bitcast.11) | data formatting | bytes 1024 | tf_op jit(solution)/shard_map/reshape | solution.py:401
  14.0 5.4 %project.1 = (bf16[1024,640]{1,0:T(8,128)(2,1)}, bf16[1024,512]{1,0:T(8,128)(2,1)}, bf16[576,1024]{1,0:T(8,128)(2,1)}, bf16[512,1024]{1,0:T(8,128)(2,1)}) custom-call(s32[128,1]{1,0:T(8,128)} %copy.13.scale_ref, bf16[128,1024]{1,0:T(8,128)(2,1)} %nope_hbm.1, bf16[128,512]{1,0:T(8,128)(2,1)} %rope_hbm.1, bf16[512,1024]{1,0:T(8,128)(2,1)} %key_hbm.3, ...), custom_call_target="tpu_custom_call" | custom-call | flops 536870912 | bytes 7500000 | tf_op jit(solution)/shard_map/project/pallas_call | solution.py:129
  19.4 10.1 %all-to-all-done.refs_0_ = bf16[16,144,128]{2,1,0:T(8,128)(2,1)S(1)} async-done(((bf16[16,144,128]{2,1,0:T(8,128)(2,1)}), bf16[16,144,128]{2,1,0:T(8,128)(2,1)S(1)}, u32[]{:S(2)}, u32[]{:S(2)}) %all-to-all-start) | async-done | bytes 589856 | tf_op jit(solution)/shard_map/all_to_all | solution.py:29
  29.5 1.3 %collective-permute-start.1 = (bf16[8,144,128]{2,1,0:T(8,128)(2,1)S(1)}, bf16[8,144,128]{2,1,0:T(8,128)(2,1)S(1)}, u32[]{:S(2)}, u32[]{:S(2)}) collective-permute-start(bf16[8,144,128]{2,1,0:T(8,128)(2,1)S(1)} %get-tuple-element.51), channel_id=1, source_target_pairs={{0,4},{4,8},{8,12},{12,0},{1,5},{5,9},{9,13},{13,1},{2,6},{6,10},{... | collective-permute-start | bytes 884744 | tf_op jit(solution)/shard_map/ppermute | solution.py:42
  30.8 1.5 %collective-permute-start = (bf16[8,144,128]{2,1,0:T(8,128)(2,1)S(1)}, bf16[8,144,128]{2,1,0:T(8,128)(2,1)S(1)}, u32[]{:S(2)}, u32[]{:S(2)}) collective-permute-start(bf16[8,144,128]{2,1,0:T(8,128)(2,1)S(1)} %get-tuple-element.52), channel_id=1, source_target_pairs={{0,12},{4,0},{8,4},{12,8},{1,13},{5,1},{9,5},{13,9},{2,14},{6,2},{... | collective-permute-start | bytes 884744 | tf_op jit(solution)/shard_map/ppermute | solution.py:47
  32.3 3.4 %collective-permute-start.2 = (bf16[16,144,128]{2,1,0:T(8,128)(2,1)S(1)}, bf16[16,144,128]{2,1,0:T(8,128)(2,1)S(1)}, u32[]{:S(2)}, u32[]{:S(2)}) collective-permute-start(bf16[16,144,128]{2,1,0:T(8,128)(2,1)S(1)} %all-to-all-done.refs_0_), channel_id=1, source_target_pairs={{0,1},{1,0},{2,3},{3,2},{4,5},{5,4},{6,7},{7,6},{8,9},{9,8},{10,11... | collective-permute-start | bytes 1769480 | tf_op jit(solution)/shard_map/ppermute | solution.py:33
  35.7 0.7 collective-permute-done.1.refs_2_
  36.4 4.0 %collective-permute-start.4 = (bf16[8,144,128]{2,1,0:T(8,128)(2,1)S(1)}, bf16[8,144,128]{2,1,0:T(8,128)(2,1)S(1)}, u32[]{:S(2)}, u32[]{:S(2)}) collective-permute-start(bf16[8,144,128]{2,1,0:T(8,128)(2,1)S(1)} %collective-permute-done.1.refs_2_), channel_id=1, source_target_pairs={{0,1},{1,0},{2,3},{3,2},{4,5},{5,4},{6,7},{7,6},{8,9},{9,8},{10,11... | collective-permute-start | bytes 884744 | tf_op jit(solution)/shard_map/ppermute | solution.py:33
  40.4 0.0 collective-permute-done.refs_1_
  40.4 0.3 collective-permute-start.3
  40.7 0.6 pad_add_fusion.place_ref
  41.2 0.4 collective-permute-done.4.refs_5_
  41.6 0.4 collective-permute-done.3.refs_4_
  42.0 0.0 collective-permute-done.2.refs_3_
  42.0 0.0 copy-done.1
  42.0 0.0 copy-done.4
  42.0 0.0 copy-done.5
  42.0 0.3 copy-done.6
  42.3 0.4 copy-done.7
  42.7 0.8 copy-done.3
  43.6 16.7 %attend.1 = (bf16[16,72,128]{2,1,0:T(8,128)(2,1)}, bf16[16,72,128]{2,1,0:T(8,128)(2,1)}, bf16[16,72,128]{2,1,0:T(8,128)(2,1)}, bf16[16,72,128]{2,1,0:T(8,128)(2,...) custom-call(s32[2]{0:T(128)} %pad_add_fusion.place_ref, ...), custom_call_target="tpu_custom_call" | custom-call | flops 9663676416 | bytes 14000000 | tf_op jit(solution)/shard_map/attend/pallas_call | solution.py:301
  60.2 0.0 copy-start.2
  60.3 0.5 collective-permute-start.7
  60.7 0.1 collective-permute-start.6
  60.9 0.4 collective-permute-start.10
  61.2 0.9 collective-permute-done.7
  62.1 1.0 add_convert_fusion.1
  63.2 2.8 %collective-permute-start.8 = (bf16[16,72,128]{2,1,0:T(8,128)(2,1)S(1)}, bf16[16,72,128]{2,1,0:T(8,128)(2,1)S(1)}, u32[]{:S(2)}, u32[]{:S(2)}) collective-permute-start(bf16[16,72,128]{2,1,0:T(8,128)(2,1)S(1)} %add_convert_fusion.1), channel_id=1, source_target_pairs={{0,4},{1,13},{4,8},{5,1},{8,12},{9,5},{12,0},{13,9},{2,6},{3,15},{... | collective-permute-start | bytes 884744 | tf_op jit(solution)/shard_map/ppermute | solution.py:53
  66.0 0.0 collective-permute-start.5
  66.0 0.0 collective-permute-done.6
  66.0 0.0 collective-permute-done.10
  66.0 3.7 %collective-permute-done.8 = bf16[16,72,128]{2,1,0:T(8,128)(2,1)S(1)} collective-permute-done((bf16[16,72,128]{2,1,0:T(8,128)(2,1)S(1)}, bf16[16,72,128]{2,1,0:T(8,128)(2,1)S(1)}, u32[]{:S(2)}, u32[]{:S(2)}) %collective-permute-start.8) | collective-permute-done | bytes 294944 | tf_op jit(solution)/shard_map/ppermute | solution.py:53
  69.7 1.3 %fusion.1 = (bf16[16,72,128]{2,1,0:T(8,128)(2,1)S(1)}, bf16[16,72,128]{2,1,0:T(8,128)(2,1)S(1)}) fusion(bf16[16,72,128]{2,1,0:T(8,128)(2,1)S(1)} %collective-permute-done.8, bf16[16,72,128]{2,1,0:T(8,128)(2,1)S(1)} %collective-permute-done.6, bf16[16,72,128]{2,1,0:T(8,128)(2,1)} %get-tuple-element.38, pred[]{:T(512)S(6)} %eq.5, ...), kind=kLoop, calls=%fused_computation.3 | loop fusion | flops 1916928 | bytes 2064385 | tf_op jit(solution)/shard_map/convert_element_type | solution.py:64
  71.0 0.8 collective-permute-start.9
  71.8 2.5 %collective-permute-start.11 = (bf16[16,72,128]{2,1,0:T(8,128)(2,1)S(1)}, bf16[16,72,128]{2,1,0:T(8,128)(2,1)S(1)}, u32[]{:S(2)}, u32[]{:S(2)}) collective-permute-start(bf16[16,72,128]{2,1,0:T(8,128)(2,1)S(1)} %get-tuple-element.54), channel_id=1, source_target_pairs={{0,12},{4,0},{8,4},{12,8},{1,13},{5,1},{9,5},{13,9},{2,14},{6,2},{... | collective-permute-start | bytes 884744 | tf_op jit(solution)/shard_map/ppermute | solution.py:47
  74.3 0.0 collective-permute-done.5
  74.3 5.3 %collective-permute-done.9 = bf16[16,72,128]{2,1,0:T(8,128)(2,1)S(1)} collective-permute-done((bf16[16,72,128]{2,1,0:T(8,128)(2,1)S(1)}, bf16[16,72,128]{2,1,0:T(8,128)(2,1)S(1)}, u32[]{:S(2)}, u32[]{:S(2)}) %collective-permute-start.9) | collective-permute-done | bytes 294944 | tf_op jit(solution)/shard_map/ppermute | solution.py:42
  79.6 0.0 collective-permute-done.11
  79.6 0.9 add_convert_fusion
  80.5 4.2 %all-to-all-start.1 = ((bf16[16,72,128]{2,1,0:T(8,128)(2,1)}), bf16[16,72,128]{2,1,0:T(8,128)(2,1)S(1)}, u32[]{:S(2)}, u32[]{:S(2)}) async-start(bf16[16,72,128]{2,1,0:T(8,128)(2,1)} %add_convert_fusion), calls=%async_computation.1 | async-start | bytes 589824 | tf_op jit(solution)/shard_map/all_to_all | solution.py:409
  84.7 9.2 %query_gradients.1 = (bf16[128,1024]{1,0:T(8,128)(2,1)}, bf16[128,512]{1,0:T(8,128)(2,1)}) custom-call(s32[128,1]{1,0:T(8,128)} %copy.13.scale_ref, bf16[1024,2048]{1,0:T(8,128)(2,1)} %get-tuple-element.44.ds_hbm, bf16[16,640,128]{2,1,0:T(8,128)(2,1)} %get-tuple-element.45.cache_hbm, bf16[512,1024]{1,0:T(8,128)(2,1)} %key_hbm.3), custom_call_target="tpu_custom_call" | custom-call | flops 2684354560 | bytes 9000000 | tf_op jit(solution)/shard_map/query_gradients/pallas_call | solution.py:374
  93.9 0.8 all-to-all-done.1
  94.8 20.7 %all_to_all.15 = bf16[16,72,128]{2,1,0:T(8,128)(2,1)S(1)} all-to-all(bf16[16,72,128]{2,1,0:T(8,128)(2,1)S(1)} %broadcast_in_dim.14), channel_id=1, replica_groups=mesh['z'=8,'y_lo'=2,'x'=4,'y_hi'=2,'core'=2] {'x','y_hi','core'}, dimensions={0} | all-to-all | bytes 589824 | tf_op jit(solution)/shard_map/all_to_all | solution.py:29
  115.5 0.7 reduce_sum.25
  (11 shorter events, 0.1 us)
Async XLA Ops:
  0.6 0.9 copy-start
  2.5 27.0 %all-to-all-start = ((bf16[16,144,128]{2,1,0:T(8,128)(2,1)}), bf16[16,144,128]{2,1,0:T(8,128)(2,1)S(1)}, u32[]{:S(2)}, u32[]{:S(2)}) async-start(bf16[16,144,128]{2,1,0:T(8,128)(2,1)} %broadcast_in_dim.12), calls=%async_computation | async-start | bytes 1179648 | tf_op jit(solution)/shard_map/all_to_all | solution.py:29
  29.5 12.5 %copy-start.1 = (bf16[16,144,128]{2,1,0:T(8,128)(2,1)}, bf16[16,144,128]{2,1,0:T(8,128)(2,1)S(1)}, u32[]{:S(2)}) copy-start(bf16[16,144,128]{2,1,0:T(8,128)(2,1)S(1)} %all-to-all-done.refs_0_) | copy-start | bytes 1769476
  29.5 6.9 %collective-permute-start.1 = (bf16[8,144,128]{2,1,0:T(8,128)(2,1)S(1)}, bf16[8,144,128]{2,1,0:T(8,128)(2,1)S(1)}, u32[]{:S(2)}, u32[]{:S(2)}) collective-permute-start(bf16[8,144,128]{2,1,0:T(8,128)(2,1)S(1)} %get-tuple-element.51), channel_id=1, source_target_pairs={{0,4},{4,8},{8,12},{12,0},{1,5},{5,9},{9,13},{13,1},{2,6},{6,10},{... | collective-permute-start | bytes 884744 | tf_op jit(solution)/shard_map/ppermute | solution.py:42
  30.8 9.5 %collective-permute-start = (bf16[8,144,128]{2,1,0:T(8,128)(2,1)S(1)}, bf16[8,144,128]{2,1,0:T(8,128)(2,1)S(1)}, u32[]{:S(2)}, u32[]{:S(2)}) collective-permute-start(bf16[8,144,128]{2,1,0:T(8,128)(2,1)S(1)} %get-tuple-element.52), channel_id=1, source_target_pairs={{0,12},{4,0},{8,4},{12,8},{1,13},{5,1},{9,5},{13,9},{2,14},{6,2},{... | collective-permute-start | bytes 884744 | tf_op jit(solution)/shard_map/ppermute | solution.py:47
  32.3 9.7 %collective-permute-start.2 = (bf16[16,144,128]{2,1,0:T(8,128)(2,1)S(1)}, bf16[16,144,128]{2,1,0:T(8,128)(2,1)S(1)}, u32[]{:S(2)}, u32[]{:S(2)}) collective-permute-start(bf16[16,144,128]{2,1,0:T(8,128)(2,1)S(1)} %all-to-all-done.refs_0_), channel_id=1, source_target_pairs={{0,1},{1,0},{2,3},{3,2},{4,5},{5,4},{6,7},{7,6},{8,9},{9,8},{10,11... | collective-permute-start | bytes 1769480 | tf_op jit(solution)/shard_map/ppermute | solution.py:33
  36.4 5.6 %copy-start.4 = (bf16[8,144,128]{2,1,0:T(8,128)(2,1)}, bf16[8,144,128]{2,1,0:T(8,128)(2,1)S(1)}, u32[]{:S(2)}) copy-start(bf16[8,144,128]{2,1,0:T(8,128)(2,1)S(1)} %collective-permute-done.1.refs_2_) | copy-start | bytes 884740
  36.4 5.2 %collective-permute-start.4 = (bf16[8,144,128]{2,1,0:T(8,128)(2,1)S(1)}, bf16[8,144,128]{2,1,0:T(8,128)(2,1)S(1)}, u32[]{:S(2)}, u32[]{:S(2)}) collective-permute-start(bf16[8,144,128]{2,1,0:T(8,128)(2,1)S(1)} %collective-permute-done.1.refs_2_), channel_id=1, source_target_pairs={{0,1},{1,0},{2,3},{3,2},{4,5},{5,4},{6,7},{7,6},{8,9},{9,8},{10,11... | collective-permute-start | bytes 884744 | tf_op jit(solution)/shard_map/ppermute | solution.py:33
  40.4 1.6 %copy-start.5 = (bf16[8,144,128]{2,1,0:T(8,128)(2,1)}, bf16[8,144,128]{2,1,0:T(8,128)(2,1)S(1)}, u32[]{:S(2)}) copy-start(bf16[8,144,128]{2,1,0:T(8,128)(2,1)S(1)} %collective-permute-done.refs_1_) | copy-start | bytes 884740
  40.4 1.6 %collective-permute-start.3 = (bf16[8,144,128]{2,1,0:T(8,128)(2,1)S(1)}, bf16[8,144,128]{2,1,0:T(8,128)(2,1)S(1)}, u32[]{:S(2)}, u32[]{:S(2)}) collective-permute-start(bf16[8,144,128]{2,1,0:T(8,128)(2,1)S(1)} %collective-permute-done.refs_1_), channel_id=1, source_target_pairs={{0,1},{1,0},{2,3},{3,2},{4,5},{5,4},{6,7},{7,6},{8,9},{9,8},{10,11... | collective-permute-start | bytes 884744 | tf_op jit(solution)/shard_map/ppermute | solution.py:33
  41.6 0.7 copy-start.6
  42.0 0.7 copy-start.7
  42.7 0.8 copy-start.3
  60.2 19.3 %copy-start.2 = (bf16[16,72,128]{2,1,0:T(8,128)(2,1)S(1)}, bf16[16,72,128]{2,1,0:T(8,128)(2,1)}, u32[]{:S(2)}) copy-start(bf16[16,72,128]{2,1,0:T(8,128)(2,1)} %get-tuple-element.36) | copy-start | bytes 884740
  60.3 1.9 %collective-permute-start.7 = (bf16[16,72,128]{2,1,0:T(8,128)(2,1)}, bf16[16,72,128]{2,1,0:T(8,128)(2,1)S(1)}, u32[]{:S(2)}, u32[]{:S(2)}) collective-permute-start(bf16[16,72,128]{2,1,0:T(8,128)(2,1)} %get-tuple-element.41), channel_id=1, source_target_pairs={{0,1},{1,0},{2,3},{3,2},{4,5},{5,4},{6,7},{7,6},{8,9},{9,8},{10,11... | collective-permute-start | bytes 884744 | tf_op jit(solution)/shard_map/ppermute | solution.py:33
  60.7 5.3 %collective-permute-start.6 = (bf16[16,72,128]{2,1,0:T(8,128)(2,1)}, bf16[16,72,128]{2,1,0:T(8,128)(2,1)S(1)}, u32[]{:S(2)}, u32[]{:S(2)}) collective-permute-start(bf16[16,72,128]{2,1,0:T(8,128)(2,1)} %get-tuple-element.39), channel_id=1, source_target_pairs={{0,1},{1,0},{2,3},{3,2},{4,5},{5,4},{6,7},{7,6},{8,9},{9,8},{10,11... | collective-permute-start | bytes 884744 | tf_op jit(solution)/shard_map/ppermute | solution.py:33
  60.9 5.2 %collective-permute-start.10 = (bf16[16,72,128]{2,1,0:T(8,128)(2,1)}, bf16[16,72,128]{2,1,0:T(8,128)(2,1)S(1)}, u32[]{:S(2)}, u32[]{:S(2)}) collective-permute-start(bf16[16,72,128]{2,1,0:T(8,128)(2,1)} %get-tuple-element.43), channel_id=1, source_target_pairs={{0,1},{1,0},{2,3},{3,2},{4,5},{5,4},{6,7},{7,6},{8,9},{9,8},{10,11... | collective-permute-start | bytes 884744 | tf_op jit(solution)/shard_map/ppermute | solution.py:33
  63.2 6.5 %collective-permute-start.8 = (bf16[16,72,128]{2,1,0:T(8,128)(2,1)S(1)}, bf16[16,72,128]{2,1,0:T(8,128)(2,1)S(1)}, u32[]{:S(2)}, u32[]{:S(2)}) collective-permute-start(bf16[16,72,128]{2,1,0:T(8,128)(2,1)S(1)} %add_convert_fusion.1), channel_id=1, source_target_pairs={{0,4},{1,13},{4,8},{5,1},{8,12},{9,5},{12,0},{13,9},{2,6},{3,15},{... | collective-permute-start | bytes 884744 | tf_op jit(solution)/shard_map/ppermute | solution.py:53
  66.0 8.3 %collective-permute-start.5 = (bf16[16,72,128]{2,1,0:T(8,128)(2,1)}, bf16[16,72,128]{2,1,0:T(8,128)(2,1)S(1)}, u32[]{:S(2)}, u32[]{:S(2)}) collective-permute-start(bf16[16,72,128]{2,1,0:T(8,128)(2,1)} %get-tuple-element.37), channel_id=1, source_target_pairs={{0,1},{1,0},{2,3},{3,2},{4,5},{5,4},{6,7},{7,6},{8,9},{9,8},{10,11... | collective-permute-start | bytes 884744 | tf_op jit(solution)/shard_map/ppermute | solution.py:33
  71.0 8.6 %collective-permute-start.9 = (bf16[16,72,128]{2,1,0:T(8,128)(2,1)S(1)}, bf16[16,72,128]{2,1,0:T(8,128)(2,1)S(1)}, u32[]{:S(2)}, u32[]{:S(2)}) collective-permute-start(bf16[16,72,128]{2,1,0:T(8,128)(2,1)S(1)} %get-tuple-element.53), channel_id=1, source_target_pairs={{0,4},{4,8},{8,12},{12,0},{1,5},{5,9},{9,13},{13,1},{2,6},{6,10},{... | collective-permute-start | bytes 884744 | tf_op jit(solution)/shard_map/ppermute | solution.py:42
  71.8 7.8 %collective-permute-start.11 = (bf16[16,72,128]{2,1,0:T(8,128)(2,1)S(1)}, bf16[16,72,128]{2,1,0:T(8,128)(2,1)S(1)}, u32[]{:S(2)}, u32[]{:S(2)}) collective-permute-start(bf16[16,72,128]{2,1,0:T(8,128)(2,1)S(1)} %get-tuple-element.54), channel_id=1, source_target_pairs={{0,12},{4,0},{8,4},{12,8},{1,13},{5,1},{9,5},{13,9},{2,14},{6,2},{... | collective-permute-start | bytes 884744 | tf_op jit(solution)/shard_map/ppermute | solution.py:47
  80.5 14.2 %all-to-all-start.1 = ((bf16[16,72,128]{2,1,0:T(8,128)(2,1)}), bf16[16,72,128]{2,1,0:T(8,128)(2,1)S(1)}, u32[]{:S(2)}, u32[]{:S(2)}) async-start(bf16[16,72,128]{2,1,0:T(8,128)(2,1)} %add_convert_fusion), calls=%async_computation.1 | async-start | bytes 589824 | tf_op jit(solution)/shard_map/all_to_all | solution.py:409

commit v7 on v6

--- a/solution.py
+++ b/solution.py
@@ -16,7 +16,7 @@
 PADDED = LATENT + LANES
 KTILE = 1024
 GROUPS = 1
-VMEM = 60 * 2**20
+VMEM = 49 * 2**20
 LOG2E = 1.4426950408889634
 UNSEEN = -1e30
 SEQ = ("z", "y_lo")
@@ -330,16 +330,18 @@
     return outs[: sums // 2], outs[sums // 2 :], dscore, whole
 
 
-def query_kernel(scale_ref, ds_hbm, cache_hbm, key_hbm, *refs):
-    nope_ref, rope_ref, ds, up_key, parts, cache, grad_buf, sems = refs
-    queries = nope_ref.shape[0]
+def query_kernel(first, ready, scale_ref, ds_hbm, cache_hbm, key_hbm, *refs):
+    nope_hbm, rope_hbm, ds, up_key, parts, cache, grad_buf, nope, rope_out, sems = refs[2 * ready :]
+    queries = nope.shape[0]
+    count = ds.shape[0] // queries
     half = ds.shape[0] // 2
+    start = first * queries
     heads = up_key.shape[1] // NOPE
     loads = [
         pltpu.make_async_copy(cache_hbm, parts, sems.at[0]),
-        pltpu.make_async_copy(ds_hbm.at[:half], ds.at[:half], sems.at[1]),
-        pltpu.make_async_copy(ds_hbm.at[half:], ds.at[half:], sems.at[2]),
-        pltpu.make_async_copy(key_hbm, up_key, sems.at[3]),
+        pltpu.make_async_copy(ds_hbm.at[start : start + half], ds.at[:half], sems.at[1]),
+        pltpu.make_async_copy(ds_hbm.at[start + half : start + 2 * half], ds.at[half:], sems.at[2]),
+        pltpu.make_async_copy(key_hbm.at[:, first * NOPE : (first + count) * NOPE], up_key, sems.at[3]),
     ]
     for load in loads:
         load.start()
@@ -355,42 +357,55 @@
         lanes = slice(h * NOPE, (h + 1) * NOPE)
         grad = grad_buf[h * queries : (h + 1) * queries, :]
         part = jnp.dot(grad[:, :LATENT].astype(jnp.bfloat16), up_key[:, lanes], preferred_element_type=jnp.float32)
-        nope_ref[:, lanes] = (part * factor).astype(jnp.bfloat16)
+        nope[:, lanes] = (part * factor).astype(jnp.bfloat16)
         rope = grad[:, LATENT:] * factor
         if h % 2 == 0:
             even = rope
         else:
             pair = slice(h // 2 * LANES, (h // 2 + 1) * LANES)
-            rope_ref[:, pair] = (even + pltpu.roll(rope, ROPE, 1)).astype(jnp.bfloat16)
-
-
-def query_gradients(scales, dscore, whole, up_key):
-    rows, keys_total = dscore.shape
+            rope_out[:, pair] = (even + pltpu.roll(rope, ROPE, 1)).astype(jnp.bfloat16)
+    stores = [
+        pltpu.make_async_copy(nope, nope_hbm.at[:, first * NOPE : (first + count) * NOPE], sems.at[4]),
+        pltpu.make_async_copy(rope_out, rope_hbm.at[:, first * ROPE : (first + count) * ROPE], sems.at[5]),
+    ]
+    for store in stores:
+        store.start()
+    for store in stores:
+        store.wait()
+
+
+def query_gradients(first, count, scales, dscore, whole, up_key, ready=()):
+    keys_total = dscore.shape[1]
     heads = up_key.shape[1] // NOPE
     queries = scales.shape[0]
+    rows = count * queries
     vmem = pl.BlockSpec(memory_space=pltpu.VMEM)
     any_place = pl.BlockSpec(memory_space=pl.ANY)
     bf16, f32 = jnp.bfloat16, jnp.float32
     return pl.pallas_call(
-        query_kernel,
+        functools.partial(query_kernel, first, len(ready) // 2),
         out_shape=(
             jax.ShapeDtypeStruct((queries, heads * NOPE), bf16),
             jax.ShapeDtypeStruct((queries, heads * ROPE), bf16),
         ),
-        in_specs=[vmem] + [any_place] * 3,
+        in_specs=[vmem] + [any_place] * (3 + len(ready)),
+        out_specs=(any_place, any_place),
         scratch_shapes=[
-            pltpu.VMEM(dscore.shape, bf16),
-            pltpu.VMEM(up_key.shape, bf16),
+            pltpu.VMEM((rows, keys_total), bf16),
+            pltpu.VMEM((up_key.shape[0], count * NOPE), bf16),
             pltpu.VMEM(whole.shape, bf16),
             pltpu.VMEM((PADDED, keys_total), bf16),
             pltpu.VMEM((rows, PADDED), f32),
-            pltpu.SemaphoreType.DMA((4,)),
+            pltpu.VMEM((queries, count * NOPE), bf16),
+            pltpu.VMEM((queries, count * ROPE), bf16),
+            pltpu.SemaphoreType.DMA((6,)),
         ],
+        input_output_aliases={4 + i: i for i in range(len(ready))},
         compiler_params=pltpu.CompilerParams(vmem_limit_bytes=58 * 2**20),
         cost_estimate=pl.CostEstimate(
             flops=2 * rows * keys_total * PADDED, bytes_accessed=9_000_000, transcendentals=0),
-        name="query_gradients",
-    )(scales, dscore, whole, up_key)
+        name=f"query_gradients_{first}",
+    )(scales, dscore, whole, up_key, *ready)
 
 
 def per_device(cache, query_nope, query_rope, scale_exp, offsets, up_key, up_value, grad_out):
@@ -405,7 +420,10 @@
     blocks = here + [swap_core(block) for block in here]
     keeps, sends, dscore, whole = attend(lax.axis_size("x"), place, offsets, blocks, *projected)
     slices = reduce_over_x(*core_sums(keeps, sends))
-    query_grads = query_gradients(scales, dscore, whole, up_key)
+    part = up_key.shape[1] // NOPE // 2
+    early = query_gradients(0, part, scales, dscore, whole, up_key)
+    slices, early = lax.optimization_barrier((slices, early))
+    query_grads = query_gradients(part, part, scales, dscore, whole, up_key, early)
     slices = add_up(lax.all_to_all(slices, SEQ, 0, 0, tiled=True))
     slices, query_grads = lax.optimization_barrier((slices, query_grads))
     return (owned_columns(slices), *query_grads)

time: 117 us -> 112 us (0.957)
  Pallas kernels: 31.3 us -> 34.5 us
  other arithmetic: 4.55 us -> 2.07 us
  waiting for transfers between devices: 22.2 us -> 19.8 us
  local copies, waits for them, and re-layouts: 4.82 us -> 3.27 us
  blocking collectives: 20.7 us -> 19.3 us
    ppermute x2, waiting for transfers between devices: 6.02 us -> 0.73 us  [to_next(): return lax.ppermute(block, 'x', [(i, (i + 1) % size) for i in range(size)])]
    pallas_call x1 -> x2, Pallas kernels: 9.2 us -> 13 us  [query_gradients(): pl.pallas_call(functools.partial(query_kernel, first, len(ready) // 2), o...]
    all_to_all x1, waiting for transfers between devices: 0.76 us -> 3.41 us  [per_device(): slices = add_up(lax.all_to_all(slices, SEQ, 0, 0, tiled=True))]
    unnamed x16 -> x4, local copies, waits for them, and re-layouts: 2.44 us -> 0.89 us
    all_to_all x1, blocking collectives: 20.7 us -> 19.3 us  [to_each(): return lax.all_to_all(copies, axes, 0, 0, tiled=True)]
  transfers between devices with their start and end apart: 14 -> 14, of which waited for: 8 -> 7; matrix products, arithmetic and copies ran while one was open for 4% -> 2% of each run, Pallas kernels for 13% -> 17%
where the time goes in v7:
time: 112 us
  Pallas kernels  34.5 us (31%)
  starting transfers between devices  32.3 us (29%)
  waiting for transfers between devices  19.8 us (18%)
  blocking collectives  19.3 us (17%)
  local copies, waits for them, and re-layouts  3.27 us (3%)
  other arithmetic  2.07 us (2%)
    all_to_all x1, blocking collectives, to_each(): return lax.all_to_all(copies, axes, 0, 0, tiled=True)  19.3 us
    pallas_call x1, Pallas kernels, attend(): pl.pallas_call(attend_kernel, out_shape=[jax.ShapeDtypeStruct((owners, he...  16 us
    pallas_call x2, Pallas kernels, query_gradients(): pl.pallas_call(functools.partial(query_kernel, first, len(ready) // 2), o...  13 us
    all_to_all x1, starting transfers between devices, to_each(): return lax.all_to_all(copies, axes, 0, 0, tiled=True)  10.3 us
    all_to_all x1, waiting for transfers between devices, to_each(): return lax.all_to_all(copies, axes, 0, 0, tiled=True)  10 us
    ppermute x7, starting transfers between devices, swap_core(): return lax.ppermute(block, 'core', [(0, 1), (1, 0)])  8.61 us
    pallas_call x1, Pallas kernels, project(): pl.pallas_call(project_kernel, out_shape=(jax.ShapeDtypeStruct((rows, PAD...  5.47 us
    all_to_all x1, starting transfers between devices, per_device(): slices = add_up(lax.all_to_all(slices, SEQ, 0, 0, tiled=True))  4.52 us
  transfers between devices with their start and end apart: 14, of which 7 were waited for; matrix products, arithmetic and copies ran while one was open for 2% of the time, Pallas kernels for 17%

profile of v7, /device:TPU:1, one launch (start us, length us, event | category | flops | bytes accessed | tf_op | source)
XLA Modules:
  0.0 111.9 jit_solution(1757120163721695045)
XLA Ops:
  0.6 0.0 copy-start
  0.7 0.9 copy-done
  1.6 0.9 broadcast_in_dim.12
  2.5 0.0 copy-start.1
  2.5 10.3 %all-to-all-start = ((bf16[16,144,128]{2,1,0:T(8,128)(2,1)}), bf16[16,144,128]{2,1,0:T(8,128)(2,1)S(1)}, u32[]{:S(2)}, u32[]{:S(2)}) async-start(bf16[16,144,128]{2,1,0:T(8,128)(2,1)} %broadcast_in_dim.12), calls=%async_computation | async-start | bytes 1179648 | tf_op jit(solution)/shard_map/all_to_all | solution.py:29
  12.7 1.4 %copy.16.scale_ref = s32[128,1]{1,0:T(8,128)} copy(s32[128,1]{0,1:T(1,128)} %bitcast.11) | data formatting | bytes 1024 | tf_op jit(solution)/shard_map/reshape | solution.py:416
  14.1 5.5 %project.1 = (bf16[1024,640]{1,0:T(8,128)(2,1)}, bf16[1024,512]{1,0:T(8,128)(2,1)}, bf16[576,1024]{1,0:T(8,128)(2,1)}, bf16[512,1024]{1,0:T(8,128)(2,1)}) custom-call(s32[128,1]{1,0:T(8,128)} %copy.16.scale_ref, bf16[128,1024]{1,0:T(8,128)(2,1)} %nope_hbm.1, bf16[128,512]{1,0:T(8,128)(2,1)} %rope_hbm.1, bf16[512,1024]{1,0:T(8,128)(2,1)} %key_hbm.5, ...), custom_call_target="tpu_custom_call" | custom-call | flops 536870912 | bytes 7500000 | tf_op jit(solution)/shard_map/project/pallas_call | solution.py:129
  19.6 10.0 %all-to-all-done.refs_0_ = bf16[16,144,128]{2,1,0:T(8,128)(2,1)S(1)} async-done(((bf16[16,144,128]{2,1,0:T(8,128)(2,1)}), bf16[16,144,128]{2,1,0:T(8,128)(2,1)S(1)}, u32[]{:S(2)}, u32[]{:S(2)}) %all-to-all-start) | async-done | bytes 589856 | tf_op jit(solution)/shard_map/all_to_all | solution.py:29
  29.7 1.3 %collective-permute-start.1 = (bf16[8,144,128]{2,1,0:T(8,128)(2,1)S(1)}, bf16[8,144,128]{2,1,0:T(8,128)(2,1)S(1)}, u32[]{:S(2)}, u32[]{:S(2)}) collective-permute-start(bf16[8,144,128]{2,1,0:T(8,128)(2,1)S(1)} %get-tuple-element.61), channel_id=1, source_target_pairs={{0,4},{4,8},{8,12},{12,0},{1,5},{5,9},{9,13},{13,1},{2,6},{6,10},{... | collective-permute-start | bytes 884744 | tf_op jit(solution)/shard_map/ppermute | solution.py:42
  31.0 1.5 %collective-permute-start = (bf16[8,144,128]{2,1,0:T(8,128)(2,1)S(1)}, bf16[8,144,128]{2,1,0:T(8,128)(2,1)S(1)}, u32[]{:S(2)}, u32[]{:S(2)}) collective-permute-start(bf16[8,144,128]{2,1,0:T(8,128)(2,1)S(1)} %get-tuple-element.62), channel_id=1, source_target_pairs={{0,12},{4,0},{8,4},{12,8},{1,13},{5,1},{9,5},{13,9},{2,14},{6,2},{... | collective-permute-start | bytes 884744 | tf_op jit(solution)/shard_map/ppermute | solution.py:47
  32.4 3.4 %collective-permute-start.2 = (bf16[16,144,128]{2,1,0:T(8,128)(2,1)S(1)}, bf16[16,144,128]{2,1,0:T(8,128)(2,1)S(1)}, u32[]{:S(2)}, u32[]{:S(2)}) collective-permute-start(bf16[16,144,128]{2,1,0:T(8,128)(2,1)S(1)} %all-to-all-done.refs_0_), channel_id=1, source_target_pairs={{0,1},{1,0},{2,3},{3,2},{4,5},{5,4},{6,7},{7,6},{8,9},{9,8},{10,11... | collective-permute-start | bytes 1769480 | tf_op jit(solution)/shard_map/ppermute | solution.py:33
  35.8 0.7 collective-permute-done.1.refs_2_
  36.5 4.0 %collective-permute-start.4 = (bf16[8,144,128]{2,1,0:T(8,128)(2,1)S(1)}, bf16[8,144,128]{2,1,0:T(8,128)(2,1)S(1)}, u32[]{:S(2)}, u32[]{:S(2)}) collective-permute-start(bf16[8,144,128]{2,1,0:T(8,128)(2,1)S(1)} %collective-permute-done.1.refs_2_), channel_id=1, source_target_pairs={{0,1},{1,0},{2,3},{3,2},{4,5},{5,4},{6,7},{7,6},{8,9},{9,8},{10,11... | collective-permute-start | bytes 884744 | tf_op jit(solution)/shard_map/ppermute | solution.py:33
  40.5 0.0 collective-permute-done.refs_1_
  40.5 0.3 collective-permute-start.3
  40.8 0.1 pad_add_fusion.place_ref
  40.9 0.9 collective-permute-done.4.refs_5_
  41.7 0.4 collective-permute-done.3.refs_4_
  42.1 0.0 collective-permute-done.2.refs_3_
  42.1 0.0 copy-done.1
  42.1 16.0 %attend.1 = (bf16[16,72,128]{2,1,0:T(8,128)(2,1)S(1)}, bf16[16,72,128]{2,1,0:T(8,128)(2,1)S(1)}, bf16[16,72,128]{2,1,0:T(8,128)(2,1)S(1)}, bf16[16,72,128]{2,1,0...) custom-call(s32[2]{0:T(128)S(1)} %pad_add_fusion.place_ref, ...), custom_call_target="tpu_custom_call" | custom-call | flops 9663676416 | bytes 14000000 | tf_op jit(solution)/shard_map/attend/pallas_call | solution.py:301
  58.2 0.5 collective-permute-start.7
  58.6 0.1 collective-permute-start.6
  58.8 0.4 collective-permute-start.10
  59.1 0.7 collective-permute-done.7
  59.8 0.1 add_convert_fusion.1
  59.9 2.8 %collective-permute-start.8 = (bf16[16,72,128]{2,1,0:T(8,128)(2,1)S(1)}, bf16[16,72,128]{2,1,0:T(8,128)(2,1)S(1)}, u32[]{:S(2)}, u32[]{:S(2)}) collective-permute-start(bf16[16,72,128]{2,1,0:T(8,128)(2,1)S(1)} %add_convert_fusion.1), channel_id=1, source_target_pairs={{0,4},{1,13},{4,8},{5,1},{8,12},{9,5},{12,0},{13,9},{2,6},{3,15},{... | collective-permute-start | bytes 884744 | tf_op jit(solution)/shard_map/ppermute | solution.py:53
  62.8 0.0 collective-permute-start.5
  62.8 0.0 collective-permute-done.6
  62.8 0.0 collective-permute-done.10
  62.8 3.7 %collective-permute-done.8 = bf16[16,72,128]{2,1,0:T(8,128)(2,1)S(1)} collective-permute-done((bf16[16,72,128]{2,1,0:T(8,128)(2,1)S(1)}, bf16[16,72,128]{2,1,0:T(8,128)(2,1)S(1)}, u32[]{:S(2)}, u32[]{:S(2)}) %collective-permute-start.8) | collective-permute-done | bytes 294944 | tf_op jit(solution)/shard_map/ppermute | solution.py:53
  66.4 0.3 fusion.1
  66.7 0.8 collective-permute-start.9
  67.5 2.5 %collective-permute-start.11 = (bf16[16,72,128]{2,1,0:T(8,128)(2,1)S(1)}, bf16[16,72,128]{2,1,0:T(8,128)(2,1)S(1)}, u32[]{:S(2)}, u32[]{:S(2)}) collective-permute-start(bf16[16,72,128]{2,1,0:T(8,128)(2,1)S(1)} %get-tuple-element.64), channel_id=1, source_target_pairs={{0,12},{4,0},{8,4},{12,8},{1,13},{5,1},{9,5},{13,9},{2,14},{6,2},{... | collective-permute-start | bytes 884744 | tf_op jit(solution)/shard_map/ppermute | solution.py:47
  70.0 6.5 %query_gradients_0.1 = (bf16[128,1024]{1,0:T(8,128)(2,1)}, bf16[128,512]{1,0:T(8,128)(2,1)}) custom-call(s32[128,1]{1,0:T(8,128)} %copy.16.scale_ref, bf16[1024,2048]{1,0:T(8,128)(2,1)} %get-tuple-element.49.ds_hbm, bf16[16,640,128]{2,1,0:T(8,128)(2,1)} %get-tuple-element.50.cache_hbm, bf16[512,1024]{1,0:T(8,128)(2,1)} %key_hbm.5), custom_call_target="tpu_custom_call" | custom-call | flops 1342177280 | bytes 9000000 | tf_op jit(solution)/shard_map/query_gradients_0/pallas_call | solution.py:385
  76.5 0.0 collective-permute-done.5
  76.5 0.0 collective-permute-done.9
  76.5 0.0 collective-permute-done.11
  76.5 0.9 add_convert_fusion
  77.4 4.5 %all-to-all-start.1 = ((bf16[16,72,128]{2,1,0:T(8,128)(2,1)}), bf16[16,72,128]{2,1,0:T(8,128)(2,1)S(1)}, u32[]{:S(2)}, u32[]{:S(2)}) async-start(bf16[16,72,128]{2,1,0:T(8,128)(2,1)} %add_convert_fusion), calls=%async_computation.1 | async-start | bytes 589824 | tf_op jit(solution)/shard_map/all_to_all | solution.py:427
  81.9 6.5 %query_gradients_4.1 = (bf16[128,1024]{1,0:T(8,128)(2,1)}, bf16[128,512]{1,0:T(8,128)(2,1)}) custom-call(s32[128,1]{1,0:T(8,128)} %copy.16.scale_ref, bf16[1024,2048]{1,0:T(8,128)(2,1)} %get-tuple-element.49.ds_hbm, bf16[16,640,128]{2,1,0:T(8,128)(2,1)} %get-tuple-element.50.cache_hbm, ...), custom_call_target="tpu_custom_call", output_to_operand_aliasing={{0}: (4, {}), {1}: (5, {})} | custom-call | flops 1342177280 | bytes 9000000 | tf_op jit(solution)/shard_map/query_gradients_4/pallas_call | solution.py:385
  88.4 3.4 %all-to-all-done.1 = bf16[16,72,128]{2,1,0:T(8,128)(2,1)S(1)} async-done(((bf16[16,72,128]{2,1,0:T(8,128)(2,1)}), bf16[16,72,128]{2,1,0:T(8,128)(2,1)S(1)}, u32[]{:S(2)}, u32[]{:S(2)}) %all-to-all-start.1) | async-done | bytes 294944 | tf_op jit(solution)/shard_map/all_to_all | solution.py:427
  91.9 19.3 %all_to_all.15 = bf16[16,72,128]{2,1,0:T(8,128)(2,1)S(1)} all-to-all(bf16[16,72,128]{2,1,0:T(8,128)(2,1)S(1)} %broadcast_in_dim.14), channel_id=1, replica_groups=mesh['z'=8,'y_lo'=2,'x'=4,'y_hi'=2,'core'=2] {'x','y_hi','core'}, dimensions={0} | all-to-all | bytes 589824 | tf_op jit(solution)/shard_map/all_to_all | solution.py:29
  111.2 0.7 reduce_sum.25
  (4 shorter events, 0.1 us)
Async XLA Ops:
  0.6 0.9 copy-start
  2.5 39.7 %copy-start.1 = (s32[2]{0:T(128)S(1)}, s32[2]{0:T(128)}, u32[]{:S(2)}) copy-start(s32[2]{0:T(128)} %offsets_ref.1) | copy-start | bytes 28
  2.5 27.2 %all-to-all-start = ((bf16[16,144,128]{2,1,0:T(8,128)(2,1)}), bf16[16,144,128]{2,1,0:T(8,128)(2,1)S(1)}, u32[]{:S(2)}, u32[]{:S(2)}) async-start(bf16[16,144,128]{2,1,0:T(8,128)(2,1)} %broadcast_in_dim.12), calls=%async_computation | async-start | bytes 1179648 | tf_op jit(solution)/shard_map/all_to_all | solution.py:29
  29.7 6.9 %collective-permute-start.1 = (bf16[8,144,128]{2,1,0:T(8,128)(2,1)S(1)}, bf16[8,144,128]{2,1,0:T(8,128)(2,1)S(1)}, u32[]{:S(2)}, u32[]{:S(2)}) collective-permute-start(bf16[8,144,128]{2,1,0:T(8,128)(2,1)S(1)} %get-tuple-element.61), channel_id=1, source_target_pairs={{0,4},{4,8},{8,12},{12,0},{1,5},{5,9},{9,13},{13,1},{2,6},{6,10},{... | collective-permute-start | bytes 884744 | tf_op jit(solution)/shard_map/ppermute | solution.py:42
  31.0 9.5 %collective-permute-start = (bf16[8,144,128]{2,1,0:T(8,128)(2,1)S(1)}, bf16[8,144,128]{2,1,0:T(8,128)(2,1)S(1)}, u32[]{:S(2)}, u32[]{:S(2)}) collective-permute-start(bf16[8,144,128]{2,1,0:T(8,128)(2,1)S(1)} %get-tuple-element.62), channel_id=1, source_target_pairs={{0,12},{4,0},{8,4},{12,8},{1,13},{5,1},{9,5},{13,9},{2,14},{6,2},{... | collective-permute-start | bytes 884744 | tf_op jit(solution)/shard_map/ppermute | solution.py:47
  32.4 9.7 %collective-permute-start.2 = (bf16[16,144,128]{2,1,0:T(8,128)(2,1)S(1)}, bf16[16,144,128]{2,1,0:T(8,128)(2,1)S(1)}, u32[]{:S(2)}, u32[]{:S(2)}) collective-permute-start(bf16[16,144,128]{2,1,0:T(8,128)(2,1)S(1)} %all-to-all-done.refs_0_), channel_id=1, source_target_pairs={{0,1},{1,0},{2,3},{3,2},{4,5},{5,4},{6,7},{7,6},{8,9},{9,8},{10,11... | collective-permute-start | bytes 1769480 | tf_op jit(solution)/shard_map/ppermute | solution.py:33
  36.5 5.2 %collective-permute-start.4 = (bf16[8,144,128]{2,1,0:T(8,128)(2,1)S(1)}, bf16[8,144,128]{2,1,0:T(8,128)(2,1)S(1)}, u32[]{:S(2)}, u32[]{:S(2)}) collective-permute-start(bf16[8,144,128]{2,1,0:T(8,128)(2,1)S(1)} %collective-permute-done.1.refs_2_), channel_id=1, source_target_pairs={{0,1},{1,0},{2,3},{3,2},{4,5},{5,4},{6,7},{7,6},{8,9},{9,8},{10,11... | collective-permute-start | bytes 884744 | tf_op jit(solution)/shard_map/ppermute | solution.py:33
  40.5 1.6 %collective-permute-start.3 = (bf16[8,144,128]{2,1,0:T(8,128)(2,1)S(1)}, bf16[8,144,128]{2,1,0:T(8,128)(2,1)S(1)}, u32[]{:S(2)}, u32[]{:S(2)}) collective-permute-start(bf16[8,144,128]{2,1,0:T(8,128)(2,1)S(1)} %collective-permute-done.refs_1_), channel_id=1, source_target_pairs={{0,1},{1,0},{2,3},{3,2},{4,5},{5,4},{6,7},{7,6},{8,9},{9,8},{10,11... | collective-permute-start | bytes 884744 | tf_op jit(solution)/shard_map/ppermute | solution.py:33
  58.2 1.7 %collective-permute-start.7 = (bf16[16,72,128]{2,1,0:T(8,128)(2,1)S(1)}, bf16[16,72,128]{2,1,0:T(8,128)(2,1)S(1)}, u32[]{:S(2)}, u32[]{:S(2)}) collective-permute-start(bf16[16,72,128]{2,1,0:T(8,128)(2,1)S(1)} %get-tuple-element.46), channel_id=1, source_target_pairs={{0,1},{1,0},{2,3},{3,2},{4,5},{5,4},{6,7},{7,6},{8,9},{9,8},{10,11... | collective-permute-start | bytes 884744 | tf_op jit(solution)/shard_map/ppermute | solution.py:33
  58.6 4.1 %collective-permute-start.6 = (bf16[16,72,128]{2,1,0:T(8,128)(2,1)S(1)}, bf16[16,72,128]{2,1,0:T(8,128)(2,1)S(1)}, u32[]{:S(2)}, u32[]{:S(2)}) collective-permute-start(bf16[16,72,128]{2,1,0:T(8,128)(2,1)S(1)} %get-tuple-element.44), channel_id=1, source_target_pairs={{0,1},{1,0},{2,3},{3,2},{4,5},{5,4},{6,7},{7,6},{8,9},{9,8},{10,11... | collective-permute-start | bytes 884744 | tf_op jit(solution)/shard_map/ppermute | solution.py:33
  58.8 4.0 %collective-permute-start.10 = (bf16[16,72,128]{2,1,0:T(8,128)(2,1)S(1)}, bf16[16,72,128]{2,1,0:T(8,128)(2,1)S(1)}, u32[]{:S(2)}, u32[]{:S(2)}) collective-permute-start(bf16[16,72,128]{2,1,0:T(8,128)(2,1)S(1)} %get-tuple-element.48), channel_id=1, source_target_pairs={{0,1},{1,0},{2,3},{3,2},{4,5},{5,4},{6,7},{7,6},{8,9},{9,8},{10,11... | collective-permute-start | bytes 884744 | tf_op jit(solution)/shard_map/ppermute | solution.py:33
  59.9 6.5 %collective-permute-start.8 = (bf16[16,72,128]{2,1,0:T(8,128)(2,1)S(1)}, bf16[16,72,128]{2,1,0:T(8,128)(2,1)S(1)}, u32[]{:S(2)}, u32[]{:S(2)}) collective-permute-start(bf16[16,72,128]{2,1,0:T(8,128)(2,1)S(1)} %add_convert_fusion.1), channel_id=1, source_target_pairs={{0,4},{1,13},{4,8},{5,1},{8,12},{9,5},{12,0},{13,9},{2,6},{3,15},{... | collective-permute-start | bytes 884744 | tf_op jit(solution)/shard_map/ppermute | solution.py:53
  62.8 13.7 %collective-permute-start.5 = (bf16[16,72,128]{2,1,0:T(8,128)(2,1)S(1)}, bf16[16,72,128]{2,1,0:T(8,128)(2,1)S(1)}, u32[]{:S(2)}, u32[]{:S(2)}) collective-permute-start(bf16[16,72,128]{2,1,0:T(8,128)(2,1)S(1)} %get-tuple-element.42), channel_id=1, source_target_pairs={{0,1},{1,0},{2,3},{3,2},{4,5},{5,4},{6,7},{7,6},{8,9},{9,8},{10,11... | collective-permute-start | bytes 884744 | tf_op jit(solution)/shard_map/ppermute | solution.py:33
  66.7 9.8 %collective-permute-start.9 = (bf16[16,72,128]{2,1,0:T(8,128)(2,1)S(1)}, bf16[16,72,128]{2,1,0:T(8,128)(2,1)S(1)}, u32[]{:S(2)}, u32[]{:S(2)}) collective-permute-start(bf16[16,72,128]{2,1,0:T(8,128)(2,1)S(1)} %get-tuple-element.63), channel_id=1, source_target_pairs={{0,4},{4,8},{8,12},{12,0},{1,5},{5,9},{9,13},{13,1},{2,6},{6,10},{... | collective-permute-start | bytes 884744 | tf_op jit(solution)/shard_map/ppermute | solution.py:42
  67.5 9.0 %collective-permute-start.11 = (bf16[16,72,128]{2,1,0:T(8,128)(2,1)S(1)}, bf16[16,72,128]{2,1,0:T(8,128)(2,1)S(1)}, u32[]{:S(2)}, u32[]{:S(2)}) collective-permute-start(bf16[16,72,128]{2,1,0:T(8,128)(2,1)S(1)} %get-tuple-element.64), channel_id=1, source_target_pairs={{0,12},{4,0},{8,4},{12,8},{1,13},{5,1},{9,5},{13,9},{2,14},{6,2},{... | collective-permute-start | bytes 884744 | tf_op jit(solution)/shard_map/ppermute | solution.py:47
  77.4 14.4 %all-to-all-start.1 = ((bf16[16,72,128]{2,1,0:T(8,128)(2,1)}), bf16[16,72,128]{2,1,0:T(8,128)(2,1)S(1)}, u32[]{:S(2)}, u32[]{:S(2)}) async-start(bf16[16,72,128]{2,1,0:T(8,128)(2,1)} %add_convert_fusion), calls=%async_computation.1 | async-start | bytes 589824 | tf_op jit(solution)/shard_map/all_to_all | solution.py:427

commit v8 on v7

--- a/solution.py
+++ b/solution.py
@@ -423,9 +423,9 @@
     part = up_key.shape[1] // NOPE // 2
     early = query_gradients(0, part, scales, dscore, whole, up_key)
     slices, early = lax.optimization_barrier((slices, early))
+    slices = add_up(lax.all_to_all(slices, SEQ, 0, 0, tiled=True))
+    slices, early = lax.optimization_barrier((slices, early))
     query_grads = query_gradients(part, part, scales, dscore, whole, up_key, early)
-    slices = add_up(lax.all_to_all(slices, SEQ, 0, 0, tiled=True))
-    slices, query_grads = lax.optimization_barrier((slices, query_grads))
     return (owned_columns(slices), *query_grads)
 
 

time: 112 us -> 112 us (level)
  starting transfers between devices: 32.3 us -> 38 us
  blocking collectives: 19.3 us -> 14.2 us
    all_to_all x1 -> x2, starting transfers between devices: 10.3 us -> 20.5 us  [to_each(): return lax.all_to_all(copies, axes, 0, 0, tiled=True)]
    all_to_all x1, blocking collectives: 19.3 us -> 14.2 us  [per_device(): slices = add_up(lax.all_to_all(slices, SEQ, 0, 0, tiled=True))]
    all_to_all x1 -> x0, starting transfers between devices: 4.52 us -> none  [per_device(): slices = add_up(lax.all_to_all(slices, SEQ, 0, 0, tiled=True))]
    all_to_all x1 -> x0, waiting for transfers between devices: 3.41 us -> none  [per_device(): slices = add_up(lax.all_to_all(slices, SEQ, 0, 0, tiled=True))]
    all_to_all x1 -> x2, waiting for transfers between devices: 10 us -> 12.7 us  [to_each(): return lax.all_to_all(copies, axes, 0, 0, tiled=True)]
where the time goes in v8:
time: 112 us
  starting transfers between devices  38 us (34%)
  Pallas kernels  34.5 us (31%)
  waiting for transfers between devices  19.1 us (17%)
  blocking collectives  14.2 us (13%)
  local copies, waits for them, and re-layouts  4.01 us (4%)
  other arithmetic  1.33 us (1%)
    all_to_all x2, starting transfers between devices, to_each(): return lax.all_to_all(copies, axes, 0, 0, tiled=True)  20.5 us
    pallas_call x1, Pallas kernels, attend(): pl.pallas_call(attend_kernel, out_shape=[jax.ShapeDtypeStruct((owners, he...  16 us
    all_to_all x1, blocking collectives, per_device(): slices = add_up(lax.all_to_all(slices, SEQ, 0, 0, tiled=True))  14.2 us
    pallas_call x2, Pallas kernels, query_gradients(): pl.pallas_call(functools.partial(query_kernel, first, len(ready) // 2), o...  13 us
    all_to_all x2, waiting for transfers between devices, to_each(): return lax.all_to_all(copies, axes, 0, 0, tiled=True)  12.7 us
    ppermute x7, starting transfers between devices, swap_core(): return lax.ppermute(block, 'core', [(0, 1), (1, 0)])  8.61 us
    pallas_call x1, Pallas kernels, project(): pl.pallas_call(project_kernel, out_shape=(jax.ShapeDtypeStruct((rows, PAD...  5.47 us
    ppermute x2, starting transfers between devices, to_previous(): return lax.ppermute(block, 'x', [(i, (i - 1) % size) for i in range(size)])  3.94 us
  transfers between devices with their start and end apart: 14, of which 7 were waited for; matrix products, arithmetic and copies ran while one was open for 2% of the time, Pallas kernels for 17%

profile of v8, /device:TPU:1, one launch (start us, length us, event | category | flops | bytes accessed | tf_op | source)
XLA Modules:
  0.0 111.9 jit_solution(11334010666064030259)
XLA Ops:
  0.6 0.0 copy-start
  0.7 0.9 copy-done
  1.6 0.9 broadcast_in_dim.12
  2.5 0.0 copy-start.1
  2.5 10.3 %all-to-all-start = ((bf16[16,144,128]{2,1,0:T(8,128)(2,1)}), bf16[16,144,128]{2,1,0:T(8,128)(2,1)S(1)}, u32[]{:S(2)}, u32[]{:S(2)}) async-start(bf16[16,144,128]{2,1,0:T(8,128)(2,1)} %broadcast_in_dim.12), calls=%async_computation | async-start | bytes 1179648 | tf_op jit(solution)/shard_map/all_to_all | solution.py:29
  12.7 1.4 %copy.16.scale_ref = s32[128,1]{1,0:T(8,128)} copy(s32[128,1]{0,1:T(1,128)} %bitcast.11) | data formatting | bytes 1024 | tf_op jit(solution)/shard_map/reshape | solution.py:416
  14.1 5.5 %project.1 = (bf16[1024,640]{1,0:T(8,128)(2,1)}, bf16[1024,512]{1,0:T(8,128)(2,1)}, bf16[576,1024]{1,0:T(8,128)(2,1)}, bf16[512,1024]{1,0:T(8,128)(2,1)}) custom-call(s32[128,1]{1,0:T(8,128)} %copy.16.scale_ref, bf16[128,1024]{1,0:T(8,128)(2,1)} %nope_hbm.1, bf16[128,512]{1,0:T(8,128)(2,1)} %rope_hbm.1, bf16[512,1024]{1,0:T(8,128)(2,1)} %key_hbm.5, ...), custom_call_target="tpu_custom_call" | custom-call | flops 536870912 | bytes 7500000 | tf_op jit(solution)/shard_map/project/pallas_call | solution.py:129
  19.6 10.0 %all-to-all-done.refs_0_ = bf16[16,144,128]{2,1,0:T(8,128)(2,1)S(1)} async-done(((bf16[16,144,128]{2,1,0:T(8,128)(2,1)}), bf16[16,144,128]{2,1,0:T(8,128)(2,1)S(1)}, u32[]{:S(2)}, u32[]{:S(2)}) %all-to-all-start) | async-done | bytes 589856 | tf_op jit(solution)/shard_map/all_to_all | solution.py:29
  29.7 1.3 %collective-permute-start.1 = (bf16[8,144,128]{2,1,0:T(8,128)(2,1)S(1)}, bf16[8,144,128]{2,1,0:T(8,128)(2,1)S(1)}, u32[]{:S(2)}, u32[]{:S(2)}) collective-permute-start(bf16[8,144,128]{2,1,0:T(8,128)(2,1)S(1)} %get-tuple-element.61), channel_id=1, source_target_pairs={{0,4},{4,8},{8,12},{12,0},{1,5},{5,9},{9,13},{13,1},{2,6},{6,10},{... | collective-permute-start | bytes 884744 | tf_op jit(solution)/shard_map/ppermute | solution.py:42
  31.0 1.5 %collective-permute-start = (bf16[8,144,128]{2,1,0:T(8,128)(2,1)S(1)}, bf16[8,144,128]{2,1,0:T(8,128)(2,1)S(1)}, u32[]{:S(2)}, u32[]{:S(2)}) collective-permute-start(bf16[8,144,128]{2,1,0:T(8,128)(2,1)S(1)} %get-tuple-element.62), channel_id=1, source_target_pairs={{0,12},{4,0},{8,4},{12,8},{1,13},{5,1},{9,5},{13,9},{2,14},{6,2},{... | collective-permute-start | bytes 884744 | tf_op jit(solution)/shard_map/ppermute | solution.py:47
  32.4 3.4 %collective-permute-start.2 = (bf16[16,144,128]{2,1,0:T(8,128)(2,1)S(1)}, bf16[16,144,128]{2,1,0:T(8,128)(2,1)S(1)}, u32[]{:S(2)}, u32[]{:S(2)}) collective-permute-start(bf16[16,144,128]{2,1,0:T(8,128)(2,1)S(1)} %all-to-all-done.refs_0_), channel_id=1, source_target_pairs={{0,1},{1,0},{2,3},{3,2},{4,5},{5,4},{6,7},{7,6},{8,9},{9,8},{10,11... | collective-permute-start | bytes 1769480 | tf_op jit(solution)/shard_map/ppermute | solution.py:33
  35.8 0.7 collective-permute-done.1.refs_2_
  36.5 4.0 %collective-permute-start.4 = (bf16[8,144,128]{2,1,0:T(8,128)(2,1)S(1)}, bf16[8,144,128]{2,1,0:T(8,128)(2,1)S(1)}, u32[]{:S(2)}, u32[]{:S(2)}) collective-permute-start(bf16[8,144,128]{2,1,0:T(8,128)(2,1)S(1)} %collective-permute-done.1.refs_2_), channel_id=1, source_target_pairs={{0,1},{1,0},{2,3},{3,2},{4,5},{5,4},{6,7},{7,6},{8,9},{9,8},{10,11... | collective-permute-start | bytes 884744 | tf_op jit(solution)/shard_map/ppermute | solution.py:33
  40.5 0.0 collective-permute-done.refs_1_
  40.5 0.3 collective-permute-start.3
  40.8 0.1 pad_add_fusion.place_ref
  40.9 0.9 collective-permute-done.4.refs_5_
  41.7 0.4 collective-permute-done.3.refs_4_
  42.1 0.0 collective-permute-done.2.refs_3_
  42.1 0.0 copy-done.1
  42.1 16.0 %attend.1 = (bf16[16,72,128]{2,1,0:T(8,128)(2,1)S(1)}, bf16[16,72,128]{2,1,0:T(8,128)(2,1)S(1)}, bf16[16,72,128]{2,1,0:T(8,128)(2,1)S(1)}, bf16[16,72,128]{2,1,0...) custom-call(s32[2]{0:T(128)S(1)} %pad_add_fusion.place_ref, ...), custom_call_target="tpu_custom_call" | custom-call | flops 9663676416 | bytes 14000000 | tf_op jit(solution)/shard_map/attend/pallas_call | solution.py:301
  58.2 0.5 collective-permute-start.7
  58.6 0.1 collective-permute-start.6
  58.8 0.4 collective-permute-start.10
  59.1 0.7 collective-permute-done.7
  59.8 0.1 add_convert_fusion.1
  59.9 2.8 %collective-permute-start.8 = (bf16[16,72,128]{2,1,0:T(8,128)(2,1)S(1)}, bf16[16,72,128]{2,1,0:T(8,128)(2,1)S(1)}, u32[]{:S(2)}, u32[]{:S(2)}) collective-permute-start(bf16[16,72,128]{2,1,0:T(8,128)(2,1)S(1)} %add_convert_fusion.1), channel_id=1, source_target_pairs={{0,4},{1,13},{4,8},{5,1},{8,12},{9,5},{12,0},{13,9},{2,6},{3,15},{... | collective-permute-start | bytes 884744 | tf_op jit(solution)/shard_map/ppermute | solution.py:53
  62.8 0.0 collective-permute-start.5
  62.8 0.0 collective-permute-done.6
  62.8 0.0 collective-permute-done.10
  62.8 3.7 %collective-permute-done.8 = bf16[16,72,128]{2,1,0:T(8,128)(2,1)S(1)} collective-permute-done((bf16[16,72,128]{2,1,0:T(8,128)(2,1)S(1)}, bf16[16,72,128]{2,1,0:T(8,128)(2,1)S(1)}, u32[]{:S(2)}, u32[]{:S(2)}) %collective-permute-start.8) | collective-permute-done | bytes 294944 | tf_op jit(solution)/shard_map/ppermute | solution.py:53
  66.4 0.3 fusion.1
  66.7 0.8 collective-permute-start.9
  67.5 2.5 %collective-permute-start.11 = (bf16[16,72,128]{2,1,0:T(8,128)(2,1)S(1)}, bf16[16,72,128]{2,1,0:T(8,128)(2,1)S(1)}, u32[]{:S(2)}, u32[]{:S(2)}) collective-permute-start(bf16[16,72,128]{2,1,0:T(8,128)(2,1)S(1)} %get-tuple-element.64), channel_id=1, source_target_pairs={{0,12},{4,0},{8,4},{12,8},{1,13},{5,1},{9,5},{13,9},{2,14},{6,2},{... | collective-permute-start | bytes 884744 | tf_op jit(solution)/shard_map/ppermute | solution.py:47
  70.0 6.5 %query_gradients_0.1 = (bf16[128,1024]{1,0:T(8,128)(2,1)}, bf16[128,512]{1,0:T(8,128)(2,1)}) custom-call(s32[128,1]{1,0:T(8,128)} %copy.16.scale_ref, bf16[1024,2048]{1,0:T(8,128)(2,1)} %get-tuple-element.49.ds_hbm, bf16[16,640,128]{2,1,0:T(8,128)(2,1)} %get-tuple-element.50.cache_hbm, bf16[512,1024]{1,0:T(8,128)(2,1)} %key_hbm.5), custom_call_target="tpu_custom_call" | custom-call | flops 1342177280 | bytes 9000000 | tf_op jit(solution)/shard_map/query_gradients_0/pallas_call | solution.py:385
  76.5 0.0 collective-permute-done.5
  76.5 0.0 collective-permute-done.9
  76.5 0.0 collective-permute-done.11
  76.5 0.2 add_convert_fusion
  76.7 14.2 %all_to_all.15 = bf16[16,72,128]{2,1,0:T(8,128)(2,1)S(1)} all-to-all(bf16[16,72,128]{2,1,0:T(8,128)(2,1)S(1)} %add_convert_fusion), channel_id=1, replica_groups=mesh['z'=8,'y_lo'=2,'x'=4,'y_hi'=2,'core'=2] {'z','y_lo'}, dimensions={0} | all-to-all | bytes 589824 | tf_op jit(solution)/shard_map/all_to_all | solution.py:426
  91.0 0.8 broadcast_in_dim.14
  91.7 10.2 %all-to-all-start.2 = ((bf16[16,72,128]{2,1,0:T(8,128)(2,1)}), bf16[16,72,128]{2,1,0:T(8,128)(2,1)S(1)}, u32[]{:S(2)}, u32[]{:S(2)}) async-start(bf16[16,72,128]{2,1,0:T(8,128)(2,1)} %broadcast_in_dim.14), calls=%async_computation.2 | async-start | bytes 589824 | tf_op jit(solution)/shard_map/all_to_all | solution.py:29
  102.0 6.5 %query_gradients_4.1 = (bf16[128,1024]{1,0:T(8,128)(2,1)}, bf16[128,512]{1,0:T(8,128)(2,1)}) custom-call(s32[128,1]{1,0:T(8,128)} %copy.16.scale_ref, bf16[1024,2048]{1,0:T(8,128)(2,1)} %get-tuple-element.49.ds_hbm, bf16[16,640,128]{2,1,0:T(8,128)(2,1)} %get-tuple-element.50.cache_hbm, ...), custom_call_target="tpu_custom_call", output_to_operand_aliasing={{0}: (4, {}), {1}: (5, {})} | custom-call | flops 1342177280 | bytes 9000000 | tf_op jit(solution)/shard_map/query_gradients_4/pallas_call | solution.py:385
  108.5 2.7 %all-to-all-done.2 = bf16[16,72,128]{2,1,0:T(8,128)(2,1)S(1)} async-done(((bf16[16,72,128]{2,1,0:T(8,128)(2,1)}), bf16[16,72,128]{2,1,0:T(8,128)(2,1)S(1)}, u32[]{:S(2)}, u32[]{:S(2)}) %all-to-all-start.2) | async-done | bytes 294944 | tf_op jit(solution)/shard_map/all_to_all | solution.py:29
  111.2 0.7 reduce_sum.25
  (3 shorter events, 0.1 us)
Async XLA Ops:
  0.6 0.9 copy-start
  2.5 39.7 %copy-start.1 = (s32[2]{0:T(128)S(1)}, s32[2]{0:T(128)}, u32[]{:S(2)}) copy-start(s32[2]{0:T(128)} %offsets_ref.1) | copy-start | bytes 28
  2.5 27.2 %all-to-all-start = ((bf16[16,144,128]{2,1,0:T(8,128)(2,1)}), bf16[16,144,128]{2,1,0:T(8,128)(2,1)S(1)}, u32[]{:S(2)}, u32[]{:S(2)}) async-start(bf16[16,144,128]{2,1,0:T(8,128)(2,1)} %broadcast_in_dim.12), calls=%async_computation | async-start | bytes 1179648 | tf_op jit(solution)/shard_map/all_to_all | solution.py:29
  29.7 6.9 %collective-permute-start.1 = (bf16[8,144,128]{2,1,0:T(8,128)(2,1)S(1)}, bf16[8,144,128]{2,1,0:T(8,128)(2,1)S(1)}, u32[]{:S(2)}, u32[]{:S(2)}) collective-permute-start(bf16[8,144,128]{2,1,0:T(8,128)(2,1)S(1)} %get-tuple-element.61), channel_id=1, source_target_pairs={{0,4},{4,8},{8,12},{12,0},{1,5},{5,9},{9,13},{13,1},{2,6},{6,10},{... | collective-permute-start | bytes 884744 | tf_op jit(solution)/shard_map/ppermute | solution.py:42
  31.0 9.5 %collective-permute-start = (bf16[8,144,128]{2,1,0:T(8,128)(2,1)S(1)}, bf16[8,144,128]{2,1,0:T(8,128)(2,1)S(1)}, u32[]{:S(2)}, u32[]{:S(2)}) collective-permute-start(bf16[8,144,128]{2,1,0:T(8,128)(2,1)S(1)} %get-tuple-element.62), channel_id=1, source_target_pairs={{0,12},{4,0},{8,4},{12,8},{1,13},{5,1},{9,5},{13,9},{2,14},{6,2},{... | collective-permute-start | bytes 884744 | tf_op jit(solution)/shard_map/ppermute | solution.py:47
  32.4 9.7 %collective-permute-start.2 = (bf16[16,144,128]{2,1,0:T(8,128)(2,1)S(1)}, bf16[16,144,128]{2,1,0:T(8,128)(2,1)S(1)}, u32[]{:S(2)}, u32[]{:S(2)}) collective-permute-start(bf16[16,144,128]{2,1,0:T(8,128)(2,1)S(1)} %all-to-all-done.refs_0_), channel_id=1, source_target_pairs={{0,1},{1,0},{2,3},{3,2},{4,5},{5,4},{6,7},{7,6},{8,9},{9,8},{10,11... | collective-permute-start | bytes 1769480 | tf_op jit(solution)/shard_map/ppermute | solution.py:33
  36.5 5.2 %collective-permute-start.4 = (bf16[8,144,128]{2,1,0:T(8,128)(2,1)S(1)}, bf16[8,144,128]{2,1,0:T(8,128)(2,1)S(1)}, u32[]{:S(2)}, u32[]{:S(2)}) collective-permute-start(bf16[8,144,128]{2,1,0:T(8,128)(2,1)S(1)} %collective-permute-done.1.refs_2_), channel_id=1, source_target_pairs={{0,1},{1,0},{2,3},{3,2},{4,5},{5,4},{6,7},{7,6},{8,9},{9,8},{10,11... | collective-permute-start | bytes 884744 | tf_op jit(solution)/shard_map/ppermute | solution.py:33
  40.5 1.6 %collective-permute-start.3 = (bf16[8,144,128]{2,1,0:T(8,128)(2,1)S(1)}, bf16[8,144,128]{2,1,0:T(8,128)(2,1)S(1)}, u32[]{:S(2)}, u32[]{:S(2)}) collective-permute-start(bf16[8,144,128]{2,1,0:T(8,128)(2,1)S(1)} %collective-permute-done.refs_1_), channel_id=1, source_target_pairs={{0,1},{1,0},{2,3},{3,2},{4,5},{5,4},{6,7},{7,6},{8,9},{9,8},{10,11... | collective-permute-start | bytes 884744 | tf_op jit(solution)/shard_map/ppermute | solution.py:33
  58.2 1.7 %collective-permute-start.7 = (bf16[16,72,128]{2,1,0:T(8,128)(2,1)S(1)}, bf16[16,72,128]{2,1,0:T(8,128)(2,1)S(1)}, u32[]{:S(2)}, u32[]{:S(2)}) collective-permute-start(bf16[16,72,128]{2,1,0:T(8,128)(2,1)S(1)} %get-tuple-element.46), channel_id=1, source_target_pairs={{0,1},{1,0},{2,3},{3,2},{4,5},{5,4},{6,7},{7,6},{8,9},{9,8},{10,11... | collective-permute-start | bytes 884744 | tf_op jit(solution)/shard_map/ppermute | solution.py:33
  58.6 4.1 %collective-permute-start.6 = (bf16[16,72,128]{2,1,0:T(8,128)(2,1)S(1)}, bf16[16,72,128]{2,1,0:T(8,128)(2,1)S(1)}, u32[]{:S(2)}, u32[]{:S(2)}) collective-permute-start(bf16[16,72,128]{2,1,0:T(8,128)(2,1)S(1)} %get-tuple-element.44), channel_id=1, source_target_pairs={{0,1},{1,0},{2,3},{3,2},{4,5},{5,4},{6,7},{7,6},{8,9},{9,8},{10,11... | collective-permute-start | bytes 884744 | tf_op jit(solution)/shard_map/ppermute | solution.py:33
  58.8 4.0 %collective-permute-start.10 = (bf16[16,72,128]{2,1,0:T(8,128)(2,1)S(1)}, bf16[16,72,128]{2,1,0:T(8,128)(2,1)S(1)}, u32[]{:S(2)}, u32[]{:S(2)}) collective-permute-start(bf16[16,72,128]{2,1,0:T(8,128)(2,1)S(1)} %get-tuple-element.48), channel_id=1, source_target_pairs={{0,1},{1,0},{2,3},{3,2},{4,5},{5,4},{6,7},{7,6},{8,9},{9,8},{10,11... | collective-permute-start | bytes 884744 | tf_op jit(solution)/shard_map/ppermute | solution.py:33
  59.9 6.5 %collective-permute-start.8 = (bf16[16,72,128]{2,1,0:T(8,128)(2,1)S(1)}, bf16[16,72,128]{2,1,0:T(8,128)(2,1)S(1)}, u32[]{:S(2)}, u32[]{:S(2)}) collective-permute-start(bf16[16,72,128]{2,1,0:T(8,128)(2,1)S(1)} %add_convert_fusion.1), channel_id=1, source_target_pairs={{0,4},{1,13},{4,8},{5,1},{8,12},{9,5},{12,0},{13,9},{2,6},{3,15},{... | collective-permute-start | bytes 884744 | tf_op jit(solution)/shard_map/ppermute | solution.py:53
  62.8 13.7 %collective-permute-start.5 = (bf16[16,72,128]{2,1,0:T(8,128)(2,1)S(1)}, bf16[16,72,128]{2,1,0:T(8,128)(2,1)S(1)}, u32[]{:S(2)}, u32[]{:S(2)}) collective-permute-start(bf16[16,72,128]{2,1,0:T(8,128)(2,1)S(1)} %get-tuple-element.42), channel_id=1, source_target_pairs={{0,1},{1,0},{2,3},{3,2},{4,5},{5,4},{6,7},{7,6},{8,9},{9,8},{10,11... | collective-permute-start | bytes 884744 | tf_op jit(solution)/shard_map/ppermute | solution.py:33
  66.7 9.8 %collective-permute-start.9 = (bf16[16,72,128]{2,1,0:T(8,128)(2,1)S(1)}, bf16[16,72,128]{2,1,0:T(8,128)(2,1)S(1)}, u32[]{:S(2)}, u32[]{:S(2)}) collective-permute-start(bf16[16,72,128]{2,1,0:T(8,128)(2,1)S(1)} %get-tuple-element.63), channel_id=1, source_target_pairs={{0,4},{4,8},{8,12},{12,0},{1,5},{5,9},{9,13},{13,1},{2,6},{6,10},{... | collective-permute-start | bytes 884744 | tf_op jit(solution)/shard_map/ppermute | solution.py:42
  67.5 9.0 %collective-permute-start.11 = (bf16[16,72,128]{2,1,0:T(8,128)(2,1)S(1)}, bf16[16,72,128]{2,1,0:T(8,128)(2,1)S(1)}, u32[]{:S(2)}, u32[]{:S(2)}) collective-permute-start(bf16[16,72,128]{2,1,0:T(8,128)(2,1)S(1)} %get-tuple-element.64), channel_id=1, source_target_pairs={{0,12},{4,0},{8,4},{12,8},{1,13},{5,1},{9,5},{13,9},{2,14},{6,2},{... | collective-permute-start | bytes 884744 | tf_op jit(solution)/shard_map/ppermute | solution.py:47
  91.7 19.5 %all-to-all-start.2 = ((bf16[16,72,128]{2,1,0:T(8,128)(2,1)}), bf16[16,72,128]{2,1,0:T(8,128)(2,1)S(1)}, u32[]{:S(2)}, u32[]{:S(2)}) async-start(bf16[16,72,128]{2,1,0:T(8,128)(2,1)} %broadcast_in_dim.14), calls=%async_computation.2 | async-start | bytes 589824 | tf_op jit(solution)/shard_map/all_to_all | solution.py:29
